TPU v7x, 32 devices: a whole 2x2x4 slice. The times are simulated.
32 devices in a mesh: dp: 4 (over z), ctx: 2 (over y), tp: 4 (over x, core).
Axes of the slice: x: 2, y: 2, z: 4, core: 2. Of those that a mesh axis runs over, the one named last changes fastest.
Arguments:
- inputs: bfloat16 [8, 1024, 768], P('dp', ('ctx', 'tp')), may hold values from -6 to 6
- segments: int32 [8, 1024], P('dp', 'ctx'), may hold values from 0 to 4, never falling along the last dimension, each value on 1 to 512 neighbouring positions
- cotangent: bfloat16 [8, 1024, 768], P('dp', ('ctx', 'tp')), may hold values from -6 to 6
- student_first_gain: bfloat16 [768], P('dp'), may hold values from 0.5 to 1.5
- student_first_shift: bfloat16 [768], P('dp'), may hold values from -3 to 3
- student_merged_weight: bfloat16 [768, 3, 768], P('dp', None, 'tp'), may hold values from -0.21875 to 0.21875
- student_merged_bias: bfloat16 [2, 12, 64], P(None, 'tp', 'dp'), may hold values from -3 to 3
- student_output_weight: bfloat16 [768, 768], P('tp', 'dp'), may hold values from -1.25 to 1.25
- student_output_bias: bfloat16 [768], P('dp'), may hold values from -3 to 3
- student_second_gain: bfloat16 [768], P('dp'), may hold values from 0.5 to 1.5
- student_second_shift: bfloat16 [768], P('dp'), may hold values from -3 to 3
- student_expand_weight: bfloat16 [768, 3072], P('dp', 'tp'), may hold values from -0.21875 to 0.21875
- student_expand_bias: bfloat16 [48, 64], P('tp', 'dp'), may hold values from -3 to 3
- student_reduce_weight: bfloat16 [3072, 768], P('tp', 'dp'), may hold values from -0.109375 to 0.109375
- student_reduce_bias: bfloat16 [768], P('dp'), may hold values from -3 to 3
- teacher_first_gain: bfloat16 [768], P('dp'), may hold values from 0.5 to 1.5
- teacher_first_shift: bfloat16 [768], P('dp'), may hold values from -3 to 3
- teacher_merged_weight: bfloat16 [768, 3, 768], P('dp', None, 'tp'), may hold values from -0.21875 to 0.21875
- teacher_merged_bias: bfloat16 [2, 12, 64], P(None, 'tp', 'dp'), may hold values from -3 to 3
- teacher_output_weight: bfloat16 [768, 768], P('tp', 'dp'), may hold values from -1.25 to 1.25
- teacher_output_bias: bfloat16 [768], P('dp'), may hold values from -3 to 3
- teacher_second_gain: bfloat16 [768], P('dp'), may hold values from 0.5 to 1.5
- teacher_second_shift: bfloat16 [768], P('dp'), may hold values from -3 to 3
- teacher_expand_weight: bfloat16 [768, 3072], P('dp', 'tp'), may hold values from -0.21875 to 0.21875
- teacher_expand_bias: bfloat16 [48, 64], P('tp', 'dp'), may hold values from -3 to 3
- teacher_reduce_weight: bfloat16 [3072, 768], P('tp', 'dp'), may hold values from -0.109375 to 0.109375
- teacher_reduce_bias: bfloat16 [768], P('dp'), may hold values from -3 to 3
Outputs:
- output: bfloat16 [8, 1024, 768], P('dp', ('ctx', 'tp'))
- input_grad: float32 [8, 1024, 768], P('dp', ('ctx', 'tp'))
- grad_student_first_gain: float32 [768], P('dp')
- grad_student_first_shift: float32 [768], P('dp')
- grad_student_merged_weight: float32 [768, 3, 768], P('dp', None, 'tp')
- grad_student_merged_bias: float32 [2, 12, 64], P(None, 'tp', 'dp')
- grad_student_output_weight: float32 [768, 768], P('tp', 'dp')
- grad_student_output_bias: float32 [768], P('dp')
- grad_student_second_gain: float32 [768], P('dp')
- grad_student_second_shift: float32 [768], P('dp')
- grad_student_expand_weight: float32 [768, 3072], P('dp', 'tp')
- grad_student_expand_bias: float32 [48, 64], P('tp', 'dp')
- grad_student_reduce_weight: float32 [3072, 768], P('tp', 'dp')
- grad_student_reduce_bias: float32 [768], P('dp')
- grad_teacher_first_gain: float32 [768], P('dp')
- grad_teacher_first_shift: float32 [768], P('dp')
- grad_teacher_merged_weight: float32 [768, 3, 768], P('dp', None, 'tp')
- grad_teacher_merged_bias: float32 [2, 12, 64], P(None, 'tp', 'dp')
- grad_teacher_output_weight: float32 [768, 768], P('tp', 'dp')
- grad_teacher_output_bias: float32 [768], P('dp')
- grad_teacher_second_gain: float32 [768], P('dp')
- grad_teacher_second_shift: float32 [768], P('dp')
- grad_teacher_expand_weight: float32 [768, 3072], P('dp', 'tp')
- grad_teacher_expand_bias: float32 [48, 64], P('tp', 'dp')
- grad_teacher_reduce_weight: float32 [3072, 768], P('tp', 'dp')
- grad_teacher_reduce_bias: float32 [768], P('dp')
Inputs may be any that keep to these rules, and one draw needn't show every extreme that they name: `segments`: within a sequence the document numbers never fall from one token to the next; a document holds 1 to 512 consecutive tokens, and each sequence has one of exactly 512.
All inputs are finite; a program needn't handle non-finite values.
Results may differ from a plain program's by a relative error of at most 0.025.
Values may be sent and summed in bfloat16 or wider, within the bound.
No kernel may reach another device: no remote copies, remote signals or barrier semaphores. Data moves between devices by JAX's collectives and lax.ppermute only.
A program may use at most 192 MiB of HBM per device.

v0:
```python
import jax
import jax.numpy as jnp
from jax import lax
from jax.experimental import pallas as pl
from jax.experimental.layout import Layout, with_layout_constraint
from jax.experimental.pallas import tpu as pltpu
from jax.sharding import PartitionSpec as P

HD = 64
DOC_MAX = 2000


EPSILON = 1e-05
GELU_SCALE = 0.7978845608028654


def from_behind(block, axis, distance):
    devices = range(lax.axis_size(axis))
    route = [(i - distance, i) for i in devices if i - distance in devices]
    return lax.ppermute(block, axis, route)


def layer_norm(values, norm_gain, norm_shift):
    center = values - jnp.mean(values, axis=-1, keepdims=True)
    spread = jnp.mean(center * center, axis=-1, keepdims=True)
    return center * lax.rsqrt(spread + EPSILON) * norm_gain + norm_shift


def gelu_tanh(values):
    return (
        0.5 * values * (1.0 + jnp.tanh(GELU_SCALE * (values + 0.044715 * values * values * values)))
    )


def spread_rows(row_block):
    return lax.all_gather(row_block, "tp", axis=1, tiled=True)


def gather_sums(partial_value):
    return lax.psum_scatter(
        partial_value.astype(jnp.bfloat16), "tp", scatter_dimension=1, tiled=True
    ).astype(jnp.float32)


def to_items(tensor, head_count):
    batches, length, features = tensor.shape
    head_size = features // head_count
    return (
        tensor.reshape(batches, length, head_count, head_size)
        .transpose(0, 2, 1, 3)
        .reshape(batches * head_count, length, head_size)
    )


def from_items(tensor, head_count):
    item_count, length, head_size = tensor.shape
    batches = item_count // head_count
    return (
        tensor.reshape(batches, head_count, length, head_size)
        .transpose(0, 2, 1, 3)
        .reshape(batches, length, head_count * head_size)
    )


def masked_scores(query_rows, key_rows, query_docs, key_docs, allowed):
    raw_scores = (
        jnp.einsum("qd,kd->qk", query_rows, key_rows, preferred_element_type=jnp.float32) * 0.125
    )
    keep_mask = allowed & (key_docs[None, :] == query_docs[:, None])
    return (jnp.where(keep_mask, raw_scores, -1e30), keep_mask)


def attend_forward(allowed):

    def attend_item(packed):
        query_rows, key_rows, value_rows, query_docs, key_docs = packed
        scores, keep_mask = masked_scores(query_rows, key_rows, query_docs, key_docs, allowed)
        row_top = jnp.max(scores, axis=-1, keepdims=True)
        raised = jnp.exp(scores - row_top)
        row_total = jnp.sum(raised, axis=-1, keepdims=True)
        weights = (raised / row_total).astype(jnp.bfloat16)
        mixed_rows = jnp.dot(weights, value_rows, preferred_element_type=jnp.float32).astype(
            jnp.bfloat16
        )
        return (mixed_rows, row_top[:, 0] + jnp.log(row_total[:, 0]))

    return attend_item


def attend_backward(allowed):

    def attend_item(packed):
        query_rows, key_rows, value_rows, query_docs, key_docs, log_total, grad_rows = packed
        scores, keep_mask = masked_scores(query_rows, key_rows, query_docs, key_docs, allowed)
        weights = jnp.where(keep_mask, jnp.exp(scores - log_total[:, None]), 0.0)
        grad_values = jnp.einsum(
            "qk,qd->kd", weights.astype(jnp.bfloat16), grad_rows, preferred_element_type=jnp.float32
        )
        grad_weights = jnp.einsum(
            "qd,kd->qk", grad_rows, value_rows, preferred_element_type=jnp.float32
        )
        centered = jnp.sum(weights * grad_weights, axis=-1, keepdims=True)
        grad_scores = (weights * (grad_weights - centered)).astype(jnp.bfloat16)
        grad_query = jnp.dot(grad_scores, key_rows, preferred_element_type=jnp.float32) * 0.125
        grad_keys = (
            jnp.einsum("qk,qd->kd", grad_scores, query_rows, preferred_element_type=jnp.float32)
            * 0.125
        )
        return (grad_query, grad_keys, grad_values)

    return attend_item


def layer_forward(stream, params, segments, key_docs, allowed, cycle_steps):
    (
        first_gain,
        first_shift,
        merged_weight,
        merged_bias,
        output_weight,
        output_bias,
        second_gain,
        second_shift,
        expand_weight,
        expand_bias,
        reduce_weight,
        reduce_bias,
    ) = params
    fetched = (
        lax.all_gather(first_gain, "dp", axis=0, tiled=True),
        lax.all_gather(first_shift, "dp", axis=0, tiled=True),
        lax.all_gather(merged_weight, "dp", axis=0, tiled=True),
        lax.all_gather(merged_bias, "dp", axis=2, tiled=True),
        lax.all_gather(output_weight, "dp", axis=1, tiled=True),
        lax.all_gather(output_bias, "dp", axis=0, tiled=True),
        lax.all_gather(second_gain, "dp", axis=0, tiled=True),
        lax.all_gather(second_shift, "dp", axis=0, tiled=True),
        lax.all_gather(expand_weight, "dp", axis=0, tiled=True),
        lax.all_gather(expand_bias, "dp", axis=1, tiled=True),
        lax.all_gather(reduce_weight, "dp", axis=1, tiled=True),
        lax.all_gather(reduce_bias, "dp", axis=0, tiled=True),
    )
    (
        first_gain,
        first_shift,
        merged_weight,
        merged_bias,
        output_weight,
        output_bias,
        second_gain,
        second_shift,
        expand_weight,
        expand_bias,
        reduce_weight,
        reduce_bias,
    ) = fetched
    head_count = merged_weight.shape[2] // HD
    normed = layer_norm(
        stream, first_gain.astype(jnp.float32), first_shift.astype(jnp.float32)
    ).astype(jnp.bfloat16)
    first_rows = spread_rows(normed)
    merged_out = jnp.einsum(
        "std,dkf->stkf", first_rows, merged_weight, preferred_element_type=jnp.float32
    )
    bias_pair = merged_bias.astype(jnp.float32).reshape(2, -1)
    query_rows = (merged_out[:, :, 0] + bias_pair[0]).astype(jnp.bfloat16)
    key_rows = merged_out[:, :, 1].astype(jnp.bfloat16)
    value_rows = (merged_out[:, :, 2] + bias_pair[1]).astype(jnp.bfloat16)
    key_list = [key_rows]
    value_list = [value_rows]
    moving = (key_rows, value_rows)
    for offset in range(cycle_steps):
        moving = from_behind((moving[0], moving[1]), "ctx", 1)
        key_list.insert(0, moving[0])
        value_list.insert(0, moving[1])
    query_items = to_items(query_rows, head_count)
    key_items = to_items(jnp.concatenate(key_list, axis=1), head_count)
    value_items = to_items(jnp.concatenate(value_list, axis=1), head_count)
    query_docs = jnp.repeat(segments, head_count, axis=0)
    window_docs = jnp.repeat(key_docs, head_count, axis=0)
    mixed_items, log_total = lax.map(
        attend_forward(allowed), (query_items, key_items, value_items, query_docs, window_docs)
    )
    mixed = from_items(mixed_items, head_count)
    attn_part = jnp.einsum("stf,fd->std", mixed, output_weight, preferred_element_type=jnp.float32)
    middle = stream + gather_sums(attn_part) + output_bias.astype(jnp.float32)
    normed_two = layer_norm(
        middle, second_gain.astype(jnp.float32), second_shift.astype(jnp.float32)
    ).astype(jnp.bfloat16)
    second_rows = spread_rows(normed_two)
    hidden = jnp.einsum(
        "std,df->stf", second_rows, expand_weight, preferred_element_type=jnp.float32
    ) + expand_bias.astype(jnp.float32).reshape(-1)
    activated = gelu_tanh(hidden).astype(jnp.bfloat16)
    mlp_part = jnp.einsum(
        "stf,fd->std", activated, reduce_weight, preferred_element_type=jnp.float32
    )
    result = middle + gather_sums(mlp_part) + reduce_bias.astype(jnp.float32)
    saved_state = (
        fetched,
        stream,
        first_rows,
        query_items,
        key_items,
        value_items,
        query_docs,
        window_docs,
        log_total,
        mixed,
        middle,
        second_rows,
        hidden,
        activated,
    )
    return (result, saved_state)


def reduce_grads(fresh):
    (
        gain_one,
        shift_one,
        merged_weights,
        merged_biases,
        output_weights,
        output_biases,
        gain_two,
        shift_two,
        expand_weights,
        expand_biases,
        reduce_weights,
        reduce_biases,
    ) = fresh
    summed = (
        lax.psum(gain_one.astype(jnp.bfloat16), "ctx").astype(jnp.float32),
        lax.psum(shift_one.astype(jnp.bfloat16), "ctx").astype(jnp.float32),
        lax.psum(merged_weights.astype(jnp.bfloat16), "ctx").astype(jnp.float32),
        lax.psum(merged_biases.astype(jnp.bfloat16), "ctx").astype(jnp.float32),
        lax.psum(output_weights.astype(jnp.bfloat16), "ctx").astype(jnp.float32),
        lax.psum(output_biases.astype(jnp.bfloat16), "ctx").astype(jnp.float32),
        lax.psum(gain_two.astype(jnp.bfloat16), "ctx").astype(jnp.float32),
        lax.psum(shift_two.astype(jnp.bfloat16), "ctx").astype(jnp.float32),
        lax.psum(expand_weights.astype(jnp.bfloat16), "ctx").astype(jnp.float32),
        lax.psum(expand_biases.astype(jnp.bfloat16), "ctx").astype(jnp.float32),
        lax.psum(reduce_weights.astype(jnp.bfloat16), "ctx").astype(jnp.float32),
        lax.psum(reduce_biases.astype(jnp.bfloat16), "ctx").astype(jnp.float32),
    )
    (
        gain_one,
        shift_one,
        merged_weights,
        merged_biases,
        output_weights,
        output_biases,
        gain_two,
        shift_two,
        expand_weights,
        expand_biases,
        reduce_weights,
        reduce_biases,
    ) = summed
    return (
        lax.psum_scatter(
            gain_one.astype(jnp.bfloat16), "dp", scatter_dimension=0, tiled=True
        ).astype(jnp.float32),
        lax.psum_scatter(
            shift_one.astype(jnp.bfloat16), "dp", scatter_dimension=0, tiled=True
        ).astype(jnp.float32),
        lax.psum_scatter(
            merged_weights.astype(jnp.bfloat16), "dp", scatter_dimension=0, tiled=True
        ).astype(jnp.float32),
        lax.psum_scatter(
            merged_biases.astype(jnp.bfloat16), "dp", scatter_dimension=2, tiled=True
        ).astype(jnp.float32),
        lax.psum_scatter(
            output_weights.astype(jnp.bfloat16), "dp", scatter_dimension=1, tiled=True
        ).astype(jnp.float32),
        lax.psum_scatter(
            output_biases.astype(jnp.bfloat16), "dp", scatter_dimension=0, tiled=True
        ).astype(jnp.float32),
        lax.psum_scatter(
            gain_two.astype(jnp.bfloat16), "dp", scatter_dimension=0, tiled=True
        ).astype(jnp.float32),
        lax.psum_scatter(
            shift_two.astype(jnp.bfloat16), "dp", scatter_dimension=0, tiled=True
        ).astype(jnp.float32),
        lax.psum_scatter(
            expand_weights.astype(jnp.bfloat16), "dp", scatter_dimension=0, tiled=True
        ).astype(jnp.float32),
        lax.psum_scatter(
            expand_biases.astype(jnp.bfloat16), "dp", scatter_dimension=1, tiled=True
        ).astype(jnp.float32),
        lax.psum_scatter(
            reduce_weights.astype(jnp.bfloat16), "dp", scatter_dimension=1, tiled=True
        ).astype(jnp.float32),
        lax.psum_scatter(
            reduce_biases.astype(jnp.bfloat16), "dp", scatter_dimension=0, tiled=True
        ).astype(jnp.float32),
    )


def layer_backward(grad_out, saved_state, allowed, cycle_steps, token_count):
    (
        fetched,
        stream,
        first_rows,
        query_items,
        key_items,
        value_items,
        query_docs,
        window_docs,
        log_total,
        mixed,
        middle,
        second_rows,
        hidden,
        activated,
    ) = saved_state
    (
        first_gain,
        first_shift,
        merged_weight,
        merged_bias,
        output_weight,
        output_bias,
        second_gain,
        second_shift,
        expand_weight,
        expand_bias,
        reduce_weight,
        reduce_bias,
    ) = fetched
    head_count = merged_weight.shape[2] // HD
    grad_branch = spread_rows(grad_out.astype(jnp.bfloat16))
    grad_reduce = jnp.einsum(
        "stf,std->fd", activated, grad_branch, preferred_element_type=jnp.float32
    )
    grad_active = jnp.einsum(
        "std,fd->stf", grad_branch, reduce_weight, preferred_element_type=jnp.float32
    )
    _, gelu_pull = jax.vjp(gelu_tanh, hidden)
    grad_hidden = gelu_pull(grad_active)[0].astype(jnp.bfloat16)
    grad_expand_bias = jnp.sum(grad_hidden, axis=(0, 1), dtype=jnp.float32).reshape(
        expand_bias.shape
    )
    grad_expand = jnp.einsum(
        "std,stf->df", second_rows, grad_hidden, preferred_element_type=jnp.float32
    )
    grad_second = gather_sums(
        jnp.einsum("stf,df->std", grad_hidden, expand_weight, preferred_element_type=jnp.float32)
    )
    _, second_pull = jax.vjp(
        layer_norm, middle, second_gain.astype(jnp.float32), second_shift.astype(jnp.float32)
    )
    grad_norm_mid, grad_second_gain, grad_second_shift = second_pull(grad_second)
    grad_middle = grad_out + grad_norm_mid
    grad_reduce_bias = jnp.sum(grad_out, axis=(0, 1))
    grad_attend = spread_rows(grad_middle.astype(jnp.bfloat16))
    grad_output = jnp.einsum("stf,std->fd", mixed, grad_attend, preferred_element_type=jnp.float32)
    grad_mixed = jnp.einsum(
        "std,fd->stf", grad_attend, output_weight, preferred_element_type=jnp.float32
    ).astype(jnp.bfloat16)
    grad_query_items, grad_key_items, grad_value_items = lax.map(
        attend_backward(allowed),
        (
            query_items,
            key_items,
            value_items,
            query_docs,
            window_docs,
            log_total,
            to_items(grad_mixed, head_count),
        ),
    )
    grad_query = from_items(grad_query_items, head_count)
    window_keys = from_items(grad_key_items, head_count)
    window_values = from_items(grad_value_items, head_count)
    local_keys = window_keys[:, cycle_steps * token_count :]
    local_values = window_values[:, cycle_steps * token_count :]
    carried = None
    for offset in range(cycle_steps, 0, -1):
        start_row = (cycle_steps - offset) * token_count
        block_keys = window_keys[:, start_row : start_row + token_count]
        block_values = window_values[:, start_row : start_row + token_count]
        if carried is not None:
            block_keys = block_keys + carried[0]
            block_values = block_values + carried[1]
        carried = (
            from_behind(block_keys.astype(jnp.bfloat16), "ctx", -1).astype(block_keys.dtype),
            from_behind(block_values.astype(jnp.bfloat16), "ctx", -1).astype(block_values.dtype),
        )
    local_keys = local_keys + carried[0]
    local_values = local_values + carried[1]
    grad_merged = jnp.stack([grad_query, local_keys, local_values], axis=2).astype(jnp.bfloat16)
    grad_merged_bias = jnp.stack(
        [
            jnp.sum(grad_merged[:, :, 0], axis=(0, 1), dtype=jnp.float32),
            jnp.sum(grad_merged[:, :, 2], axis=(0, 1), dtype=jnp.float32),
        ]
    ).reshape(merged_bias.shape)
    grad_merged_weight = jnp.einsum(
        "std,stkf->dkf", first_rows, grad_merged, preferred_element_type=jnp.float32
    )
    grad_first = gather_sums(
        jnp.einsum("stkf,dkf->std", grad_merged, merged_weight, preferred_element_type=jnp.float32)
    )
    _, first_pull = jax.vjp(
        layer_norm, stream, first_gain.astype(jnp.float32), first_shift.astype(jnp.float32)
    )
    grad_norm_in, grad_first_gain, grad_first_shift = first_pull(grad_first)
    grad_input = grad_middle + grad_norm_in
    grad_output_bias = jnp.sum(grad_middle, axis=(0, 1))
    vector_grads = lax.psum(
        (
            grad_first_gain,
            grad_first_shift,
            grad_second_gain,
            grad_second_shift,
            grad_output_bias,
            grad_reduce_bias,
        ),
        "tp",
    )
    fresh = (
        vector_grads[0],
        vector_grads[1],
        grad_merged_weight,
        grad_merged_bias,
        grad_output,
        vector_grads[4],
        vector_grads[2],
        vector_grads[3],
        grad_expand,
        grad_expand_bias,
        grad_reduce,
        vector_grads[5],
    )
    return (grad_input, reduce_grads(fresh))


def general_shards(
    inputs,
    segments,
    cotangent,
    student_first_gain,
    student_first_shift,
    student_merged_weight,
    student_merged_bias,
    student_output_weight,
    student_output_bias,
    student_second_gain,
    student_second_shift,
    student_expand_weight,
    student_expand_bias,
    student_reduce_weight,
    student_reduce_bias,
    teacher_first_gain,
    teacher_first_shift,
    teacher_merged_weight,
    teacher_merged_bias,
    teacher_output_weight,
    teacher_output_bias,
    teacher_second_gain,
    teacher_second_shift,
    teacher_expand_weight,
    teacher_expand_bias,
    teacher_reduce_weight,
    teacher_reduce_bias,
):
    student = (
        student_first_gain,
        student_first_shift,
        student_merged_weight,
        student_merged_bias,
        student_output_weight,
        student_output_bias,
        student_second_gain,
        student_second_shift,
        student_expand_weight,
        student_expand_bias,
        student_reduce_weight,
        student_reduce_bias,
    )
    teacher = (
        teacher_first_gain,
        teacher_first_shift,
        teacher_merged_weight,
        teacher_merged_bias,
        teacher_output_weight,
        teacher_output_bias,
        teacher_second_gain,
        teacher_second_shift,
        teacher_expand_weight,
        teacher_expand_bias,
        teacher_reduce_weight,
        teacher_reduce_bias,
    )
    token_count = segments.shape[1]
    context_size = lax.axis_size("ctx")
    context_index = lax.axis_index("ctx")
    doc_long = min(DOC_MAX, token_count * context_size // 2)
    cycle_steps = min((doc_long - 2) // token_count + 1, context_size - 1)
    doc_list = [segments]
    moving = segments
    for offset in range(cycle_steps):
        moving = from_behind(moving, "ctx", 1)
        doc_list.insert(0, moving)
    key_docs = jnp.concatenate(doc_list, axis=1)
    places = jnp.arange((cycle_steps + 1) * token_count, dtype=jnp.int32)
    relative = places - cycle_steps * token_count
    source = cycle_steps - places // token_count
    query_place = jnp.arange(token_count, dtype=jnp.int32)
    allowed = (relative[None, :] <= query_place[:, None]) & (source <= context_index)[None, :]
    stream = inputs.astype(jnp.float32)
    middle_stream, student_saved = layer_forward(
        stream, student, segments, key_docs, allowed, cycle_steps
    )
    final_stream, teacher_saved = layer_forward(
        middle_stream, teacher, segments, key_docs, allowed, cycle_steps
    )
    teacher_in_grad, teacher_grads = layer_backward(
        cotangent.astype(jnp.float32), teacher_saved, allowed, cycle_steps, token_count
    )
    input_grad, student_grads = layer_backward(
        teacher_in_grad, student_saved, allowed, cycle_steps, token_count
    )
    return (
        (final_stream.astype(jnp.bfloat16), input_grad)
        + tuple(student_grads)
        + tuple(teacher_grads)
    )


BF16 = jnp.bfloat16
F32 = jnp.float32
NEG = -1e30
TILE = 256
RELATIVE = (0, 2, 1, 3)


def row_major(value):
    return with_layout_constraint(value, Layout(major_to_minor=tuple(range(value.ndim))))


def swap(value, axis, bit):
    route = [(i, i ^ bit) for i in range(lax.axis_size(axis))]
    if value.ndim == 2:
        return row_major(lax.ppermute(row_major(value), axis, route))
    return lax.ppermute(value, axis, route)


def cross_core(value):
    return swap(value, "tp", 1)


def cross_x(value):
    return swap(value, "tp", 2)


def cross_y(value):
    return swap(value, "ctx", 1)


def cross_near(value):
    return swap(value, "dp", 1)


def cross_far(value):
    return swap(value, "dp", 2)


def cross_both(value):
    return swap(value, "dp", 3)


def stacked(*values):
    return jnp.concatenate(values, axis=0)


def beside(*values):
    return jnp.concatenate(values, axis=1)


def y_order(own, other, y_index, axis):
    return jnp.where(
        y_index == 0,
        jnp.concatenate([own, other], axis=axis),
        jnp.concatenate([other, own], axis=axis),
    )


def pin(*values):
    return lax.optimization_barrier(values)


def window_start(block, doc_max):
    return max(0, (block * TILE - doc_max + 1) // TILE) * TILE


def upright(line):
    size = line.shape[1]
    rows = lax.broadcasted_iota(jnp.int32, (size, size), 0)
    columns = lax.broadcasted_iota(jnp.int32, (size, size), 1)
    return jnp.sum(jnp.where(rows == columns, line, 0.0), axis=1, keepdims=True)


def join(pieces, whole):
    row, column = 0, 0
    most = whole.shape[0] * whole.shape[1] // sum(piece.shape[1] for piece in pieces)
    for piece in pieces:
        rows = min(piece.shape[0], most) if len(pieces) == 4 else piece.shape[0]
        whole[row : row + rows, column : column + piece.shape[1]] = piece[:rows, :]
        row += rows
        if row == whole.shape[0]:
            row, column = 0, column + piece.shape[1]


def dot_across(left, right):
    return lax.dot_general(left, right, (((1,), (1,)), ((), ())), preferred_element_type=F32)


def dot_down(left, right):
    return lax.dot_general(left, right, (((0,), (0,)), ((), ())), preferred_element_type=F32)


def token_place(me, member, half, rows):
    return pl.multiple_of((half * 4 + (me ^ (2 * (member & 1) + (member >> 1)))) * rows, rows)


def flat(column):
    size = column.shape[0]
    rows = lax.broadcasted_iota(jnp.int32, (size, size), 0)
    columns = lax.broadcasted_iota(jnp.int32, (size, size), 1)
    return jnp.sum(jnp.where(rows == columns, column, 0.0), axis=0, keepdims=True)


def fill_masks_across(docs, masks, doc_max):
    for block in range(docs.shape[1] // TILE):
        start, stop = window_start(block, doc_max), (block + 1) * TILE
        here = slice(block * TILE, stop)
        rows = block * TILE + lax.broadcasted_iota(jnp.int32, (TILE, stop - start), 0)
        columns = start + lax.broadcasted_iota(jnp.int32, (TILE, stop - start), 1)
        same = upright(docs[:, here]) == docs[:, start:stop]
        masks[here, : stop - start] = jnp.where(same & (columns <= rows), 0.0, NEG)


def mask_columns(length, doc_max):
    return max((block + 1) * TILE - window_start(block, doc_max) for block in range(length // TILE))


def fill_masks(docs, masks, doc_max):
    at = 0
    for block in range(docs.shape[1] // TILE):
        start = window_start(block, doc_max)
        size = (block + 1) * TILE - start
        for first in range(0, size, TILE):
            keys = slice(start + first, start + first + TILE)
            same = upright(docs[:, keys]) == docs[:, block * TILE : (block + 1) * TILE]
            if start + first == block * TILE:
                rows = lax.broadcasted_iota(jnp.int32, (TILE, TILE), 0)
                columns = lax.broadcasted_iota(jnp.int32, (TILE, TILE), 1)
                same = same & (rows <= columns)
            masks[at : at + TILE, :] = jnp.where(same, 0.0, NEG)
            at += TILE


def mask_rows(length, doc_max):
    return sum(
        (block + 1) * TILE - window_start(block, doc_max) for block in range(length // TILE)
    )


def split_heads(value, target, first, me, member):
    rows = value.shape[0] // 2
    for half in range(2):
        place = pl.ds(token_place(me, member, half, rows), rows)
        for j in range(value.shape[1] // HD):
            target[first + j, place, :] = value[half * rows : (half + 1) * rows, j * HD : (j + 1) * HD]


def merge_heads(source, me, member, rows):
    return jnp.concatenate(
        [
            jnp.concatenate(
                [
                    source[j, pl.ds(token_place(me, member, half, rows), rows), :]
                    for j in range(source.shape[0])
                ],
                axis=1,
            )
            for half in range(2)
        ],
        axis=0,
    )


def by_member(count, step):
    for i in range(count):
        step(i)


def attention_forward_kernel(
    heads,
    doc_max,
    count,
    scaled,
    me_ref,
    near_ref,
    far_ref,
    bias_ref,
    docs,
    *refs,
):
    mixed, attend_ref, masks = refs[-3:]
    refs = refs[:-3]
    sources = (near_ref, far_ref)
    if scaled:
        gains, refs, normed = refs[0], refs[1:-2], refs[-2:]
        for source, target in zip(sources, normed):
            target[...] = (source[...].astype(F32) * gains[0:1, :] + gains[1:2, :]).astype(BF16)
        sources = normed
    pieces, (sent_ref, kept_ref, split_ref, mixed_ref, log_ref) = refs[:count], refs[count:]
    join(pieces, attend_ref)
    fill_masks_across(docs, masks, doc_max)
    me = me_ref[0]
    width = heads * HD
    size = near_ref.shape[0] // 2
    length = 4 * size
    for source, first in zip(sources, (0, 2)):

        def project(i, source=source, first=first):
            at = pl.ds(pl.multiple_of(i * size, size), size)
            value = jnp.dot(source[at, :], attend_ref[:, : 3 * width], preferred_element_type=F32)
            value = (value + bias_ref[...]).astype(BF16)
            split_heads(value[:, :width] * BF16(0.125), split_ref, 0, me, first + i)
            split_heads(value[:, width:], split_ref, heads, me, first + i)

        by_member(2, project)

    def attend(h):
        for block in range(length // TILE):
            start, stop = window_start(block, doc_max), (block + 1) * TILE
            here = slice(block * TILE, stop)
            key, value = split_ref[heads + h, start:stop, :], split_ref[2 * heads + h, start:stop, :]
            scores = dot_across(split_ref[h, here, :], key) + masks[here, : stop - start]
            top = jnp.max(scores, axis=1, keepdims=True)
            raised = jnp.exp(scores - top)
            total = jnp.sum(raised, axis=1, keepdims=True)
            product = jnp.dot(raised.astype(BF16), value, preferred_element_type=F32)
            mixed[h, here, :] = (product * (1.0 / total)).astype(BF16)
            log_ref[h, :, here] = flat(top + jnp.log(total))

    lax.fori_loop(0, heads, lambda h, carry: (attend(h), carry)[1], 0)
    for out, first in ((sent_ref, 2), (kept_ref, 0)):

        def finish(i, out=out, first=first):
            rows = merge_heads(mixed, me, first + i, size // 2)
            mixed_ref[pl.ds(pl.multiple_of((first + i) * size, size), size), :] = rows
            at = pl.ds(pl.multiple_of(i * size, size), size)
            out[at, :] = dot_across(rows, attend_ref[:, 3 * width :]).astype(out.dtype)

        by_member(2, finish)


def attention_backward_kernel(
    heads,
    doc_max,
    count,
    me_ref,
    near_ref,
    far_ref,
    docs,
    split_ref,
    log_ref,
    *refs,
):
    pieces, (sent_ref, kept_ref, out_ref, sum_ref) = refs[:count], refs[count:-4]
    grad, total, attend_ref, masks = refs[-4:]
    join(pieces, attend_ref)
    fill_masks(docs, masks, doc_max)
    me = me_ref[0]
    width = heads * HD
    size = near_ref.shape[0] // 2
    length = 4 * size
    for source, first in ((near_ref, 0), (far_ref, 2)):

        def project(i, source=source, first=first):
            at = pl.ds(pl.multiple_of(i * size, size), size)
            value = jnp.dot(source[at, :], attend_ref[:, 3 * width :], preferred_element_type=F32)
            split_heads(value.astype(BF16), grad, 0, me, first + i)

        by_member(2, project)

    def attend(h):
        total[heads + h] = jnp.zeros((length, HD), F32)
        total[2 * heads + h] = jnp.zeros((length, HD), F32)
        at = 0
        for block in range(length // TILE):
            start, stop = window_start(block, doc_max), (block + 1) * TILE
            here, window = slice(block * TILE, stop), slice(start, stop)
            query, key, value = (
                split_ref[h, here, :],
                split_ref[heads + h, window, :],
                split_ref[2 * heads + h, window, :],
            )
            grad_rows = grad[h, here, :]
            scores = dot_across(key, query) + masks[at : at + stop - start, :]
            at += stop - start
            weights = jnp.exp(scores - log_ref[h, :, here])
            weighted = weights * dot_across(value, grad_rows)
            centered = jnp.sum(weighted, axis=0, keepdims=True)
            grad_scores = (weighted - weights * centered).astype(BF16)
            total[2 * heads + h, window, :] += jnp.dot(
                weights.astype(BF16), grad_rows, preferred_element_type=F32
            )
            total[heads + h, window, :] += jnp.dot(
                grad_scores, query, preferred_element_type=F32
            )
            total[h, here, :] = dot_down(key, grad_scores).T * 0.125

    lax.fori_loop(0, heads, lambda h, carry: (attend(h), carry)[1], 0)
    sum_ref[...] = jnp.zeros_like(sum_ref)
    for out, first in ((sent_ref, 2), (kept_ref, 0)):

        def finish(i, out=out, first=first):
            rows = merge_heads(total, me, first + i, size // 2).astype(BF16)
            out_ref[pl.ds(pl.multiple_of((first + i) * size, size), size), :] = rows
            sum_ref[...] += jnp.sum(rows.astype(F32), axis=0, keepdims=True)
            at = pl.ds(pl.multiple_of(i * size, size), size)
            out[at, :] = dot_across(rows, attend_ref[:, : 3 * width]).astype(out.dtype)

        by_member(2, finish)


VMEM = pl.BlockSpec(memory_space=pltpu.VMEM)
SMEM = pl.BlockSpec(memory_space=pltpu.SMEM)


def call(body, name, inputs, outputs, scratch, flops, transcendentals, limit=24):
    size = sum(v.size * v.dtype.itemsize for v in list(inputs) + list(outputs))
    return pl.pallas_call(
        body,
        out_shape=tuple(outputs),
        in_specs=[SMEM if v.ndim == 1 else VMEM for v in inputs],
        out_specs=tuple(VMEM for _ in outputs),
        scratch_shapes=scratch,
        cost_estimate=pl.CostEstimate(
            flops=flops, transcendentals=transcendentals, bytes_accessed=size
        ),
        compiler_params=pltpu.CompilerParams(vmem_limit_bytes=limit << 20),
        name=name,
    )(*inputs)


def shaped(rows, columns, kind):
    return jax.ShapeDtypeStruct((rows, columns), kind)


def attention_forward(near, far, attend, bias, context, doc_max, gains=()):
    me, docs = context
    half, features = near.shape
    width = bias.shape[1] // 3
    heads = width // HD
    area = heads * 2 * half * half

    def body(*refs):
        attention_forward_kernel(heads, doc_max, len(attend), len(gains) > 0, *refs)

    return call(
        body,
        "attention_forward",
        (me, near, far, bias, docs) + tuple(gains) + tuple(attend),
        (
            shaped(half, features, BF16),
            shaped(half, features, F32),
            jax.ShapeDtypeStruct((3 * heads, 2 * half, HD), BF16),
            shaped(2 * half, width, BF16),
            jax.ShapeDtypeStruct((heads, 1, 2 * half), F32),
        )
        + (shaped(half, features, BF16),) * (2 * len(gains)),
        [
            pltpu.VMEM((heads, 2 * half, HD), BF16),
            pltpu.VMEM((features, 4 * width), BF16),
            pltpu.VMEM((2 * half, mask_columns(2 * half, doc_max)), F32),
        ],
        16 * HD * area,
        area,
    )


def attention_backward(near, far, attend, context, saved, doc_max):
    me, docs = context
    split, _, log_total = saved
    half, features = near.shape
    heads = split.shape[0] // 3
    width = heads * HD
    area = heads * 2 * half * half

    def body(*refs):
        attention_backward_kernel(heads, doc_max, len(attend), *refs)

    return call(
        body,
        "attention_backward",
        (me, near, far, docs, split, log_total) + tuple(attend),
        (
            shaped(half, features, BF16),
            shaped(half, features, F32),
            shaped(2 * half, 3 * width, BF16),
            shaped(1, 3 * width, F32),
        ),
        [
            pltpu.VMEM((heads, 2 * half, HD), BF16),
            pltpu.VMEM((3 * heads, 2 * half, HD), F32),
            pltpu.VMEM((features, 4 * width), BF16),
            pltpu.VMEM((mask_rows(2 * half, doc_max), TILE), F32),
        ],
        40 * HD * area,
        area,
    )


CHUNK = 256


def gelu_both(values):
    inner = GELU_SCALE * (values + 0.044715 * values * values * values)
    bent = jnp.tanh(inner)
    value = 0.5 * values * (1.0 + bent)
    slope = 0.5 * (1.0 + bent) + 0.5 * values * (1.0 - bent * bent) * GELU_SCALE * (
        1.0 + 3.0 * 0.044715 * values * values
    )
    return value, slope


def split_parts(weight):
    size = min(weight.shape[1], 768)
    return [slice(at, at + size) for at in range(0, weight.shape[1], size)]


def feed_forward_kernel(
    count, near_ref, far_ref, bias_ref, *refs
):
    sent_ref, kept_ref, expand_ref, reduce_ref = refs[-4:]
    join(refs[:count], expand_ref)
    join(refs[count:-4], reduce_ref)
    parts = split_parts(expand_ref)
    for piece, out in ((far_ref, sent_ref), (near_ref, kept_ref)):

        def step(i, carry):
            at = pl.ds(pl.multiple_of(i * CHUNK, CHUNK), CHUNK)
            rows = piece[at, :]
            total = None
            for columns in parts:
                hidden = jnp.dot(rows, expand_ref[:, columns], preferred_element_type=F32)
                active = gelu_tanh(hidden + bias_ref[:, columns]).astype(BF16)
                product = dot_across(active, reduce_ref[:, columns])
                total = product if total is None else total + product
            out[at, :] = total.astype(out.dtype)
            return carry

        lax.fori_loop(0, piece.shape[0] // CHUNK, step, 0)


def feed_forward(near, far, expand, reduce, bias):
    half, features = near.shape
    hidden = bias.shape[1]

    def body(*refs):
        feed_forward_kernel(len(expand), *refs)

    return call(
        body,
        "feed_forward",
        (near, far, bias) + tuple(expand) + tuple(reduce),
        (shaped(half, features, BF16), shaped(half, features, F32)),
        [pltpu.VMEM((features, hidden), BF16), pltpu.VMEM((features, hidden), BF16)],
        8 * half * features * hidden,
        2 * half * hidden,
    )


def feed_backward_kernel(
    count,
    near_ref,
    far_ref,
    near_grad,
    far_grad,
    bias_ref,
    *refs,
):
    sent_ref, kept_ref, active_ref, hidden_ref, sum_ref, expand_ref, reduce_ref = refs[-7:]
    join(refs[:count], expand_ref)
    join(refs[count:-7], reduce_ref)
    parts = split_parts(expand_ref)
    half = near_ref.shape[0]
    sum_ref[...] = jnp.zeros_like(sum_ref)
    for piece, grads, out, base in (
        (far_ref, far_grad, sent_ref, half),
        (near_ref, near_grad, kept_ref, 0),
    ):

        def step(i, carry):
            place = pl.multiple_of(i * CHUNK, CHUNK)
            at = pl.ds(place, CHUNK)
            whole = pl.ds(pl.multiple_of(base + place, CHUNK), CHUNK)
            rows = piece[at, :]
            grad_rows = grads[at, :]
            total = None
            for columns in parts:
                hidden = jnp.dot(rows, expand_ref[:, columns], preferred_element_type=F32)
                value, slope = gelu_both(hidden + bias_ref[:, columns])
                active_ref[whole, columns] = value.astype(BF16)
                grad_active = jnp.dot(
                    grad_rows, reduce_ref[:, columns], preferred_element_type=F32
                )
                grad_hidden = (grad_active * slope).astype(BF16)
                hidden_ref[whole, columns] = grad_hidden
                sum_ref[:, columns] += jnp.sum(grad_hidden.astype(F32), axis=0, keepdims=True)
                product = dot_across(grad_hidden, expand_ref[:, columns])
                total = product if total is None else total + product
            out[at, :] = total.astype(out.dtype)
            return carry

        lax.fori_loop(0, half // CHUNK, step, 0)


def feed_backward(near, far, near_grad, far_grad, expand, reduce, bias):
    half, features = near.shape
    hidden = bias.shape[1]

    def body(*refs):
        feed_backward_kernel(len(expand), *refs)

    return call(
        body,
        "feed_backward",
        (near, far, near_grad, far_grad, bias) + tuple(expand) + tuple(reduce),
        (
            shaped(half, features, BF16),
            shaped(half, features, F32),
            shaped(2 * half, hidden, BF16),
            shaped(2 * half, hidden, BF16),
            shaped(1, hidden, F32),
        ),
        [pltpu.VMEM((features, hidden), BF16), pltpu.VMEM((features, hidden), BF16)],
        12 * half * features * hidden,
        2 * half * hidden,
    )


def row_block(rows, columns):
    return pl.BlockSpec((rows, columns), lambda i: (0, 0))


def row_call(body, name, inputs, rows, outputs):
    specs = [row_block(v.shape[0] if v.shape[0] <= 16 else rows, v.shape[1]) for v in inputs]
    size = sum(rows * v.shape[1] * v.dtype.itemsize for v in inputs)
    return pl.pallas_call(
        body,
        grid=(1,),
        out_shape=tuple(outputs),
        in_specs=specs,
        out_specs=tuple(row_block(*v.shape) for v in outputs),
        cost_estimate=pl.CostEstimate(
            flops=20 * rows * inputs[0].shape[1], transcendentals=rows, bytes_accessed=2 * size
        ),
        compiler_params=pltpu.CompilerParams(vmem_limit_bytes=18 << 20),
        name=name,
    )(*inputs)


STEP = 128


def add_norm(base, partial, across, vectors, bias_at, norm_vectors, norm_at):
    rows, columns = base.shape

    def body(base_ref, bias_ref, vector_ref, partial_ref, across_ref, sum_ref, norm_ref):
        bias = bias_ref[bias_at : bias_at + 1, :]
        gain, shift = vector_ref[norm_at : norm_at + 1, :], vector_ref[norm_at + 1 : norm_at + 2, :]

        def step(i, carry):
            here = pl.ds(pl.multiple_of(i * STEP, STEP), STEP)
            there = pl.ds(pl.multiple_of((i * STEP + rows // 2) % rows, STEP), STEP)
            total = partial_ref[here, :].astype(F32) + across_ref[there, :].astype(F32)
            total = base_ref[here, :].astype(F32) + bias + total
            sum_ref[here, :] = total
            norm_ref[here, :] = (normalize(total)[0] * gain + shift).astype(BF16)
            return carry

        lax.fori_loop(0, rows // STEP, step, 0)

    return row_call(
        body,
        "add_norm",
        [base, vectors, norm_vectors, partial, across],
        rows,
        (shaped(rows, columns, F32), shaped(rows, columns, BF16)),
    )


def norm_back_near(skip, partial, across, value, vectors, norm_at, sums, sums_at):
    rows, columns = skip.shape

    def body(skip_ref, value_ref, vector_ref, old_ref, partial_ref, across_ref, *outs):
        grad_ref, low_ref, sum_ref = outs
        gain = vector_ref[norm_at : norm_at + 1, :]
        sum_ref[...] = old_ref[...]

        def step(i, own):
            here = pl.ds(pl.multiple_of(i * STEP, STEP), STEP)
            there = pl.ds(pl.multiple_of((i * STEP + rows // 2) % rows, STEP), STEP)
            grad = partial_ref[here, :].astype(F32) + across_ref[there, :].astype(F32)
            unit, scale = normalize(value_ref[here, :].astype(F32))
            skipped = skip_ref[here, :].astype(F32)
            if own:
                for j, each in enumerate((grad * unit, grad, skipped)):
                    sum_ref[sums_at + j : sums_at + j + 1, :] += jnp.sum(each, axis=0, keepdims=True)
            total = skipped + norm_pullback(grad, unit, scale, gain)
            grad_ref[here, :] = total
            low_ref[here, :] = total.astype(BF16)

        count = rows // STEP // 2
        lax.fori_loop(0, count, lambda i, carry: (step(i, True), carry)[1], 0)
        lax.fori_loop(count, 2 * count, lambda i, carry: (step(i, False), carry)[1], 0)

    return row_call(
        body,
        "norm_back_near",
        [skip, value, vectors, sums, partial, across],
        rows,
        (shaped(rows, columns, F32), shaped(rows, columns, BF16), shaped(16, columns, F32)),
    )


def norm_only(values):
    rows, columns = values.shape

    def body(value_ref, unit_ref):
        unit_ref[...] = normalize(value_ref[...].astype(F32))[0].astype(BF16)

    return row_call(body, "norm_only", [values], rows, (shaped(rows, columns, BF16),))[0]


def norm_back(skip, addends, value, vectors, norm_at, sums, sums_at):
    rows, columns = addends[-1].shape

    def body(*refs):
        skip_ref, value_ref, vector_ref, old_ref = refs[:4]
        parts, (grad_ref, low_ref, sum_ref) = refs[4:-3], refs[-3:]
        grad = parts[0][...].astype(F32)
        for part in parts[1:]:
            grad = grad + part[...].astype(F32)
        unit, scale = normalize(value_ref[...].astype(F32))
        skipped = skip_ref[...]
        sum_ref[...] = old_ref[...]
        for i, each in enumerate((grad * unit, grad, skipped)):
            sum_ref[sums_at + i : sums_at + i + 1, :] = jnp.sum(each, axis=0, keepdims=True)
        total = skipped + norm_pullback(grad, unit, scale, vector_ref[norm_at : norm_at + 1, :])
        grad_ref[...] = total
        low_ref[...] = total.astype(BF16)

    return row_call(
        body,
        "norm_back",
        [skip, value, vectors, sums] + list(addends),
        rows,
        (shaped(rows, columns, F32), shaped(rows, columns, BF16), shaped(16, columns, F32)),
    )


def normalize(values):
    center = values - jnp.mean(values, axis=-1, keepdims=True)
    spread = jnp.mean(center * center, axis=-1, keepdims=True)
    scale = lax.rsqrt(spread + EPSILON)
    return center * scale, scale


def norm_rows(values, gain, shift):
    return (normalize(values)[0] * gain + shift).astype(BF16)


def norm_pullback(grad, unit, scale, gain):
    inner = grad * gain
    return scale * (
        inner
        - jnp.mean(inner, axis=-1, keepdims=True)
        - unit * jnp.mean(inner * unit, axis=-1, keepdims=True)
    )


def times(left, right, kind=F32):
    return jnp.dot(left, right, preferred_element_type=F32).astype(kind)


def times_across(left, right, kind=F32):
    return dot_across(left, right).astype(kind)


def times_down(left, right, kind=F32):
    return row_major(dot_down(left, right).astype(kind))


def gather_rows(rows):
    near = stacked(rows, cross_x(rows))
    return near, cross_core(near)


def add_half(value, cross):
    middle = value.shape[0] // 2
    return value[:middle].astype(F32) + cross(value[middle:].astype(BF16)).astype(F32)


def add_columns(value, cross):
    middle = value.shape[1] // 2
    return value[:, :middle].astype(F32) + cross(value[:, middle:].astype(BF16)).astype(F32)


def column_halves(shard, y_index):
    middle = shard.shape[1] // 2
    own = jnp.where(y_index == 0, shard[:, :middle], shard[:, middle:])
    other = jnp.where(y_index == 0, shard[:, middle:], shard[:, :middle])
    return own, other


def natural_columns(own, other, y_index):
    return jnp.where(y_index == 0, beside(own, other), beside(other, own))


def order_matrix(width, z_index):
    rows = width // 4
    natural = lax.broadcasted_iota(jnp.int32, (width, width), 0)
    place = lax.broadcasted_iota(jnp.int32, (width, width), 1)
    step, inner = place // rows, place % rows
    distance = 2 * (step & 1) + (step >> 1)
    return (natural == (z_index ^ distance) * rows + inner).astype(BF16)


def my_rows(pair, y_index):
    own = jnp.where(y_index == 0, pair[0], pair[1])
    sent = jnp.where(y_index == 0, pair[1], pair[0])
    return y_order(own, cross_y(sent), y_index, 0)


ROWS = 64
SPARE = ROWS // 2


def turn(value):
    size = value.shape[0]
    eye = (
        lax.broadcasted_iota(jnp.int32, (size, size), 0)
        == lax.broadcasted_iota(jnp.int32, (size, size), 1)
    ).astype(BF16)
    return dot_down(value, eye)


def pack_vectors(blocks, place):
    flat = []
    for gains, merged_bias, expand_bias in blocks:
        flat += list(gains) + [merged_bias.transpose(1, 0, 2), expand_bias]

    number = len(flat)

    def body(*refs):
        refs = refs[1:]
        out, part, sem = refs[number], refs[number + 1 : -1], refs[-1]
        copies = [
            pltpu.make_async_copy(refs[i], part[i], sem.at[i]) for i in range(number)
        ]
        for copy in copies:
            copy.start()
        out[...] = jnp.zeros_like(out)
        for copy in copies:
            copy.wait()
        for b in range(2):
            vectors, merged_bias, expand_bias = part[8 * b : 8 * b + 6], part[8 * b + 6], part[8 * b + 7]
            for i in range(6):
                local = vectors[i].shape[0]
                out[6 * b + i : 6 * b + i + 1, :local] = vectors[i][...].astype(F32).reshape(1, local)
            for h in range(merged_bias.shape[0]):
                value = merged_bias[h].astype(F32)
                out[16 + 8 * b + 2 * h : 18 + 8 * b + 2 * h, : value.shape[1]] = value
            value = expand_bias[...].astype(F32)
            out[32 + 16 * b : 32 + 16 * b + value.shape[0], : value.shape[1]] = value

    return pl.pallas_call(
        body,
        out_shape=shaped(ROWS, 256, F32),
        in_specs=[SMEM] + [pl.BlockSpec(memory_space=pltpu.HBM)] * number,
        out_specs=VMEM,
        scratch_shapes=[pltpu.VMEM(v.shape, v.dtype) for v in flat]
        + [pltpu.SemaphoreType.DMA((number,))],
        compiler_params=pltpu.CompilerParams(vmem_limit_bytes=60 << 20),
        name="pack_vectors",
    )(place, *flat)


def prepare_first(place, merged, output, blocks):
    flat = []
    for gains, merged_bias, expand_bias in blocks:
        flat += list(gains) + [merged_bias.transpose(1, 0, 2), expand_bias]
    flat += [merged.transpose(1, 0, 2), output]
    number = len(flat)
    local = output.shape[1]

    def body(*refs):
        out, part, small, sem = refs[number], refs[number + 1 : -2], refs[-2], refs[-1]
        copies = [pltpu.make_async_copy(refs[i], part[i], sem.at[i]) for i in range(number)]
        for copy in copies:
            copy.start()
        small[...] = jnp.zeros_like(small)
        for copy in copies:
            copy.wait()
        for b in range(2):
            vectors, merged_bias, expand_bias = part[8 * b : 8 * b + 6], part[8 * b + 6], part[8 * b + 7]
            for i in range(6):
                small[6 * b + i : 6 * b + i + 1, :local] = (
                    vectors[i][...].astype(F32).reshape(1, local)
                )
            for h in range(merged_bias.shape[0]):
                value = merged_bias[h].astype(F32)
                small[16 + 8 * b + 2 * h : 18 + 8 * b + 2 * h, : value.shape[1]] = value
            value = expand_bias[...].astype(F32)
            small[32 + 16 * b : 32 + 16 * b + value.shape[0], : value.shape[1]] = value
        merged_ref, output_ref = part[-2:]
        pieces = [merged_ref[k] for k in range(3)] + [turn(output_ref[...]).astype(BF16)]
        out[:local, :] = jnp.concatenate(pieces, axis=1)
        out[local:, :256] = small[:SPARE, :].astype(BF16)
        out[local:, 256:512] = small[SPARE:, :].astype(BF16)
        out[local:, 512:] = jnp.zeros((SPARE, 4 * local - 512), BF16)

    return pl.pallas_call(
        body,
        out_shape=shaped(local + SPARE, 4 * local, BF16),
        in_specs=[pl.BlockSpec(memory_space=pltpu.HBM)] * number,
        out_specs=VMEM,
        scratch_shapes=[pltpu.VMEM(v.shape, v.dtype) for v in flat]
        + [pltpu.VMEM((ROWS, 256), F32), pltpu.SemaphoreType.DMA((number,))],
        compiler_params=pltpu.CompilerParams(vmem_limit_bytes=60 << 20),
        name="prepare_first",
    )(*flat)


def unpack_vectors(pieces, place, local, merged_shape, expand_shape):
    heads, few = merged_shape[1], merged_shape[2]
    groups = expand_shape[0]
    width = heads * 4 * few

    def body(place_ref, *refs):
        pieces, outs, pieces_ref = refs[:4], refs[4:-1], refs[-1]
        for k in range(4):
            for i in range(2):
                pieces_ref[k * ROWS + i * SPARE : k * ROWS + (i + 1) * SPARE, :] = pieces[k][
                    local:, 256 * i : 256 * (i + 1)
                ].astype(F32)
        y, z = place_ref[0], place_ref[1]
        for b in range(2):
            gains, bias, hidden = outs[3 * b : 3 * b + 3]
            for k in range(4):
                gains[0:6, k * local : (k + 1) * local] = pieces_ref[
                    k * ROWS + 6 * b : k * ROWS + 6 * b + 6, :local
                ]
            bias[...] = jnp.zeros_like(bias)
            for natural in range(4):
                distance = z ^ natural
                base = (2 * (distance & 1) + (distance >> 1)) * ROWS
                part = pieces_ref[pl.ds(pl.multiple_of(base, ROWS), ROWS), :128]
                for i in range(2):
                    for h in range(heads):
                        line = 16 + 8 * b + 2 * h + i
                        at = 2 * i * width + h * 4 * few + natural * few
                        bias[:, at : at + few] = part[line : line + 1, :few]
                lines = part[32 + 16 * b : 32 + 16 * b + groups]
                half = groups // 2
                lines = jnp.where(
                    y == 0, lines, jnp.concatenate([lines[half:], lines[:half]], axis=0)
                )
                for p in range(groups):
                    at = p * 4 * few + natural * few
                    hidden[:, at : at + few] = lines[p : p + 1, :few]

    one = (
        shaped(8, 4 * local, F32),
        shaped(1, 3 * width, F32),
        shaped(1, groups * 4 * few, F32),
    )
    return pl.pallas_call(
        body,
        out_shape=one + one,
        in_specs=[SMEM] + [VMEM] * 4,
        out_specs=(VMEM,) * 6,
        scratch_shapes=[pltpu.VMEM((4 * ROWS, 256), F32)],
        compiler_params=pltpu.CompilerParams(vmem_limit_bytes=8 << 20),
        name="unpack_vectors",
    )(place, *pieces)


def prepare_attend(merged, output):
    local = output.shape[1]

    def body(merged_ref, output_ref, attend):
        pieces = [merged_ref[k] for k in range(3)] + [turn(output_ref[...]).astype(BF16)]
        attend[...] = jnp.concatenate(pieces, axis=1)

    return pl.pallas_call(
        body,
        out_shape=shaped(local, 4 * local, BF16),
        in_specs=[VMEM, VMEM],
        out_specs=VMEM,
        compiler_params=pltpu.CompilerParams(vmem_limit_bytes=12 << 20),
        name="prepare_attend",
    )(merged.transpose(1, 0, 2), output)


def prepare_feed(place, expand, reduce):
    local, half = expand.shape[0], expand.shape[1] // 2

    def body(place_ref, expand_ref, reduce_ref, feed):
        y = place_ref[0]
        first, second = reduce_ref[:, :half], reduce_ref[:, half:]
        feed[:, :half] = jnp.where(y == 0, expand_ref[:, :half], expand_ref[:, half:])
        feed[:, half : 2 * half] = jnp.where(y == 0, first, second)
        feed[:, 2 * half :] = jnp.where(y == 0, second, first)

    return pl.pallas_call(
        body,
        out_shape=shaped(local, 3 * half, BF16),
        in_specs=[SMEM, VMEM, VMEM],
        out_specs=VMEM,
        compiler_params=pltpu.CompilerParams(vmem_limit_bytes=12 << 20),
        name="prepare_feed",
    )(place, expand, reduce.T)


def pack_grads(sums, biases, hiddens, place, local, merged_shape, expand_shape):
    heads, few = merged_shape[1], merged_shape[2]
    groups = expand_shape[0]
    width = heads * 4 * few

    def body(place_ref, sum_ref, bias_s, bias_t, hidden_s, hidden_t, out):
        y, z = place_ref[0], place_ref[1]
        out[...] = jnp.zeros_like(out)
        for k in range(4):
            out[k * ROWS : k * ROWS + 12, :local] = sum_ref[0:12, k * local : (k + 1) * local]
        for natural in range(4):
            distance = z ^ natural
            base = pl.multiple_of((2 * (distance & 1) + (distance >> 1)) * ROWS, ROWS)
            lines = []
            for bias in (bias_s, bias_t):
                for h in range(heads):
                    for i in range(2):
                        at = 2 * i * width + h * 4 * few + natural * few
                        lines.append(bias[:, at : at + few])
                lines.append(jnp.zeros((2, few), F32))
            for hidden in (hidden_s, hidden_t):
                rows = [
                    hidden[:, p * 4 * few + natural * few : p * 4 * few + natural * few + few]
                    for p in range(groups)
                ]
                first, second = rows[: groups // 2], rows[groups // 2 :]
                first, second = jnp.concatenate(first, axis=0), jnp.concatenate(second, axis=0)
                lines.append(jnp.where(y == 0, first, second))
                lines.append(jnp.where(y == 0, second, first))
                lines.append(jnp.zeros((16 - groups, few), F32))
            out[pl.ds(pl.multiple_of(base + 16, 16), ROWS - 16), :few] = jnp.concatenate(lines, axis=0)

    return pl.pallas_call(
        body,
        out_shape=shaped(4 * ROWS, 256, F32),
        in_specs=[SMEM] + [VMEM] * 5,
        out_specs=VMEM,
        compiler_params=pltpu.CompilerParams(vmem_limit_bytes=4 << 20),
        name="pack_grads",
    )(place, sums, *biases, *hiddens)


def unpack_grads(mine, arrived, local, merged_shape, expand_shape):
    heads, few = merged_shape[1], merged_shape[2]
    groups = expand_shape[0]

    def body(mine_ref, arrived_ref, *outs):
        total = mine_ref[0:ROWS, :] + arrived_ref[...]
        for b in range(2):
            vectors, merged_bias, expand_bias = outs[8 * b : 8 * b + 6], outs[8 * b + 6], outs[8 * b + 7]
            for i in range(6):
                vectors[i][...] = total[6 * b + i : 6 * b + i + 1, :local].reshape(local)
            for h in range(heads):
                merged_bias[h] = total[16 + 8 * b + 2 * h : 18 + 8 * b + 2 * h, :few]
            expand_bias[...] = total[32 + 16 * b : 32 + 16 * b + groups, :few]

    one = [jax.ShapeDtypeStruct((local,), F32)] * 6 + [
        jax.ShapeDtypeStruct((heads, 2, few), F32),
        jax.ShapeDtypeStruct(expand_shape, F32),
    ]
    values = pl.pallas_call(
        body,
        out_shape=tuple(one + one),
        in_specs=[VMEM] * 2,
        out_specs=(VMEM,) * 16,
        compiler_params=pltpu.CompilerParams(vmem_limit_bytes=4 << 20),
        name="unpack_grads",
    )(mine, arrived)
    return [v.transpose(1, 0, 2) if v.ndim == 3 else v for v in values]


def finish_feed(mine, theirs, place, half):
    local = mine.shape[0]
    whole = mine.shape[1] == 3 * half

    def body(place_ref, mine_ref, theirs_ref, expand, reduce):
        y = place_ref[0]
        own, other = mine_ref[:, :half].astype(F32), theirs_ref[:, :half].astype(F32)
        expand[:, :half] = jnp.where(y == 0, own, other)
        expand[:, half:] = jnp.where(y == 0, other, own)
        if whole:
            total = mine_ref[:, half:].astype(F32) + theirs_ref[:, half:].astype(F32)
            own, other = total[:, :half], total[:, half:]
        else:
            own, other = mine_ref[:, half:].astype(F32), theirs_ref[:, half:].astype(F32)
        reduce[:, :half] = jnp.where(y == 0, own, other)
        reduce[:, half:] = jnp.where(y == 0, other, own)

    expand, reduce = pl.pallas_call(
        body,
        out_shape=(shaped(local, 2 * half, F32), shaped(local, 2 * half, F32)),
        in_specs=[SMEM, VMEM, VMEM],
        out_specs=(VMEM, VMEM),
        compiler_params=pltpu.CompilerParams(vmem_limit_bytes=12 << 20),
        name="finish_feed",
    )(place, mine, theirs)
    return expand, reduce.T


def finish_attend(added, mine, theirs, place):
    local = mine.shape[0]

    def body(place_ref, *refs):
        mine_ref, theirs_ref, merged, output = refs[-4:]
        y = place_ref[0]
        own, other = mine_ref[...], theirs_ref[...]
        split = jnp.concatenate(
            [jnp.where(y == 0, own, other), jnp.where(y == 0, other, own)], axis=1
        )
        output[...] = turn(split[:, -local:])
        whole = split.astype(F32)
        if added:
            total = refs[0][...].astype(F32) + refs[1][...].astype(F32)
            whole = jnp.concatenate([total, whole], axis=1)
        for k in range(3):
            merged[k] = whole[:, k * local : (k + 1) * local]

    merged, output = pl.pallas_call(
        body,
        out_shape=(jax.ShapeDtypeStruct((3, local, local), F32), shaped(local, local, F32)),
        in_specs=[SMEM] + [VMEM] * (2 + len(added)),
        out_specs=(VMEM, VMEM),
        compiler_params=pltpu.CompilerParams(vmem_limit_bytes=12 << 20),
        name="finish_attend",
    )(place, *added, mine, theirs)
    return merged.transpose(1, 0, 2), output


def halves_added(kept, arrived):
    middle = kept.shape[0] // 2
    return (kept[middle:] + arrived[middle:].astype(F32)).astype(BF16)


def core_sum(kept, arrived):
    return (kept + arrived.astype(F32)).astype(BF16)


def send_columns(value, cross):
    middle = value.shape[1] // 2
    return cross(value[:, middle:].astype(BF16))


def keep_columns(value, arrived):
    return value[:, : value.shape[1] // 2].astype(F32) + arrived.astype(F32)


def send_rows(value, cross):
    middle = value.shape[0] // 2
    return cross(value[middle:].astype(BF16))


def keep_rows(value, arrived):
    return value[: value.shape[0] // 2].astype(F32) + arrived.astype(F32)


def fast_shards(inputs, segments, cotangent, *params):
    y_index = lax.axis_index("ctx")
    z_index = lax.axis_index("dp")
    me = lax.axis_index("tp")
    tokens, features = inputs.shape[1], inputs.shape[2]
    length = segments.shape[1] * 2
    doc_max = min(DOC_MAX, length // 2)
    blocks = (params[:12], params[12:])
    local = features // 4
    half = local * 2

    small = [((p[0], p[1], p[5], p[6], p[7], p[11]), p[3], p[9]) for p in blocks]
    place = jnp.stack([y_index, z_index]).astype(jnp.int32)
    p = blocks[0]
    attend = prepare_first(place, p[2], p[4], small)
    inputs, attend = pin(inputs, attend)
    far, near = cross_far(attend), cross_near(attend)
    sent_rows = jnp.where(y_index == 0, inputs[1], inputs[0])
    sent_docs = jnp.where(y_index == 0, segments[1:2], segments[0:1]).astype(BF16)
    sent_docs = jnp.pad(sent_docs, ((0, 15), (0, features - sent_docs.shape[1])))
    moved = cross_y(stacked(sent_rows, sent_docs))
    kept_rows = jnp.where(y_index == 0, inputs[0], inputs[1])
    kept_docs = jnp.where(y_index == 0, segments[0:1], segments[1:2]).astype(F32)
    chooser = order_matrix(features, z_index)
    raw = times(y_order(kept_rows, moved[:tokens], y_index, 0), chooser, BF16)
    docs = y_order(
        kept_docs, moved[tokens : tokens + 1, : kept_docs.shape[1]].astype(F32), y_index, 1
    )
    context = (me.astype(jnp.int32).reshape(1), docs)
    both = cross_near(far)
    feed = prepare_feed(place, blocks[0][8], blocks[0][10])
    feed, far = pin(feed, far)
    p_far = cross_far(feed[:, : 2 * half])
    moved_grad = cross_y(jnp.where(y_index == 0, cotangent[1], cotangent[0]))
    raw, place_t, output_t = pin(raw, place, blocks[1][4])
    own_a = prepare_attend(blocks[1][2], output_t)
    feed_t = prepare_feed(place_t, blocks[1][8], blocks[1][10])

    stream = stacked(raw, cross_x(raw))
    stream, near, both, p_far, own_a, feed_t, moved_grad = pin(
        stream, near, both, p_far, own_a, feed_t, moved_grad
    )
    near_s = norm_only(stream)
    gains_s, bias_s, hidden_s, gains_t, bias_t, hidden_t = unpack_vectors(
        (attend, far, near, both), place, local, blocks[0][3].shape, blocks[0][9].shape
    )
    far_s = cross_core(near_s)
    attend_s = (attend, far, near, both)
    e_two = stacked(feed[:, :half], p_far[:, :half])
    e_near = cross_near(e_two)
    r_far = cross_far(feed[:, 2 * half :])
    grad_out = times(
        y_order(jnp.where(y_index == 0, cotangent[0], cotangent[1]), moved_grad, y_index, 0),
        chooser,
        BF16,
    )
    moved_grad = cross_x(grad_out)
    sent, kept, *saved_s, near_s, far_s = attention_forward(
        near_s, far_s, attend_s, bias_s, context, doc_max, (gains_s,)
    )
    sent, e_near, r_far, moved_grad = pin(sent, e_near, r_far, moved_grad)
    e_s = stacked(e_two, e_near)
    e_other = cross_y(e_s)
    r_two = stacked(feed[:, half:], beside(p_far[:, half:], r_far))
    r_near = cross_near(r_two)
    a_far = cross_far(own_a)
    partial = core_sum(kept, cross_core(sent))
    middle_s, near_two_s = add_norm(stream, partial, cross_x(partial), gains_s, 2, gains_s, 3)
    near_two_s, e_other, r_near, a_far, feed_t = pin(near_two_s, e_other, r_near, a_far, feed_t)
    a_two = stacked(own_a, a_far)
    a_near = cross_near(a_two)
    te_far, tr_far = cross_far(feed_t[:, :half]), cross_far(feed_t[:, 2 * half :])
    far_two_s = cross_core(near_two_s)
    feed_s = (near_two_s, far_two_s), ((e_s, e_other), (r_two, r_near), hidden_s)
    sent, kept = feed_forward(*feed_s[0], *feed_s[1])
    partial = core_sum(kept, cross_core(sent))
    between, near_t = add_norm(middle_s, partial, cross_x(partial), gains_s, 5, gains_t, 0)

    near_t, a_near, te_far, tr_far, feed_t = pin(near_t, a_near, te_far, tr_far, feed_t)
    attend_t = (a_two, a_near)
    te_two = stacked(feed_t[:, :half], te_far)
    te_near = cross_near(te_two)
    tr_far_one = cross_far(feed_t[:, half : 2 * half])
    far_t = cross_core(near_t)
    sent, kept, *saved_t = attention_forward(near_t, far_t, attend_t, bias_t, context, doc_max)
    sent, te_near, tr_far_one = pin(sent, te_near, tr_far_one)
    te = stacked(te_two, te_near)
    te_other = cross_y(te)
    tr_two = stacked(feed_t[:, half:], beside(tr_far_one, tr_far))
    tr_near = cross_near(tr_two)
    branch = stacked(grad_out, moved_grad)
    branch_far = cross_core(branch)
    partial = core_sum(kept, cross_core(sent))
    middle_t, near_two_t = add_norm(between, partial, cross_x(partial), gains_t, 2, gains_t, 3)
    near_two_t, te_other, tr_near, branch_far = pin(near_two_t, te_other, tr_near, branch_far)
    far_two_t = cross_core(near_two_t)
    feed_t = (near_two_t, far_two_t), ((te, te_other), (tr_two, tr_near), hidden_t)

    sums = jnp.zeros((16, features), F32)
    sent, kept, active, grad_hidden, hidden_sum_t = feed_backward(
        *feed_t[0], branch, branch_far, *feed_t[1]
    )
    partial = core_sum(kept, cross_core(sent))
    final_sent, final_kept = feed_forward(*feed_t[0], *feed_t[1])
    part_r = times_down(stacked(branch, branch_far), active, BF16)
    part_e = times_down(stacked(near_two_t, far_two_t), grad_hidden, BF16)
    grad_middle, near_grad, sums = norm_back_near(
        branch, partial, cross_x(partial), middle_t, gains_t, 3, sums, 9
    )
    near_grad, part_r, part_e, final_sent, final_kept = pin(
        near_grad, part_r, part_e, final_sent, final_kept
    )
    r_moved, e_moved = send_rows(part_r, cross_near), send_columns(part_e, cross_y)
    far_grad = cross_core(near_grad)
    final_arrived = cross_core(final_sent)
    final_across = cross_x(halves_added(final_kept, final_arrived))
    sent, kept, grad_qkv, qkv_sum_t = attention_backward(
        near_grad, far_grad, attend_t, context, saved_t, doc_max
    )
    sent, final_across = pin(sent, final_across)
    partial = core_sum(kept, cross_core(sent))
    part_a = beside(
        times_down(stacked(near_t, far_t), grad_qkv, BF16),
        times_down(stacked(near_grad, far_grad), saved_t[1], BF16),
    )
    part_a = beside(*column_halves(part_a, y_index))
    grad_between, branch, sums = norm_back_near(
        grad_middle, partial, cross_x(partial), between, gains_t, 0, sums, 6
    )

    branch, r_moved, e_moved, part_a = pin(branch, r_moved, e_moved, part_a)
    part_e, part_r = keep_columns(part_e, e_moved), keep_rows(part_r, r_moved)
    e_moved, r_moved = send_rows(part_e, cross_near), send_rows(part_r, cross_far)
    a_moved = send_columns(part_a, cross_y)
    branch_far = cross_core(branch)
    sent, kept, active, grad_hidden, hidden_sum_s = feed_backward(
        *feed_s[0], branch, branch_far, *feed_s[1]
    )
    partial = core_sum(kept, cross_core(sent))
    feed_r = times_down(stacked(branch, branch_far), active, BF16)
    feed_e = times_down(stacked(near_two_s, far_two_s), grad_hidden, BF16)
    grad_middle, near_grad, sums = norm_back_near(
        grad_between, partial, cross_x(partial), middle_s, gains_s, 3, sums, 3
    )
    near_grad, e_moved, r_moved, a_moved, feed_e, feed_r = pin(
        near_grad, e_moved, r_moved, a_moved, feed_e, feed_r
    )
    part_e, part_r = keep_rows(part_e, e_moved), keep_rows(part_r, r_moved)
    part_a = keep_columns(part_a, a_moved)
    e_moved, a_moved = send_rows(part_e, cross_far), send_rows(part_a, cross_near)
    fe_moved = cross_y(feed_e[:half, half:])
    far_grad = cross_core(near_grad)
    sent, kept, grad_qkv, qkv_sum_s = attention_backward(
        near_grad, far_grad, attend_s, context, saved_s, doc_max
    )
    sent, e_moved, a_moved, fe_moved, feed_r = pin(sent, e_moved, a_moved, fe_moved, feed_r)
    part_e, part_a = keep_rows(part_e, e_moved), keep_rows(part_a, a_moved)
    fe_moved_two = cross_y(feed_e[half:, half:])
    fr_moved, at_moved = send_rows(feed_r, cross_near), send_rows(part_a, cross_far)
    arrived = cross_core(sent)
    across = cross_x(halves_added(kept, arrived))
    grad_a = beside(
        times_down(stacked(near_s, far_s), grad_qkv, BF16),
        times_down(stacked(near_grad, far_grad), saved_s[1], BF16),
    )
    whole = features - 256
    grad_z, grad_a = grad_a[:, :whole], grad_a[:, whole:]
    grad_a, y_moved = column_halves(grad_a, y_index)
    y_moved, z_moved = cross_y(y_moved), send_rows(grad_z, cross_near)
    grad_in, _, sums = norm_back(
        grad_middle, (kept, arrived, across), stream, gains_s, 0, sums, 0
    )
    sums_moved = cross_core(sums)
    input_grad = lax.dot_general(
        grad_in,
        chooser.astype(F32),
        (((1,), (1,)), ((), ())),
        precision=lax.Precision.HIGHEST,
        preferred_element_type=F32,
    )

    def swapped(value):
        first, second = value[:tokens], value[tokens:]
        return cross_y(jnp.where(y_index == 0, second, first))

    def restore(value, received):
        kept = jnp.where(y_index == 0, value[:tokens], value[tokens:])
        return jnp.where(y_index == 0, jnp.stack([kept, received]), jnp.stack([received, kept]))

    y_moved, z_moved, sums_moved, input_grad, fe_moved_two, fr_moved, at_moved = pin(
        y_moved, z_moved, sums_moved, input_grad, fe_moved_two, fr_moved, at_moved
    )
    grad_a = grad_a.astype(F32) + y_moved.astype(F32)
    grad_z = keep_rows(grad_z, z_moved)
    y_moved, z_moved = send_rows(grad_a, cross_near), send_rows(grad_z, cross_far)
    sums = sums + sums_moved
    sums_moved = cross_x(sums)
    feed_e, feed_r = keep_columns(feed_e, stacked(fe_moved, fe_moved_two)), keep_rows(feed_r, fr_moved)
    fe_moved, fr_moved = send_rows(feed_e, cross_near), send_rows(feed_r, cross_far)
    mine_t = beside(part_e, part_r, keep_rows(part_a, at_moved)).astype(BF16)
    theirs_t = cross_y(
        beside(
            mine_t[:, :half], mine_t[:, 2 * half : 3 * half], mine_t[:, half : 2 * half], mine_t[:, 3 * half :]
        )
    )
    grad_moved = swapped(input_grad.astype(BF16)).astype(F32)
    y_moved, z_moved, sums_moved, fe_moved, fr_moved = pin(
        y_moved, z_moved, sums_moved, fe_moved, fr_moved
    )
    grad_a = keep_rows(grad_a, y_moved)
    grad_z = keep_rows(grad_z, z_moved).astype(BF16)
    y_moved, z_moved = send_rows(grad_a, cross_far), cross_y(grad_z)
    feed_e, feed_r = keep_rows(feed_e, fe_moved), keep_rows(feed_r, fr_moved)
    fe_moved = send_rows(feed_e, cross_far)
    pack = pack_grads(
        sums + sums_moved,
        (qkv_sum_s, qkv_sum_t),
        (hidden_sum_s, hidden_sum_t),
        place,
        local,
        params[3].shape,
        params[9].shape,
    )
    pack_moved = cross_y(pack)
    y_moved, fe_moved = pin(y_moved, fe_moved)
    mine_a = keep_rows(grad_a, y_moved).astype(BF16)
    theirs_a = cross_y(mine_a)
    mine_s = beside(keep_rows(feed_e, fe_moved), feed_r).astype(BF16)
    theirs_s = cross_y(
        beside(mine_s[:, :half], mine_s[:, 2 * half :], mine_s[:, half : 2 * half])
    )
    z_moved, pack_moved, theirs_t = pin(z_moved, pack_moved, theirs_t)
    pack = pack + pack_moved
    pack_near = cross_near(pack[2 * ROWS :])
    expand_grad_t, reduce_grad_t = finish_feed(
        mine_t[:, : 3 * half], theirs_t[:, : 3 * half], place, half
    )
    pack_near, theirs_a, expand_grad_t, reduce_grad_t = pin(
        pack_near, theirs_a, expand_grad_t, reduce_grad_t
    )
    pack = pack[: 2 * ROWS] + pack_near
    pack_far = cross_far(pack[ROWS:])
    merged_grad_s, output_grad_s = finish_attend(
        (grad_z, z_moved), mine_a, theirs_a, place
    )
    merged_grad_t, output_grad_t = finish_attend(
        (), mine_t[:, 3 * half :], theirs_t[:, 3 * half :], place
    )
    expand_grad_s, reduce_grad_s = finish_feed(mine_s, theirs_s, place, half)
    vectors = unpack_grads(pack, pack_far, local, params[3].shape, params[9].shape)
    middle_t, final_across, grad_between = pin(middle_t, final_across, grad_between)
    rows = 2 * tokens
    final = middle_t[:rows] + gains_t[5:6] + final_kept[:rows] + final_across.astype(F32)
    final = final + final_arrived[:rows].astype(F32)
    final = times_across(final.astype(BF16), chooser, BF16)
    outputs = [restore(final, swapped(final)), restore(input_grad, grad_moved)]
    for vector, merged, output, expand, reduce in (
        (vectors[:8], merged_grad_s, output_grad_s, expand_grad_s, reduce_grad_s),
        (vectors[8:], merged_grad_t, output_grad_t, expand_grad_t, reduce_grad_t),
    ):
        outputs += [
            vector[0],
            vector[1],
            merged,
            vector[6],
            output,
            vector[2],
            vector[3],
            vector[4],
            expand,
            vector[7],
            reduce,
            vector[5],
        ]
    return tuple(outputs)


def solution(mesh):
    quick = (mesh.shape["dp"], mesh.shape["ctx"], mesh.shape["tp"]) == (4, 2, 4)
    placed = (
        P("dp", ("ctx", "tp"), None),
        P("dp", "ctx"),
        P("dp", ("ctx", "tp"), None),
        P("dp"),
        P("dp"),
        P("dp", None, "tp"),
        P(None, "tp", "dp"),
        P("tp", "dp"),
        P("dp"),
        P("dp"),
        P("dp"),
        P("dp", "tp"),
        P("tp", "dp"),
        P("tp", "dp"),
        P("dp"),
        P("dp"),
        P("dp"),
        P("dp", None, "tp"),
        P(None, "tp", "dp"),
        P("tp", "dp"),
        P("dp"),
        P("dp"),
        P("dp"),
        P("dp", "tp"),
        P("tp", "dp"),
        P("tp", "dp"),
        P("dp"),
    )
    return jax.shard_map(
        fast_shards if quick else general_shards,
        mesh=mesh,
        in_specs=placed,
        out_specs=(
            P("dp", ("ctx", "tp"), None),
            P("dp", ("ctx", "tp"), None),
            P("dp"),
            P("dp"),
            P("dp", None, "tp"),
            P(None, "tp", "dp"),
            P("tp", "dp"),
            P("dp"),
            P("dp"),
            P("dp"),
            P("dp", "tp"),
            P("tp", "dp"),
            P("tp", "dp"),
            P("dp"),
            P("dp"),
            P("dp"),
            P("dp", None, "tp"),
            P(None, "tp", "dp"),
            P("tp", "dp"),
            P("dp"),
            P("dp"),
            P("dp"),
            P("dp", "tp"),
            P("tp", "dp"),
            P("tp", "dp"),
            P("dp"),
        ),
        check_vma=False,
    )
```

profile of v0, /device:TPU:0, one launch (start us, length us, event | category | flops | bytes accessed | tf_op | source)
XLA Modules:
  0.0 353.7 jit_solution(16881320836685946489)
XLA Ops:
  0.7 2.4 prepare_first.1.refs_0_.refs_6_
  3.1 3.1 collective-permute-start.2
  6.2 2.6 collective-permute-start.3
  10.6 1.6 collective-permute-start
  13.5 5.5 %collective-permute-done = bf16[144,768]{1,0:T(8,128)(2,1)S(1)} collective-permute-done((bf16[144,768]{1,0:T(8,128)(2,1)S(1)}, bf16[144,768]{1,0:T(8,128)(2,1)S(1)}, u32[]{:S(2)}, u32[]{:S(2)}) %collective-permute-start) | collective-permute-done | bytes 221216 | tf_op jit(solution)/shard_map/ppermute | solution.py:547
  19.9 1.6 collective-permute-start.1
  22.4 1.9 collective-permute-done.3.refs_1_.refs_7_
  24.7 2.7 collective-permute-start.4
  27.8 9.4 %collective-permute-done.5 = bf16[192,768]{1,0:T(8,128)(2,1)S(1)} collective-permute-done((bf16[192,768]{1,0:T(8,128)(2,1)S(1)}, bf16[192,768]{1,0:T(8,128)(2,1)S(1)}, u32[]{:S(2)}, u32[]{:S(2)}) %collective-permute-start.5) | collective-permute-done | bytes 294944 | tf_op jit(solution)/shard_map/ppermute | solution.py:547
  38.7 1.9 collective-permute-start.8
  41.4 1.5 collective-permute-start.10
  42.9 1.6 collective-permute-start.9
  45.3 7.7 %attention_forward.2 = (bf16[512,768]{1,0:T(8,128)(2,1)S(1)}, f32[512,768]{1,0:T(8,128)S(1)}, bf16[9,1024,64]{2,1,0:T(8,128)(2,1)S(1)}, bf16[1024,192]{1,0:T(8,1...) custom-call(s32[1]{0:T(128)} %bitcast.11.refs_0_, ...), custom_call_target="tpu_custom_call" | custom-call | flops 1610612736 | bytes 8497412 | tf_op jit(solution)/shard_map/attention_forward/pallas_call | solution.py:840
  53.2 2.3 collective-permute-done.11
  56.8 1.6 collective-permute-start.13
  58.4 1.6 collective-permute-start.14
  61.6 13.8 %collective-permute-done.12.across_ref = bf16[512,768]{1,0:T(8,128)(2,1)S(1)} collective-permute-done((bf16[512,768]{1,0:T(8,128)(2,1)S(1)}, bf16[512,768]{1,0:T(8,128)(2,1)S(1)}, u32[]{:S(2)}, u32[]{:S(2)}) %collective-permute-start.12) | collective-permute-done | bytes 786464 | tf_op jit(solution)/shard_map/ppermute | solution.py:547
  76.4 2.3 collective-permute-done.15
  79.6 2.3 collective-permute-done.16.refs_1_
  81.9 4.0 %feed_forward.2 = (bf16[512,768]{1,0:T(8,128)(2,1)S(1)}, f32[512,768]{1,0:T(8,128)S(1)}) custom-call(bf16[512,768]{1,0:T(8,128)(2,1)S(1)} %get-tuple-element.211.refs_0_, bf16[512,768]{1,0:T(8,128)(2,1)S(1)} %collective-permute-done.16.refs_1_, f32[1,768]{1,0:T(1,128)S(1)} %get-tuple-element.212.refs_2_.refs_4_, ...), custom_call_target="tpu_custom_call" | custom-call | flops 2415919104 | bytes 6294528 | tf_op jit(solution)/shard_map/feed_forward/pallas_call | solution.py:840
  86.1 2.1 collective-permute-done.17
  92.5 1.6 collective-permute-start.21
  94.1 14.0 %collective-permute-done.18.across_ref = bf16[512,768]{1,0:T(8,128)(2,1)S(1)} collective-permute-done((bf16[512,768]{1,0:T(8,128)(2,1)S(1)}, bf16[512,768]{1,0:T(8,128)(2,1)S(1)}, u32[]{:S(2)}, u32[]{:S(2)}) %collective-permute-start.18) | collective-permute-done | bytes 786464 | tf_op jit(solution)/shard_map/ppermute | solution.py:547
  111.2 2.5 collective-permute-start.23
  113.9 7.3 %attention_forward.3 = (bf16[512,768]{1,0:T(8,128)(2,1)S(1)}, f32[512,768]{1,0:T(8,128)S(1)}, bf16[9,1024,64]{2,1,0:T(8,128)(2,1)S(1)}, bf16[1024,192]{1,0:T(8,128)(2,1)S(1)}, f32[3,1,1024]{2,1,0:T(1,128)S(1)}) custom-call(s32[1]{0:T(128)} %bitcast.11.refs_0_, bf16[512,768]{1,0:T(8,128)(2,1)S(1)} %get-tuple-element.221.refs_1_, ...), custom_call_target="tpu_custom_call" | custom-call | flops 1610612736 | bytes 6703364 | tf_op jit(solution)/shard_map/attention_forward/pallas_call | solution.py:840
  121.3 2.5 collective-permute-done.24
  125.1 1.7 collective-permute-done.25
  128.7 1.8 collective-permute-start.28
  130.5 16.0 %collective-permute-done.26.across_ref = bf16[512,768]{1,0:T(8,128)(2,1)S(1)} collective-permute-done((bf16[512,768]{1,0:T(8,128)(2,1)S(1)}, bf16[512,768]{1,0:T(8,128)(2,1)S(1)}, u32[]{:S(2)}, u32[]{:S(2)}) %collective-permute-start.26) | collective-permute-done | bytes 786464 | tf_op jit(solution)/shard_map/ppermute | solution.py:547
  147.7 2.3 collective-permute-done.30.refs_1_
  150.0 5.4 %feed_backward.2 = (bf16[512,768]{1,0:T(8,128)(2,1)S(1)}, f32[512,768]{1,0:T(8,128)S(1)}, bf16[1024,768]{1,0:T(8,128)(2,1)S(1)}, bf16[1024,768]{1,0:T(8,128)(2,1)S(1)}, f32[1,768]{1,0:T(1,128)S(1)}) custom-call(bf16[512,768]{1,0:T(8,128)(2,1)S(1)} %get-tuple-element.235.refs_0_, bf16[512,768]{1,0:T(8,128)(2,1)S(1)} %collective-permute-done.30.refs_1_, ...), custom_call_target="tpu_custom_call" | custom-call | flops 3623878656 | bytes 11016192 | tf_op jit(solution)/shard_map/feed_backward/pallas_call | solution.py:840
  155.6 2.1 collective-permute-done.31
  159.0 3.9 %feed_forward.3 = (bf16[512,768]{1,0:T(8,128)(2,1)S(1)}, f32[512,768]{1,0:T(8,128)S(1)}) custom-call(bf16[512,768]{1,0:T(8,128)(2,1)S(1)} %get-tuple-element.235.refs_0_, bf16[512,768]{1,0:T(8,128)(2,1)S(1)} %collective-permute-done.30.refs_1_, f32[1,768]{1,0:T(1,128)S(1)} %get-tuple-element.237.refs_4_.refs_2_, ...), custom_call_target="tpu_custom_call" | custom-call | flops 2415919104 | bytes 6294528 | tf_op jit(solution)/shard_map/feed_forward/pallas_call | solution.py:840
  165.9 11.7 %collective-permute-done.32.across_ref = bf16[512,768]{1,0:T(8,128)(2,1)S(1)} collective-permute-done((bf16[512,768]{1,0:T(8,128)(2,1)S(1)}, bf16[512,768]{1,0:T(8,128)(2,1)S(1)}, u32[]{:S(2)}, u32[]{:S(2)}) %collective-permute-start.32) | collective-permute-done | bytes 786464 | tf_op jit(solution)/shard_map/ppermute | solution.py:547
  177.6 1.5 norm_back_near.3
  179.7 1.8 collective-permute-done.34
  182.6 10.0 %attention_backward.2 = (bf16[512,768]{1,0:T(8,128)(2,1)S(1)}, f32[512,768]{1,0:T(8,128)S(1)}, bf16[1024,576]{1,0:T(8,128)(2,1)S(1)}, f32[1,576]{1,0:T(1,128)S(1)}) custom-call(s32[1]{0:T(128)} %bitcast.11.refs_0_, bf16[512,768]{1,0:T(8,128)(2,1)S(1)} %get-tuple-element.247.refs_1_, bf16[512,768]{1,0:T(8,128)(2,1)S(1)} %collective-permute-done.33.refs_2_, ...), custom_call_target="tpu_custom_call" | custom-call | flops 4026531840 | bytes 7489796 | tf_op jit(solution)/shard_map/attention_backward/pallas_call | solution.py:840
  192.9 1.8 collective-permute-start.39
  199.1 15.8 %collective-permute-done.37.across_ref = bf16[512,768]{1,0:T(8,128)(2,1)S(1)} collective-permute-done((bf16[512,768]{1,0:T(8,128)(2,1)S(1)}, bf16[512,768]{1,0:T(8,128)(2,1)S(1)}, u32[]{:S(2)}, u32[]{:S(2)}) %collective-permute-start.37) | collective-permute-done | bytes 786464 | tf_op jit(solution)/shard_map/ppermute | solution.py:547
  218.8 5.3 %feed_backward.3 = (bf16[512,768]{1,0:T(8,128)(2,1)S(1)}, f32[512,768]{1,0:T(8,128)S(1)}, bf16[1024,768]{1,0:T(8,128)(2,1)S(1)}, bf16[1024,768]{1,0:T(8,128)(2,1)S(1)}, f32[1,768]{1,0:T(1,128)S(1)}) custom-call(bf16[512,768]{1,0:T(8,128)(2,1)S(1)} %get-tuple-element.211.refs_0_, bf16[512,768]{1,0:T(8,128)(2,1)S(1)} %collective-permute-done.16.refs_1_, ...), custom_call_target="tpu_custom_call" | custom-call | flops 3623878656 | bytes 11016192 | tf_op jit(solution)/shard_map/feed_backward/pallas_call | solution.py:840
  224.4 1.6 collective-permute-start.38
  227.1 2.3 collective-permute-start.45
  235.3 13.7 %collective-permute-done.43.across_ref = bf16[512,768]{1,0:T(8,128)(2,1)S(1)} collective-permute-done((bf16[512,768]{1,0:T(8,128)(2,1)S(1)}, bf16[512,768]{1,0:T(8,128)(2,1)S(1)}, u32[]{:S(2)}, u32[]{:S(2)}) %collective-permute-start.43) | collective-permute-done | bytes 786464 | tf_op jit(solution)/shard_map/ppermute | solution.py:547
  250.7 1.8 collective-permute-start.50
  253.2 1.6 collective-permute-start.52
  255.4 9.8 %attention_backward.3 = (bf16[512,768]{1,0:T(8,128)(2,1)S(1)}, f32[512,768]{1,0:T(8,128)S(1)}, bf16[1024,576]{1,0:T(8,128)(2,1)S(1)}, f32[1,576]{1,0:T(1,128)S(1)}) custom-call(s32[1]{0:T(128)} %bitcast.11.refs_0_, bf16[512,768]{1,0:T(8,128)(2,1)S(1)} %get-tuple-element.276.refs_1_, bf16[512,768]{1,0:T(8,128)(2,1)S(1)} %collective-permute-done.47.refs_2_, ...), custom_call_target="tpu_custom_call" | custom-call | flops 4026531840 | bytes 7686404 | tf_op jit(solution)/shard_map/attention_backward/pallas_call | solution.py:840
  267.6 1.6 collective-permute-start.48
  272.7 9.5 %collective-permute-done.54.refs_6_ = bf16[256,768]{1,0:T(8,128)(2,1)S(1)} collective-permute-done((bf16[256,768]{1,0:T(8,128)(2,1)S(1)}, bf16[256,768]{1,0:T(8,128)(2,1)S(1)}, u32[]{:S(2)}, u32[]{:S(2)}) %collective-permute-start.54) | collective-permute-done | bytes 393248 | tf_op jit(solution)/shard_map/ppermute | solution.py:547
  282.2 1.6 collective-permute-start.58
  286.7 7.7 %collective-permute-done.58 = bf16[192,384]{1,0:T(8,128)(2,1)S(1)} collective-permute-done((bf16[192,384]{1,0:T(8,128)(2,1)S(1)}, bf16[192,384]{1,0:T(8,128)(2,1)S(1)}, u32[]{:S(2)}, u32[]{:S(2)}) %collective-permute-start.58) | collective-permute-done | bytes 147488 | tf_op jit(solution)/shard_map/ppermute | solution.py:547
  294.4 1.8 collective-permute-done.57
  296.4 1.7 collective-permute-start.60
  305.8 4.5 %collective-permute-done.61 = bf16[192,512]{1,0:T(8,128)(2,1)S(1)} collective-permute-done((bf16[192,512]{1,0:T(8,128)(2,1)S(1)}, bf16[192,512]{1,0:T(8,128)(2,1)S(1)}, u32[]{:S(2)}, u32[]{:S(2)}) %collective-permute-start.61) | collective-permute-done | bytes 196640 | tf_op jit(solution)/shard_map/ppermute | solution.py:547
  310.3 5.0 %collective-permute-done.63 = bf16[384,384]{1,0:T(8,128)(2,1)S(1)} collective-permute-done((bf16[384,384]{1,0:T(8,128)(2,1)S(1)}, bf16[384,384]{1,0:T(8,128)(2,1)S(1)}, u32[]{:S(2)}, u32[]{:S(2)}) %collective-permute-start.63) | collective-permute-done | bytes 294944 | tf_op jit(solution)/shard_map/ppermute | solution.py:547
  315.3 6.6 %collective-permute-done.64 = bf16[192,768]{1,0:T(8,128)(2,1)S(1)} collective-permute-done((bf16[192,768]{1,0:T(8,128)(2,1)S(1)}, bf16[192,768]{1,0:T(8,128)(2,1)S(1)}, u32[]{:S(2)}, u32[]{:S(2)}) %collective-permute-start.64) | collective-permute-done | bytes 294944 | tf_op jit(solution)/shard_map/ppermute | solution.py:547
  323.6 3.0 collective-permute-start.70
  327.5 4.2 %collective-permute-done.69 = bf16[192,128]{1,0:T(8,128)(2,1)S(1)} collective-permute-done((bf16[192,128]{1,0:T(8,128)(2,1)S(1)}, bf16[192,128]{1,0:T(8,128)(2,1)S(1)}, u32[]{:S(2)}, u32[]{:S(2)}) %collective-permute-start.69) | collective-permute-done | bytes 49184 | tf_op jit(solution)/shard_map/ppermute | solution.py:547
  332.2 1.6 collective-permute-done.70
  336.1 4.5 %collective-permute-done.66 = f32[256,256]{1,0:T(8,128)S(1)} collective-permute-done((f32[256,256]{1,0:T(8,128)S(1)}, f32[256,256]{1,0:T(8,128)S(1)}, u32[]{:S(2)}, u32[]{:S(2)}) %collective-permute-start.66) | collective-permute-done | bytes 262176 | tf_op jit(solution)/shard_map/ppermute | solution.py:547
  340.8 1.6 finish_feed.2
  342.4 3.2 collective-permute-done.68
  347.7 1.6 finish_attend.3
  349.3 1.7 finish_attend.2
  351.8 1.6 finish_feed.3
  (237 shorter events, 75.8 us)
Async XLA Ops:
  3.1 24.7 %collective-permute-start.2 = (bf16[224,768]{1,0:T(8,128)(2,1)}, bf16[224,768]{1,0:T(8,128)(2,1)S(1)}, u32[]{:S(2)}, u32[]{:S(2)}) collective-permute-start(bf16[224,768]{1,0:T(8,128)(2,1)} %prepare_first.1.refs_0_.refs_6_), channel_id=1, source_target_pairs={{0,8},{8,0},{16,24},{24,16},{1,9},{9,1},{17,25},{25,17},{2,10},{10... | collective-permute-start | bytes 1032200 | tf_op jit(solution)/shard_map/ppermute | solution.py:547
  6.2 18.1 %collective-permute-start.3 = (bf16[224,768]{1,0:T(8,128)(2,1)}, bf16[224,768]{1,0:T(8,128)(2,1)S(1)}, u32[]{:S(2)}, u32[]{:S(2)}) collective-permute-start(bf16[224,768]{1,0:T(8,128)(2,1)} %prepare_first.1.refs_0_.refs_6_), channel_id=1, source_target_pairs={{0,16},{8,24},{16,0},{24,8},{1,17},{9,25},{17,1},{25,9},{2,18},{10... | collective-permute-start | bytes 1032200 | tf_op jit(solution)/shard_map/ppermute | solution.py:547
  10.6 8.4 %collective-permute-start = (bf16[144,768]{1,0:T(8,128)(2,1)S(1)}, bf16[144,768]{1,0:T(8,128)(2,1)S(1)}, u32[]{:S(2)}, u32[]{:S(2)}) collective-permute-start(bf16[144,768]{1,0:T(8,128)(2,1)S(1)} %fusion.86), channel_id=1, source_target_pairs={{0,4},{4,0},{1,5},{5,1},{2,6},{6,2},{3,7},{7,3},{8,12},{12,8},{9,1... | collective-permute-start | bytes 663560 | tf_op jit(solution)/shard_map/ppermute | solution.py:547
  12.2 15.6 %collective-permute-start.6 = (bf16[128,768]{1,0:T(8,128)(2,1)S(1)}, bf16[128,768]{1,0:T(8,128)(2,1)S(1)}, u32[]{:S(2)}, u32[]{:S(2)}) collective-permute-start(bf16[128,768]{1,0:T(8,128)(2,1)S(1)} %get-tuple-element.365), channel_id=1, source_target_pairs={{0,4},{4,0},{1,5},{5,1},{2,6},{6,2},{3,7},{7,3},{8,12},{12,8},{9,1... | collective-permute-start | bytes 589832 | tf_op jit(solution)/shard_map/ppermute | solution.py:547
  19.9 7.8 %collective-permute-start.1 = (bf16[256,768]{1,0:T(8,128)(2,1)S(1)}, bf16[256,768]{1,0:T(8,128)(2,1)S(1)}, u32[]{:S(2)}, u32[]{:S(2)}) collective-permute-start(bf16[256,768]{1,0:T(8,128)(2,1)S(1)} %convolution_convert_fusion.2), channel_id=1, source_target_pairs={{0,2},{1,3},{2,0},{3,1},{4,6},{5,7},{6,4},{7,5},{8,10},{9,11},{10,... | collective-permute-start | bytes 1179656 | tf_op jit(solution)/shard_map/ppermute | solution.py:547
  24.3 12.9 %collective-permute-start.5 = (bf16[192,768]{1,0:T(8,128)(2,1)S(1)}, bf16[192,768]{1,0:T(8,128)(2,1)S(1)}, u32[]{:S(2)}, u32[]{:S(2)}) collective-permute-start(bf16[192,768]{1,0:T(8,128)(2,1)S(1)} %get-tuple-element.359), channel_id=1, source_target_pairs={{0,16},{8,24},{16,0},{24,8},{1,17},{9,25},{17,1},{25,9},{2,18},{10... | collective-permute-start | bytes 884744 | tf_op jit(solution)/shard_map/ppermute | solution.py:547
  24.7 13.5 %collective-permute-start.4 = (bf16[224,768]{1,0:T(8,128)(2,1)S(1)}, bf16[224,768]{1,0:T(8,128)(2,1)S(1)}, u32[]{:S(2)}, u32[]{:S(2)}) collective-permute-start(bf16[224,768]{1,0:T(8,128)(2,1)S(1)} %collective-permute-done.3.refs_1_.refs_7_), channel_id=1, source_target_pairs={{0,8},{8,0},{16,24},{24,16},{1,9},{9,1},{17,25},{25,17},{2,10},{10... | collective-permute-start | bytes 1032200 | tf_op jit(solution)/shard_map/ppermute | solution.py:547
  38.6 6.8 %collective-permute-start.7 = (bf16[512,768]{1,0:T(8,128)(2,1)S(1)}, bf16[512,768]{1,0:T(8,128)(2,1)S(1)}, u32[]{:S(2)}, u32[]{:S(2)}) collective-permute-start(bf16[512,768]{1,0:T(8,128)(2,1)S(1)} %norm_only.1.refs_1_), channel_id=1, source_target_pairs={{0,1},{1,0},{2,3},{3,2},{4,5},{5,4},{6,7},{7,6},{8,9},{9,8},{10,11... | collective-permute-start | bytes 2359304 | tf_op jit(solution)/shard_map/ppermute | solution.py:547
  38.7 14.3 %collective-permute-start.8 = (bf16[384,384]{1,0:T(8,128)(2,1)S(1)}, bf16[384,384]{1,0:T(8,128)(2,1)S(1)}, u32[]{:S(2)}, u32[]{:S(2)}) collective-permute-start(bf16[384,384]{1,0:T(8,128)(2,1)S(1)} %pad_maximum_fusion.10), channel_id=1, source_target_pairs={{0,8},{8,0},{16,24},{24,16},{1,9},{9,1},{17,25},{25,17},{2,10},{10... | collective-permute-start | bytes 884744 | tf_op jit(solution)/shard_map/ppermute | solution.py:547
  41.4 11.7 %collective-permute-start.10 = (bf16[256,768]{1,0:T(8,128)(2,1)S(1)}, bf16[256,768]{1,0:T(8,128)(2,1)S(1)}, u32[]{:S(2)}, u32[]{:S(2)}) collective-permute-start(bf16[256,768]{1,0:T(8,128)(2,1)S(1)} %convolution_convert_fusion.1), channel_id=1, source_target_pairs={{0,2},{1,3},{2,0},{3,1},{4,6},{5,7},{6,4},{7,5},{8,10},{9,11},{10,... | collective-permute-start | bytes 1179656 | tf_op jit(solution)/shard_map/ppermute | solution.py:547
  42.9 10.1 %collective-permute-start.9 = (bf16[192,384]{1,0:T(8,128)(2,1)S(1)}, bf16[192,384]{1,0:T(8,128)(2,1)S(1)}, u32[]{:S(2)}, u32[]{:S(2)}) collective-permute-start(bf16[192,384]{1,0:T(8,128)(2,1)S(1)} %get-tuple-element.360), channel_id=1, source_target_pairs={{0,16},{8,24},{16,0},{24,8},{1,17},{9,25},{17,1},{25,9},{2,18},{10... | collective-permute-start | bytes 442376 | tf_op jit(solution)/shard_map/ppermute | solution.py:547
  55.7 19.6 %collective-permute-start.12 = (bf16[512,768]{1,0:T(8,128)(2,1)S(1)}, bf16[512,768]{1,0:T(8,128)(2,1)S(1)}, u32[]{:S(2)}, u32[]{:S(2)}) collective-permute-start(bf16[512,768]{1,0:T(8,128)(2,1)S(1)} %add_convert_fusion.5.partial_ref), channel_id=1, source_target_pairs={{0,2},{1,3},{2,0},{3,1},{4,6},{5,7},{6,4},{7,5},{8,10},{9,11},{10,... | collective-permute-start | bytes 2359304 | tf_op jit(solution)/shard_map/ppermute | solution.py:547
  56.8 21.9 %collective-permute-start.13 = (bf16[768,384]{1,0:T(8,128)(2,1)S(1)}, bf16[768,384]{1,0:T(8,128)(2,1)S(1)}, u32[]{:S(2)}, u32[]{:S(2)}) collective-permute-start(bf16[768,384]{1,0:T(8,128)(2,1)S(1)} %pad_maximum_fusion.4.refs_3_.refs_5_), channel_id=1, source_target_pairs={{0,4},{4,0},{1,5},{5,1},{2,6},{6,2},{3,7},{7,3},{8,12},{12,8},{9,1... | collective-permute-start | bytes 1769480 | tf_op jit(solution)/shard_map/ppermute | solution.py:547
  58.4 21.2 %collective-permute-start.14 = (bf16[384,768]{1,0:T(8,128)(2,1)S(1)}, bf16[384,768]{1,0:T(8,128)(2,1)S(1)}, u32[]{:S(2)}, u32[]{:S(2)}) collective-permute-start(bf16[384,768]{1,0:T(8,128)(2,1)S(1)} %maximum_maximum_fusion.refs_5_.refs_7_), channel_id=1, source_target_pairs={{0,8},{8,0},{16,24},{24,16},{1,9},{9,1},{17,25},{25,17},{2,10},{10... | collective-permute-start | bytes 1769480 | tf_op jit(solution)/shard_map/ppermute | solution.py:547
  60.0 18.6 %collective-permute-start.15 = (bf16[192,768]{1,0:T(8,128)(2,1)S(1)}, bf16[192,768]{1,0:T(8,128)(2,1)S(1)}, u32[]{:S(2)}, u32[]{:S(2)}) collective-permute-start(bf16[192,768]{1,0:T(8,128)(2,1)S(1)} %prepare_attend.1), channel_id=1, source_target_pairs={{0,16},{8,24},{16,0},{24,8},{1,17},{9,25},{17,1},{25,9},{2,18},{10... | collective-permute-start | bytes 884744 | tf_op jit(solution)/shard_map/ppermute | solution.py:547
  88.5 19.6 %collective-permute-start.18 = (bf16[512,768]{1,0:T(8,128)(2,1)S(1)}, bf16[512,768]{1,0:T(8,128)(2,1)S(1)}, u32[]{:S(2)}, u32[]{:S(2)}) collective-permute-start(bf16[512,768]{1,0:T(8,128)(2,1)S(1)} %add_convert_fusion.4.partial_ref), channel_id=1, source_target_pairs={{0,2},{1,3},{2,0},{3,1},{4,6},{5,7},{6,4},{7,5},{8,10},{9,11},{10,... | collective-permute-start | bytes 2359304 | tf_op jit(solution)/shard_map/ppermute | solution.py:547
  89.6 21.5 %collective-permute-start.19 = (bf16[384,768]{1,0:T(8,128)(2,1)S(1)}, bf16[384,768]{1,0:T(8,128)(2,1)S(1)}, u32[]{:S(2)}, u32[]{:S(2)}) collective-permute-start(bf16[384,768]{1,0:T(8,128)(2,1)S(1)} %constant_dynamic-update-slice_fusion.refs_5_.refs_6_), channel_id=1, source_target_pairs={{0,8},{8,0},{16,24},{24,16},{1,9},{9,1},{17,25},{25,17},{2,10},{10... | collective-permute-start | bytes 1769480 | tf_op jit(solution)/shard_map/ppermute | solution.py:547
  91.1 18.1 %collective-permute-start.20 = (bf16[192,384]{1,0:T(8,128)(2,1)S(1)}, bf16[192,384]{1,0:T(8,128)(2,1)S(1)}, u32[]{:S(2)}, u32[]{:S(2)}) collective-permute-start(bf16[192,384]{1,0:T(8,128)(2,1)S(1)} %get-tuple-element.357), channel_id=1, source_target_pairs={{0,16},{8,24},{16,0},{24,8},{1,17},{9,25},{17,1},{25,9},{2,18},{10... | collective-permute-start | bytes 442376 | tf_op jit(solution)/shard_map/ppermute | solution.py:547
  92.5 17.5 %collective-permute-start.21 = (bf16[192,384]{1,0:T(8,128)(2,1)S(1)}, bf16[192,384]{1,0:T(8,128)(2,1)S(1)}, u32[]{:S(2)}, u32[]{:S(2)}) collective-permute-start(bf16[192,384]{1,0:T(8,128)(2,1)S(1)} %get-tuple-element.356), channel_id=1, source_target_pairs={{0,16},{8,24},{16,0},{24,8},{1,17},{9,25},{17,1},{25,9},{2,18},{10... | collective-permute-start | bytes 442376 | tf_op jit(solution)/shard_map/ppermute | solution.py:547
  111.2 13.3 %collective-permute-start.23 = (bf16[384,384]{1,0:T(8,128)(2,1)S(1)}, bf16[384,384]{1,0:T(8,128)(2,1)S(1)}, u32[]{:S(2)}, u32[]{:S(2)}) collective-permute-start(bf16[384,384]{1,0:T(8,128)(2,1)S(1)} %pad_maximum_fusion.11), channel_id=1, source_target_pairs={{0,8},{8,0},{16,24},{24,16},{1,9},{9,1},{17,25},{25,17},{2,10},{10... | collective-permute-start | bytes 884744 | tf_op jit(solution)/shard_map/ppermute | solution.py:547
  113.6 10.1 %collective-permute-start.24 = (bf16[192,384]{1,0:T(8,128)(2,1)S(1)}, bf16[192,384]{1,0:T(8,128)(2,1)S(1)}, u32[]{:S(2)}, u32[]{:S(2)}) collective-permute-start(bf16[192,384]{1,0:T(8,128)(2,1)S(1)} %get-tuple-element.354), channel_id=1, source_target_pairs={{0,16},{8,24},{16,0},{24,8},{1,17},{9,25},{17,1},{25,9},{2,18},{10... | collective-permute-start | bytes 442376 | tf_op jit(solution)/shard_map/ppermute | solution.py:547
  124.5 23.1 %collective-permute-start.29 = (bf16[512,768]{1,0:T(8,128)(2,1)S(1)}, bf16[512,768]{1,0:T(8,128)(2,1)S(1)}, u32[]{:S(2)}, u32[]{:S(2)}) collective-permute-start(bf16[512,768]{1,0:T(8,128)(2,1)S(1)} %pad_maximum_fusion.2.refs_2_.skip_ref), channel_id=1, source_target_pairs={{0,1},{1,0},{2,3},{3,2},{4,5},{5,4},{6,7},{7,6},{8,9},{9,8},{10,11... | collective-permute-start | bytes 2359304 | tf_op jit(solution)/shard_map/ppermute | solution.py:547
  126.9 19.6 %collective-permute-start.26 = (bf16[512,768]{1,0:T(8,128)(2,1)S(1)}, bf16[512,768]{1,0:T(8,128)(2,1)S(1)}, u32[]{:S(2)}, u32[]{:S(2)}) collective-permute-start(bf16[512,768]{1,0:T(8,128)(2,1)S(1)} %add_convert_fusion.3.partial_ref), channel_id=1, source_target_pairs={{0,2},{1,3},{2,0},{3,1},{4,6},{5,7},{6,4},{7,5},{8,10},{9,11},{10,... | collective-permute-start | bytes 2359304 | tf_op jit(solution)/shard_map/ppermute | solution.py:547
  128.1 19.6 %collective-permute-start.27 = (bf16[768,384]{1,0:T(8,128)(2,1)S(1)}, bf16[768,384]{1,0:T(8,128)(2,1)S(1)}, u32[]{:S(2)}, u32[]{:S(2)}) collective-permute-start(bf16[768,384]{1,0:T(8,128)(2,1)S(1)} %pad_maximum_fusion.5.refs_5_.refs_3_), channel_id=1, source_target_pairs={{0,4},{4,0},{1,5},{5,1},{2,6},{6,2},{3,7},{7,3},{8,12},{12,8},{9,1... | collective-permute-start | bytes 1769480 | tf_op jit(solution)/shard_map/ppermute | solution.py:547
  128.7 18.9 %collective-permute-start.28 = (bf16[384,768]{1,0:T(8,128)(2,1)S(1)}, bf16[384,768]{1,0:T(8,128)(2,1)S(1)}, u32[]{:S(2)}, u32[]{:S(2)}) collective-permute-start(bf16[384,768]{1,0:T(8,128)(2,1)S(1)} %maximum_maximum_fusion.1.refs_7_.refs_5_), channel_id=1, source_target_pairs={{0,8},{8,0},{16,24},{24,16},{1,9},{9,1},{17,25},{25,17},{2,10},{10... | collective-permute-start | bytes 1769480 | tf_op jit(solution)/shard_map/ppermute | solution.py:547
  157.9 19.6 %collective-permute-start.32 = (bf16[512,768]{1,0:T(8,128)(2,1)S(1)}, bf16[512,768]{1,0:T(8,128)(2,1)S(1)}, u32[]{:S(2)}, u32[]{:S(2)}) collective-permute-start(bf16[512,768]{1,0:T(8,128)(2,1)S(1)} %add_convert_fusion.2.partial_ref), channel_id=1, source_target_pairs={{0,2},{1,3},{2,0},{3,1},{4,6},{5,7},{6,4},{7,5},{8,10},{9,11},{10,... | collective-permute-start | bytes 2359304 | tf_op jit(solution)/shard_map/ppermute | solution.py:547
  179.2 3.4 collective-permute-start.33
  181.6 11.2 %collective-permute-start.35 = (bf16[256,768]{1,0:T(8,128)(2,1)S(1)}, bf16[256,768]{1,0:T(8,128)(2,1)S(1)}, u32[]{:S(2)}, u32[]{:S(2)}) collective-permute-start(bf16[256,768]{1,0:T(8,128)(2,1)S(1)} %add_convert_fusion.8), channel_id=1, source_target_pairs={{0,2},{1,3},{2,0},{3,1},{4,6},{5,7},{6,4},{7,5},{8,10},{9,11},{10,... | collective-permute-start | bytes 1179656 | tf_op jit(solution)/shard_map/ppermute | solution.py:547
  192.9 23.6 %collective-permute-start.39 = (bf16[384,768]{1,0:T(8,128)(2,1)S(1)}, bf16[384,768]{1,0:T(8,128)(2,1)S(1)}, u32[]{:S(2)}, u32[]{:S(2)}) collective-permute-start(bf16[384,768]{1,0:T(8,128)(2,1)S(1)} %slice.316), channel_id=1, source_target_pairs={{0,8},{8,0},{16,24},{24,16},{1,9},{9,1},{17,25},{25,17},{2,10},{10... | collective-permute-start | bytes 1769480 | tf_op jit(solution)/shard_map/ppermute | solution.py:547
  194.7 21.8 %collective-permute-start.40 = (bf16[768,384]{1,0:T(8,128)(2,1)S(1)}, bf16[768,384]{1,0:T(8,128)(2,1)S(1)}, u32[]{:S(2)}, u32[]{:S(2)}) collective-permute-start(bf16[768,384]{1,0:T(8,128)(2,1)S(1)} %slice.317), channel_id=1, source_target_pairs={{0,4},{4,0},{1,5},{5,1},{2,6},{6,2},{3,7},{7,3},{8,12},{12,8},{9,1... | collective-permute-start | bytes 1769480 | tf_op jit(solution)/shard_map/ppermute | solution.py:547
  195.4 19.5 %collective-permute-start.37 = (bf16[512,768]{1,0:T(8,128)(2,1)S(1)}, bf16[512,768]{1,0:T(8,128)(2,1)S(1)}, u32[]{:S(2)}, u32[]{:S(2)}) collective-permute-start(bf16[512,768]{1,0:T(8,128)(2,1)S(1)} %add_convert_fusion.1.partial_ref), channel_id=1, source_target_pairs={{0,2},{1,3},{2,0},{3,1},{4,6},{5,7},{6,4},{7,5},{8,10},{9,11},{10,... | collective-permute-start | bytes 2359304 | tf_op jit(solution)/shard_map/ppermute | solution.py:547
  224.1 5.9 %collective-permute-start.42 = (bf16[512,768]{1,0:T(8,128)(2,1)S(1)}, bf16[512,768]{1,0:T(8,128)(2,1)S(1)}, u32[]{:S(2)}, u32[]{:S(2)}) collective-permute-start(bf16[512,768]{1,0:T(8,128)(2,1)S(1)} %get-tuple-element.269), channel_id=1, source_target_pairs={{0,1},{1,0},{2,3},{3,2},{4,5},{5,4},{6,7},{7,6},{8,9},{9,8},{10,11... | collective-permute-start | bytes 2359304 | tf_op jit(solution)/shard_map/ppermute | solution.py:547
  224.4 7.2 %collective-permute-start.38 = (bf16[128,768]{1,0:T(8,128)(2,1)S(1)}, bf16[128,768]{1,0:T(8,128)(2,1)S(1)}, u32[]{:S(2)}, u32[]{:S(2)}) collective-permute-start(bf16[128,768]{1,0:T(8,128)(2,1)S(1)} %get-tuple-element.363), channel_id=1, source_target_pairs={{0,4},{4,0},{1,5},{5,1},{2,6},{6,2},{3,7},{7,3},{8,12},{12,8},{9,1... | collective-permute-start | bytes 589832 | tf_op jit(solution)/shard_map/ppermute | solution.py:547
  226.1 24.4 %collective-permute-start.44 = (bf16[384,384]{1,0:T(8,128)(2,1)S(1)}, bf16[384,384]{1,0:T(8,128)(2,1)S(1)}, u32[]{:S(2)}, u32[]{:S(2)}) collective-permute-start(bf16[384,384]{1,0:T(8,128)(2,1)S(1)} %slice.503), channel_id=1, source_target_pairs={{0,8},{8,0},{16,24},{24,16},{1,9},{9,1},{17,25},{25,17},{2,10},{10... | collective-permute-start | bytes 884744 | tf_op jit(solution)/shard_map/ppermute | solution.py:547
  227.1 23.5 %collective-permute-start.45 = (bf16[192,768]{1,0:T(8,128)(2,1)S(1)}, bf16[192,768]{1,0:T(8,128)(2,1)S(1)}, u32[]{:S(2)}, u32[]{:S(2)}) collective-permute-start(bf16[192,768]{1,0:T(8,128)(2,1)S(1)} %slice.502), channel_id=1, source_target_pairs={{0,16},{8,24},{16,0},{24,8},{1,17},{9,25},{17,1},{25,9},{2,18},{10... | collective-permute-start | bytes 884744 | tf_op jit(solution)/shard_map/ppermute | solution.py:547
  229.5 21.1 %collective-permute-start.46 = (bf16[768,384]{1,0:T(8,128)(2,1)S(1)}, bf16[768,384]{1,0:T(8,128)(2,1)S(1)}, u32[]{:S(2)}, u32[]{:S(2)}) collective-permute-start(bf16[768,384]{1,0:T(8,128)(2,1)S(1)} %slice.324), channel_id=1, source_target_pairs={{0,4},{4,0},{1,5},{5,1},{2,6},{6,2},{3,7},{7,3},{8,12},{12,8},{9,1... | collective-permute-start | bytes 1769480 | tf_op jit(solution)/shard_map/ppermute | solution.py:547
  230.2 18.8 %collective-permute-start.43 = (bf16[512,768]{1,0:T(8,128)(2,1)S(1)}, bf16[512,768]{1,0:T(8,128)(2,1)S(1)}, u32[]{:S(2)}, u32[]{:S(2)}) collective-permute-start(bf16[512,768]{1,0:T(8,128)(2,1)S(1)} %add_convert_fusion.partial_ref), channel_id=1, source_target_pairs={{0,2},{1,3},{2,0},{3,1},{4,6},{5,7},{6,4},{7,5},{8,10},{9,11},{10,... | collective-permute-start | bytes 2359304 | tf_op jit(solution)/shard_map/ppermute | solution.py:547
  250.6 4.8 %collective-permute-start.47 = (bf16[512,768]{1,0:T(8,128)(2,1)S(1)}, bf16[512,768]{1,0:T(8,128)(2,1)S(1)}, u32[]{:S(2)}, u32[]{:S(2)}) collective-permute-start(bf16[512,768]{1,0:T(8,128)(2,1)S(1)} %get-tuple-element.276.refs_1_), channel_id=1, source_target_pairs={{0,1},{1,0},{2,3},{3,2},{4,5},{5,4},{6,7},{7,6},{8,9},{9,8},{10,11... | collective-permute-start | bytes 2359304 | tf_op jit(solution)/shard_map/ppermute | solution.py:547
  250.7 14.4 %collective-permute-start.50 = (bf16[192,384]{1,0:T(8,128)(2,1)S(1)}, bf16[192,384]{1,0:T(8,128)(2,1)S(1)}, u32[]{:S(2)}, u32[]{:S(2)}) collective-permute-start(bf16[192,384]{1,0:T(8,128)(2,1)S(1)} %slice.507), channel_id=1, source_target_pairs={{0,16},{8,24},{16,0},{24,8},{1,17},{9,25},{17,1},{25,9},{2,18},{10... | collective-permute-start | bytes 442376 | tf_op jit(solution)/shard_map/ppermute | solution.py:547
  252.7 12.5 %collective-permute-start.51 = (bf16[384,384]{1,0:T(8,128)(2,1)S(1)}, bf16[384,384]{1,0:T(8,128)(2,1)S(1)}, u32[]{:S(2)}, u32[]{:S(2)}) collective-permute-start(bf16[384,384]{1,0:T(8,128)(2,1)S(1)} %slice.501), channel_id=1, source_target_pairs={{0,8},{8,0},{16,24},{24,16},{1,9},{9,1},{17,25},{25,17},{2,10},{10... | collective-permute-start | bytes 884744 | tf_op jit(solution)/shard_map/ppermute | solution.py:547
  253.2 12.0 %collective-permute-start.52 = (bf16[384,384]{1,0:T(8,128)(2,1)S(1)}, bf16[384,384]{1,0:T(8,128)(2,1)S(1)}, u32[]{:S(2)}, u32[]{:S(2)}) collective-permute-start(bf16[384,384]{1,0:T(8,128)(2,1)S(1)} %get-tuple-element.353), channel_id=1, source_target_pairs={{0,4},{4,0},{1,5},{5,1},{2,6},{6,2},{3,7},{7,3},{8,12},{12,8},{9,1... | collective-permute-start | bytes 884744 | tf_op jit(solution)/shard_map/ppermute | solution.py:547
  254.7 30.6 %collective-permute-start.56 = (bf16[384,384]{1,0:T(8,128)(2,1)S(1)}, bf16[384,384]{1,0:T(8,128)(2,1)S(1)}, u32[]{:S(2)}, u32[]{:S(2)}) collective-permute-start(bf16[384,384]{1,0:T(8,128)(2,1)S(1)} %get-tuple-element.352), channel_id=1, source_target_pairs={{0,4},{4,0},{1,5},{5,1},{2,6},{6,2},{3,7},{7,3},{8,12},{12,8},{9,1... | collective-permute-start | bytes 884744 | tf_op jit(solution)/shard_map/ppermute | solution.py:547
  265.2 6.1 %collective-permute-start.53 = (bf16[512,768]{1,0:T(8,128)(2,1)S(1)}, bf16[512,768]{1,0:T(8,128)(2,1)S(1)}, u32[]{:S(2)}, u32[]{:S(2)}) collective-permute-start(bf16[512,768]{1,0:T(8,128)(2,1)S(1)} %get-tuple-element.291), channel_id=1, source_target_pairs={{0,1},{1,0},{2,3},{3,2},{4,5},{5,4},{6,7},{7,6},{8,9},{9,8},{10,11... | collective-permute-start | bytes 2359304 | tf_op jit(solution)/shard_map/ppermute | solution.py:547
  267.6 26.8 %collective-permute-start.48 = (bf16[768,128]{1,0:T(8,128)(2,1)S(1)}, bf16[768,128]{1,0:T(8,128)(2,1)S(1)}, u32[]{:S(2)}, u32[]{:S(2)}) collective-permute-start(bf16[768,128]{1,0:T(8,128)(2,1)S(1)} %get-tuple-element.348), channel_id=1, source_target_pairs={{0,4},{4,0},{1,5},{5,1},{2,6},{6,2},{3,7},{7,3},{8,12},{12,8},{9,1... | collective-permute-start | bytes 589832 | tf_op jit(solution)/shard_map/ppermute | solution.py:547
  269.1 25.3 %collective-permute-start.49 = (bf16[384,512]{1,0:T(8,128)(2,1)S(1)}, bf16[384,512]{1,0:T(8,128)(2,1)S(1)}, u32[]{:S(2)}, u32[]{:S(2)}) collective-permute-start(bf16[384,512]{1,0:T(8,128)(2,1)S(1)} %slice.383), channel_id=1, source_target_pairs={{0,8},{8,0},{16,24},{24,16},{1,9},{9,1},{17,25},{25,17},{2,10},{10... | collective-permute-start | bytes 1179656 | tf_op jit(solution)/shard_map/ppermute | solution.py:547
  269.9 26.3 %collective-permute-start.57 = (bf16[384,768]{1,0:T(8,128)(2,1)S(1)}, bf16[384,768]{1,0:T(8,128)(2,1)S(1)}, u32[]{:S(2)}, u32[]{:S(2)}) collective-permute-start(bf16[384,768]{1,0:T(8,128)(2,1)S(1)} %slice.336), channel_id=1, source_target_pairs={{0,8},{8,0},{16,24},{24,16},{1,9},{9,1},{17,25},{25,17},{2,10},{10... | collective-permute-start | bytes 1769480 | tf_op jit(solution)/shard_map/ppermute | solution.py:547
  271.4 10.7 %collective-permute-start.54 = (bf16[256,768]{1,0:T(8,128)(2,1)S(1)}, bf16[256,768]{1,0:T(8,128)(2,1)S(1)}, u32[]{:S(2)}, u32[]{:S(2)}) collective-permute-start(bf16[256,768]{1,0:T(8,128)(2,1)S(1)} %add_convert_fusion.6), channel_id=1, source_target_pairs={{0,2},{1,3},{2,0},{3,1},{4,6},{5,7},{6,4},{7,5},{8,10},{9,11},{10,... | collective-permute-start | bytes 1179656 | tf_op jit(solution)/shard_map/ppermute | solution.py:547
  282.2 12.2 %collective-permute-start.58 = (bf16[192,384]{1,0:T(8,128)(2,1)S(1)}, bf16[192,384]{1,0:T(8,128)(2,1)S(1)}, u32[]{:S(2)}, u32[]{:S(2)}) collective-permute-start(bf16[192,384]{1,0:T(8,128)(2,1)S(1)} %slice.506), channel_id=1, source_target_pairs={{0,16},{8,24},{16,0},{24,8},{1,17},{9,25},{17,1},{25,9},{2,18},{10... | collective-permute-start | bytes 442376 | tf_op jit(solution)/shard_map/ppermute | solution.py:547
  285.3 10.8 %collective-permute-start.55 = (f32[16,768]{1,0:T(8,128)S(1)}, f32[16,768]{1,0:T(8,128)S(1)}, u32[]{:S(2)}, u32[]{:S(2)}) collective-permute-start(f32[16,768]{1,0:T(8,128)S(1)} %get-tuple-element.292), channel_id=1, source_target_pairs={{0,1},{1,0},{2,3},{3,2},{4,5},{5,4},{6,7},{7,6},{8,9},{9,8},{10,11... | collective-permute-start | bytes 147464 | tf_op jit(solution)/shard_map/ppermute | solution.py:547
  296.4 8.2 %collective-permute-start.60 = (bf16[384,128]{1,0:T(8,128)(2,1)S(1)}, bf16[384,128]{1,0:T(8,128)(2,1)S(1)}, u32[]{:S(2)}, u32[]{:S(2)}) collective-permute-start(bf16[384,128]{1,0:T(8,128)(2,1)S(1)} %slice.508), channel_id=1, source_target_pairs={{0,8},{8,0},{16,24},{24,16},{1,9},{9,1},{17,25},{25,17},{2,10},{10... | collective-permute-start | bytes 294920 | tf_op jit(solution)/shard_map/ppermute | solution.py:547
  298.3 12.0 %collective-permute-start.61 = (bf16[192,512]{1,0:T(8,128)(2,1)S(1)}, bf16[192,512]{1,0:T(8,128)(2,1)S(1)}, u32[]{:S(2)}, u32[]{:S(2)}) collective-permute-start(bf16[192,512]{1,0:T(8,128)(2,1)S(1)} %slice.504), channel_id=1, source_target_pairs={{0,16},{8,24},{16,0},{24,8},{1,17},{9,25},{17,1},{25,9},{2,18},{10... | collective-permute-start | bytes 589832 | tf_op jit(solution)/shard_map/ppermute | solution.py:547
  299.7 4.1 %collective-permute-start.62 = (f32[16,768]{1,0:T(8,128)S(1)}, f32[16,768]{1,0:T(8,128)S(1)}, u32[]{:S(2)}, u32[]{:S(2)}) collective-permute-start(f32[16,768]{1,0:T(8,128)S(1)} %add.148), channel_id=1, source_target_pairs={{0,2},{1,3},{2,0},{3,1},{4,6},{5,7},{6,4},{7,5},{8,10},{9,11},{10,... | collective-permute-start | bytes 147464 | tf_op jit(solution)/shard_map/ppermute | solution.py:547
  300.9 14.4 %collective-permute-start.63 = (bf16[384,384]{1,0:T(8,128)(2,1)S(1)}, bf16[384,384]{1,0:T(8,128)(2,1)S(1)}, u32[]{:S(2)}, u32[]{:S(2)}) collective-permute-start(bf16[384,384]{1,0:T(8,128)(2,1)S(1)} %slice.500), channel_id=1, source_target_pairs={{0,8},{8,0},{16,24},{24,16},{1,9},{9,1},{17,25},{25,17},{2,10},{10... | collective-permute-start | bytes 884744 | tf_op jit(solution)/shard_map/ppermute | solution.py:547
  301.9 20.0 %collective-permute-start.64 = (bf16[192,768]{1,0:T(8,128)(2,1)S(1)}, bf16[192,768]{1,0:T(8,128)(2,1)S(1)}, u32[]{:S(2)}, u32[]{:S(2)}) collective-permute-start(bf16[192,768]{1,0:T(8,128)(2,1)S(1)} %slice.499), channel_id=1, source_target_pairs={{0,16},{8,24},{16,0},{24,8},{1,17},{9,25},{17,1},{25,9},{2,18},{10... | collective-permute-start | bytes 884744 | tf_op jit(solution)/shard_map/ppermute | solution.py:547
  303.7 37.0 %collective-permute-start.59 = (bf16[128,768]{1,0:T(8,128)(2,1)S(1)}, bf16[128,768]{1,0:T(8,128)(2,1)S(1)}, u32[]{:S(2)}, u32[]{:S(2)}) collective-permute-start(bf16[128,768]{1,0:T(8,128)(2,1)S(1)} %slice_select_fusion), channel_id=1, source_target_pairs={{0,4},{4,0},{1,5},{5,1},{2,6},{6,2},{3,7},{7,3},{8,12},{12,8},{9,1... | collective-permute-start | bytes 589832 | tf_op jit(solution)/shard_map/ppermute | solution.py:547
  304.6 36.0 %collective-permute-start.67 = (bf16[192,1536]{1,0:T(8,128)(2,1)S(1)}, bf16[192,1536]{1,0:T(8,128)(2,1)S(1)}, u32[]{:S(2)}, u32[]{:S(2)}) collective-permute-start(bf16[192,1536]{1,0:T(8,128)(2,1)S(1)} %pad_maximum_fusion.6), channel_id=1, source_target_pairs={{0,4},{4,0},{1,5},{5,1},{2,6},{6,2},{3,7},{7,3},{8,12},{12,8},{9,1... | collective-permute-start | bytes 1769480 | tf_op jit(solution)/shard_map/ppermute | solution.py:547
  321.9 12.7 %collective-permute-start.65 = (bf16[192,512]{1,0:T(8,128)(2,1)S(1)}, bf16[192,512]{1,0:T(8,128)(2,1)S(1)}, u32[]{:S(2)}, u32[]{:S(2)}) collective-permute-start(bf16[192,512]{1,0:T(8,128)(2,1)S(1)} %fusion.68.refs_0_), channel_id=1, source_target_pairs={{0,4},{4,0},{1,5},{5,1},{2,6},{6,2},{3,7},{7,3},{8,12},{12,8},{9,1... | collective-permute-start | bytes 589832 | tf_op jit(solution)/shard_map/ppermute | solution.py:547
  323.5 8.2 %collective-permute-start.69 = (bf16[192,128]{1,0:T(8,128)(2,1)S(1)}, bf16[192,128]{1,0:T(8,128)(2,1)S(1)}, u32[]{:S(2)}, u32[]{:S(2)}) collective-permute-start(bf16[192,128]{1,0:T(8,128)(2,1)S(1)} %slice.509), channel_id=1, source_target_pairs={{0,16},{8,24},{16,0},{24,8},{1,17},{9,25},{17,1},{25,9},{2,18},{10... | collective-permute-start | bytes 147464 | tf_op jit(solution)/shard_map/ppermute | solution.py:547
  323.6 10.2 %collective-permute-start.70 = (bf16[192,384]{1,0:T(8,128)(2,1)S(1)}, bf16[192,384]{1,0:T(8,128)(2,1)S(1)}, u32[]{:S(2)}, u32[]{:S(2)}) collective-permute-start(bf16[192,384]{1,0:T(8,128)(2,1)S(1)} %slice.505), channel_id=1, source_target_pairs={{0,16},{8,24},{16,0},{24,8},{1,17},{9,25},{17,1},{25,9},{2,18},{10... | collective-permute-start | bytes 442376 | tf_op jit(solution)/shard_map/ppermute | solution.py:547
  331.7 8.9 %collective-permute-start.66 = (f32[256,256]{1,0:T(8,128)S(1)}, f32[256,256]{1,0:T(8,128)S(1)}, u32[]{:S(2)}, u32[]{:S(2)}) collective-permute-start(f32[256,256]{1,0:T(8,128)S(1)} %pack_grads.1), channel_id=1, source_target_pairs={{0,4},{4,0},{1,5},{5,1},{2,6},{6,2},{3,7},{7,3},{8,12},{12,8},{9,1... | collective-permute-start | bytes 786440 | tf_op jit(solution)/shard_map/ppermute | solution.py:547
  333.8 8.6 %collective-permute-start.71 = (bf16[192,128]{1,0:T(8,128)(2,1)S(1)}, bf16[192,128]{1,0:T(8,128)(2,1)S(1)}, u32[]{:S(2)}, u32[]{:S(2)}) collective-permute-start(bf16[192,128]{1,0:T(8,128)(2,1)S(1)} %fusion.87.refs_2_), channel_id=1, source_target_pairs={{0,4},{4,0},{1,5},{5,1},{2,6},{6,2},{3,7},{7,3},{8,12},{12,8},{9,1... | collective-permute-start | bytes 147464 | tf_op jit(solution)/shard_map/ppermute | solution.py:547
  334.6 17.2 %collective-permute-start.73 = (bf16[192,1152]{1,0:T(8,128)(2,1)S(1)}, bf16[192,1152]{1,0:T(8,128)(2,1)S(1)}, u32[]{:S(2)}, u32[]{:S(2)}) collective-permute-start(bf16[192,1152]{1,0:T(8,128)(2,1)S(1)} %get-tuple-element.374), channel_id=1, source_target_pairs={{0,4},{4,0},{1,5},{5,1},{2,6},{6,2},{3,7},{7,3},{8,12},{12,8},{9,1... | collective-permute-start | bytes 1327112 | tf_op jit(solution)/shard_map/ppermute | solution.py:547
  340.6 5.0 %collective-permute-start.68 = (f32[128,256]{1,0:T(8,128)S(1)}, f32[128,256]{1,0:T(8,128)S(1)}, u32[]{:S(2)}, u32[]{:S(2)}) collective-permute-start(f32[128,256]{1,0:T(8,128)S(1)} %slice.404), channel_id=1, source_target_pairs={{0,8},{8,0},{16,24},{24,16},{1,9},{9,1},{17,25},{25,17},{2,10},{10... | collective-permute-start | bytes 393224 | tf_op jit(solution)/shard_map/ppermute | solution.py:547
  345.7 5.4 %collective-permute-start.72 = (f32[64,256]{1,0:T(8,128)S(1)}, f32[64,256]{1,0:T(8,128)S(1)}, u32[]{:S(2)}, u32[]{:S(2)}) collective-permute-start(f32[64,256]{1,0:T(8,128)S(1)} %slice.410), channel_id=1, source_target_pairs={{0,16},{8,24},{16,0},{24,8},{1,17},{9,25},{17,1},{25,9},{2,18},{10... | collective-permute-start | bytes 196616 | tf_op jit(solution)/shard_map/ppermute | solution.py:547
  (20 other events, 178.5 us)
where the time goes:
time: 358 us; the launch traced here: 354 us
  waiting for transfers between devices  177 us (49%)
  starting transfers between devices  76.5 us (21%)
  Pallas kernels  75.6 us (21%)
  matrix products  13.6 us (4%)
  other arithmetic  8.01 us (2%)
    ppermute x74, waiting for transfers between devices, swap(): return row_major(lax.ppermute(row_major(value), axis, route))  177 us
    ppermute x74, starting transfers between devices, swap(): return row_major(lax.ppermute(row_major(value), axis, route))  76.5 us
    pallas_call x8, Pallas kernels, call(): pl.pallas_call(body, out_shape=tuple(outputs), in_specs=[SMEM if v.ndim =...  53.4 us
    dot_general x8, matrix products, dot_down(): lax.dot_general(left, right, (((0,), (0,)), ((), ())), preferred_element_...  9.94 us
    pallas_call x8, Pallas kernels, row_call(): pl.pallas_call(body, grid=(1,), out_shape=tuple(outputs), in_specs=specs,...  9.69 us
  transfers between devices with their start and end apart: 74, of which 39 were waited for; matrix products, arithmetic and copies ran while one was open for 6% of the time, Pallas kernels for 16%

commit v1 on v0

--- a/solution.py
+++ b/solution.py
@@ -1570,6 +1570,10 @@
     return (kept + arrived.astype(F32)).astype(BF16)
 
 
+def added(first, second):
+    return (first.astype(F32) + second.astype(F32)).astype(BF16)
+
+
 def send_columns(value, cross):
     middle = value.shape[1] // 2
     return cross(value[:, middle:].astype(BF16))
@@ -1691,72 +1695,83 @@
         *feed_t[0], branch, branch_far, *feed_t[1]
     )
     partial = core_sum(kept, cross_core(sent))
-    final_sent, final_kept = feed_forward(*feed_t[0], *feed_t[1])
     part_r = times_down(stacked(branch, branch_far), active, BF16)
+    part_r, partial = pin(part_r, partial)
+    r_moved = send_rows(part_r, cross_near)
     part_e = times_down(stacked(near_two_t, far_two_t), grad_hidden, BF16)
+    e_moved = send_columns(part_e, cross_y)
+    late_t, _ = pin(near_two_t, part_e)
+    final_sent, final_kept = feed_forward(late_t, far_two_t, *feed_t[1])
     grad_middle, near_grad, sums = norm_back_near(
         branch, partial, cross_x(partial), middle_t, gains_t, 3, sums, 9
     )
-    near_grad, part_r, part_e, final_sent, final_kept = pin(
-        near_grad, part_r, part_e, final_sent, final_kept
-    )
-    r_moved, e_moved = send_rows(part_r, cross_near), send_columns(part_e, cross_y)
+    near_grad, r_moved, e_moved, final_sent, final_kept = pin(
+        near_grad, r_moved, e_moved, final_sent, final_kept
+    )
+    part_e, part_r = keep_columns(part_e, e_moved), keep_rows(part_r, r_moved)
+    e_moved = send_rows(part_e, cross_near)
     far_grad = cross_core(near_grad)
-    final_arrived = cross_core(final_sent)
-    final_across = cross_x(halves_added(final_kept, final_arrived))
     sent, kept, grad_qkv, qkv_sum_t = attention_backward(
         near_grad, far_grad, attend_t, context, saved_t, doc_max
     )
-    sent, final_across = pin(sent, final_across)
+    sent, e_moved, part_r = pin(sent, e_moved, part_r)
+    part_e = keep_rows(part_e, e_moved)
+    e_moved, r_moved = send_rows(part_e, cross_far), send_rows(part_r, cross_far)
     partial = core_sum(kept, cross_core(sent))
     part_a = beside(
         times_down(stacked(near_t, far_t), grad_qkv, BF16),
         times_down(stacked(near_grad, far_grad), saved_t[1], BF16),
     )
-    part_a = beside(*column_halves(part_a, y_index))
+    part_a, a_moved = column_halves(part_a, y_index)
+    a_moved = cross_y(a_moved)
     grad_between, branch, sums = norm_back_near(
         grad_middle, partial, cross_x(partial), between, gains_t, 0, sums, 6
     )
 
-    branch, r_moved, e_moved, part_a = pin(branch, r_moved, e_moved, part_a)
-    part_e, part_r = keep_columns(part_e, e_moved), keep_rows(part_r, r_moved)
-    e_moved, r_moved = send_rows(part_e, cross_near), send_rows(part_r, cross_far)
-    a_moved = send_columns(part_a, cross_y)
+    branch, e_moved, r_moved, a_moved = pin(branch, e_moved, r_moved, a_moved)
+    part_e, part_r = keep_rows(part_e, e_moved), keep_rows(part_r, r_moved)
+    part_a = part_a.astype(F32) + a_moved.astype(F32)
     branch_far = cross_core(branch)
     sent, kept, active, grad_hidden, hidden_sum_s = feed_backward(
         *feed_s[0], branch, branch_far, *feed_s[1]
     )
     partial = core_sum(kept, cross_core(sent))
     feed_r = times_down(stacked(branch, branch_far), active, BF16)
+    feed_r, part_a, partial = pin(feed_r, part_a, partial)
+    fr_moved, a_moved = send_rows(feed_r, cross_near), send_rows(part_a, cross_near)
     feed_e = times_down(stacked(near_two_s, far_two_s), grad_hidden, BF16)
+    fe_moved = send_columns(feed_e, cross_y)
     grad_middle, near_grad, sums = norm_back_near(
         grad_between, partial, cross_x(partial), middle_s, gains_s, 3, sums, 3
     )
-    near_grad, e_moved, r_moved, a_moved, feed_e, feed_r = pin(
-        near_grad, e_moved, r_moved, a_moved, feed_e, feed_r
-    )
-    part_e, part_r = keep_rows(part_e, e_moved), keep_rows(part_r, r_moved)
-    part_a = keep_columns(part_a, a_moved)
-    e_moved, a_moved = send_rows(part_e, cross_far), send_rows(part_a, cross_near)
-    fe_moved = cross_y(feed_e[:half, half:])
+    near_grad, a_moved, fr_moved, fe_moved, part_e, part_r = pin(
+        near_grad, a_moved, fr_moved, fe_moved, part_e, part_r
+    )
+    part_a, feed_r, feed_e = (
+        keep_rows(part_a, a_moved),
+        keep_rows(feed_r, fr_moved),
+        keep_columns(feed_e, fe_moved),
+    )
+    a_moved, fe_moved = send_rows(part_a, cross_far), send_rows(feed_e, cross_near)
+    mine_t = beside(part_e, part_r).astype(BF16)
+    theirs_t = cross_y(
+        beside(mine_t[:, :half], mine_t[:, 2 * half :], mine_t[:, half : 2 * half])
+    )
     far_grad = cross_core(near_grad)
     sent, kept, grad_qkv, qkv_sum_s = attention_backward(
         near_grad, far_grad, attend_s, context, saved_s, doc_max
     )
-    sent, e_moved, a_moved, fe_moved, feed_r = pin(sent, e_moved, a_moved, fe_moved, feed_r)
-    part_e, part_a = keep_rows(part_e, e_moved), keep_rows(part_a, a_moved)
-    fe_moved_two = cross_y(feed_e[half:, half:])
-    fr_moved, at_moved = send_rows(feed_r, cross_near), send_rows(part_a, cross_far)
+    sent, a_moved, fe_moved, theirs_t, feed_r = pin(sent, a_moved, fe_moved, theirs_t, feed_r)
+    mine_at, feed_e = keep_rows(part_a, a_moved), keep_rows(feed_e, fe_moved)
+    fr_moved, fe_moved = send_rows(feed_r, cross_far), send_rows(feed_e, cross_far)
     arrived = cross_core(sent)
     across = cross_x(halves_added(kept, arrived))
     grad_a = beside(
         times_down(stacked(near_s, far_s), grad_qkv, BF16),
         times_down(stacked(near_grad, far_grad), saved_s[1], BF16),
     )
-    whole = features - 256
-    grad_z, grad_a = grad_a[:, :whole], grad_a[:, whole:]
     grad_a, y_moved = column_halves(grad_a, y_index)
-    y_moved, z_moved = cross_y(y_moved), send_rows(grad_z, cross_near)
+    y_moved = cross_y(y_moved)
     grad_in, _, sums = norm_back(
         grad_middle, (kept, arrived, across), stream, gains_s, 0, sums, 0
     )
@@ -1777,31 +1792,17 @@
         kept = jnp.where(y_index == 0, value[:tokens], value[tokens:])
         return jnp.where(y_index == 0, jnp.stack([kept, received]), jnp.stack([received, kept]))
 
-    y_moved, z_moved, sums_moved, input_grad, fe_moved_two, fr_moved, at_moved = pin(
-        y_moved, z_moved, sums_moved, input_grad, fe_moved_two, fr_moved, at_moved
-    )
+    grad_moved = swapped(input_grad.astype(BF16))
+    y_moved, sums_moved = pin(y_moved, sums_moved)
     grad_a = grad_a.astype(F32) + y_moved.astype(F32)
-    grad_z = keep_rows(grad_z, z_moved)
-    y_moved, z_moved = send_rows(grad_a, cross_near), send_rows(grad_z, cross_far)
+    y_moved = send_rows(grad_a, cross_near)
     sums = sums + sums_moved
     sums_moved = cross_x(sums)
-    feed_e, feed_r = keep_columns(feed_e, stacked(fe_moved, fe_moved_two)), keep_rows(feed_r, fr_moved)
-    fe_moved, fr_moved = send_rows(feed_e, cross_near), send_rows(feed_r, cross_far)
-    mine_t = beside(part_e, part_r, keep_rows(part_a, at_moved)).astype(BF16)
-    theirs_t = cross_y(
-        beside(
-            mine_t[:, :half], mine_t[:, 2 * half : 3 * half], mine_t[:, half : 2 * half], mine_t[:, 3 * half :]
-        )
-    )
-    grad_moved = swapped(input_grad.astype(BF16)).astype(F32)
-    y_moved, z_moved, sums_moved, fe_moved, fr_moved = pin(
-        y_moved, z_moved, sums_moved, fe_moved, fr_moved
-    )
-    grad_a = keep_rows(grad_a, y_moved)
-    grad_z = keep_rows(grad_z, z_moved).astype(BF16)
-    y_moved, z_moved = send_rows(grad_a, cross_far), cross_y(grad_z)
-    feed_e, feed_r = keep_rows(feed_e, fe_moved), keep_rows(feed_r, fr_moved)
-    fe_moved = send_rows(feed_e, cross_far)
+    final_arrived = cross_core(final_sent)
+    fe_moved, fr_moved, mine_at, sums_moved, final_arrived, grad_moved = pin(
+        fe_moved, fr_moved, mine_at, sums_moved, final_arrived, grad_moved
+    )
+    final_across = cross_x(halves_added(final_kept, final_arrived))
     pack = pack_grads(
         sums + sums_moved,
         (qkv_sum_s, qkv_sum_t),
@@ -1811,39 +1812,42 @@
         params[3].shape,
         params[9].shape,
     )
+    mine_s = beside(keep_rows(feed_e, fe_moved), keep_rows(feed_r, fr_moved), mine_at).astype(BF16)
+    pack, mine_s = pin(pack, mine_s)
     pack_moved = cross_y(pack)
-    y_moved, fe_moved = pin(y_moved, fe_moved)
-    mine_a = keep_rows(grad_a, y_moved).astype(BF16)
-    theirs_a = cross_y(mine_a)
-    mine_s = beside(keep_rows(feed_e, fe_moved), feed_r).astype(BF16)
     theirs_s = cross_y(
-        beside(mine_s[:, :half], mine_s[:, 2 * half :], mine_s[:, half : 2 * half])
-    )
-    z_moved, pack_moved, theirs_t = pin(z_moved, pack_moved, theirs_t)
-    pack = pack + pack_moved
-    pack_near = cross_near(pack[2 * ROWS :])
-    expand_grad_t, reduce_grad_t = finish_feed(
-        mine_t[:, : 3 * half], theirs_t[:, : 3 * half], place, half
-    )
-    pack_near, theirs_a, expand_grad_t, reduce_grad_t = pin(
-        pack_near, theirs_a, expand_grad_t, reduce_grad_t
-    )
-    pack = pack[: 2 * ROWS] + pack_near
-    pack_far = cross_far(pack[ROWS:])
-    merged_grad_s, output_grad_s = finish_attend(
-        (grad_z, z_moved), mine_a, theirs_a, place
-    )
-    merged_grad_t, output_grad_t = finish_attend(
-        (), mine_t[:, 3 * half :], theirs_t[:, 3 * half :], place
-    )
-    expand_grad_s, reduce_grad_s = finish_feed(mine_s, theirs_s, place, half)
-    vectors = unpack_grads(pack, pack_far, local, params[3].shape, params[9].shape)
-    middle_t, final_across, grad_between = pin(middle_t, final_across, grad_between)
+        beside(
+            mine_s[:, :half], mine_s[:, 2 * half : 3 * half], mine_s[:, half : 2 * half], mine_s[:, 3 * half :]
+        )
+    )
+    expand_grad_t, reduce_grad_t = finish_feed(mine_t, theirs_t, place, half)
+    y_moved, final_across, expand_grad_t = pin(y_moved, final_across, expand_grad_t)
+    grad_a = keep_rows(grad_a, y_moved)
+    y_moved = send_rows(grad_a, cross_far)
     rows = 2 * tokens
     final = middle_t[:rows] + gains_t[5:6] + final_kept[:rows] + final_across.astype(F32)
     final = final + final_arrived[:rows].astype(F32)
     final = times_across(final.astype(BF16), chooser, BF16)
-    outputs = [restore(final, swapped(final)), restore(input_grad, grad_moved)]
+    y_moved, pack_moved, final = pin(y_moved, pack_moved, final)
+    pack = pack + pack_moved
+    pack_near = cross_near(pack[2 * ROWS :])
+    mine_a = keep_rows(grad_a, y_moved).astype(BF16)
+    theirs_a = cross_y(mine_a)
+    final_moved = swapped(final)
+    merged_grad_t, output_grad_t = finish_attend(
+        (), mine_s[:, 3 * half :], theirs_s[:, 3 * half :], place
+    )
+    pack_near, output_grad_t = pin(pack_near, output_grad_t)
+    pack = pack[: 2 * ROWS] + pack_near
+    pack_far = cross_far(pack[ROWS:])
+    theirs_a, final_moved = pin(theirs_a, final_moved)
+    grad_moved = grad_moved.astype(F32)
+    merged_grad_s, output_grad_s = finish_attend((), mine_a, theirs_a, place)
+    expand_grad_s, reduce_grad_s = finish_feed(
+        mine_s[:, : 3 * half], theirs_s[:, : 3 * half], place, half
+    )
+    vectors = unpack_grads(pack, pack_far, local, params[3].shape, params[9].shape)
+    outputs = [restore(final, final_moved), restore(input_grad, grad_moved)]
     for vector, merged, output, expand, reduce in (
         (vectors[:8], merged_grad_s, output_grad_s, expand_grad_s, reduce_grad_s),
         (vectors[8:], merged_grad_t, output_grad_t, expand_grad_t, reduce_grad_t),

time: 358 us -> 334 us (0.933)
  waiting for transfers between devices: 177 us -> 161 us
  starting transfers between devices: 76.5 us -> 68.2 us
    ppermute x74 -> x70, waiting for transfers between devices: 177 us -> 161 us  [swap(): return row_major(lax.ppermute(row_major(value), axis, route))]
    ppermute x74 -> x70, starting transfers between devices: 76.5 us -> 68.2 us  [swap(): return row_major(lax.ppermute(row_major(value), axis, route))]
  transfers between devices with their start and end apart: 74 -> 70, of which waited for: 39 -> 41; matrix products, arithmetic and copies ran while one was open for 6% -> 7% of each run, Pallas kernels for 16% -> 18%
where the time goes in v1:
time: 334 us; the launch traced here: 329 us
  waiting for transfers between devices  161 us (48%)
  Pallas kernels  75.6 us (23%)
  starting transfers between devices  68.2 us (20%)
  matrix products  13.6 us (4%)
  other arithmetic  8.1 us (2%)
    ppermute x70, waiting for transfers between devices, swap(): return row_major(lax.ppermute(row_major(value), axis, route))  161 us
    ppermute x70, starting transfers between devices, swap(): return row_major(lax.ppermute(row_major(value), axis, route))  68.2 us
    pallas_call x8, Pallas kernels, call(): pl.pallas_call(body, out_shape=tuple(outputs), in_specs=[SMEM if v.ndim =...  53.3 us
    dot_general x8, matrix products, dot_down(): lax.dot_general(left, right, (((0,), (0,)), ((), ())), preferred_element_...  9.94 us
    pallas_call x8, Pallas kernels, row_call(): pl.pallas_call(body, grid=(1,), out_shape=tuple(outputs), in_specs=specs,...  9.86 us
  transfers between devices with their start and end apart: 70, of which 41 were waited for; matrix products, arithmetic and copies ran while one was open for 7% of the time, Pallas kernels for 18%

profile of v1, /device:TPU:0, one launch (start us, length us, event | category | flops | bytes accessed | tf_op | source)
XLA Modules:
  0.0 329.4 jit_solution(14949728558898911736)
XLA Ops:
  0.7 2.4 prepare_first.1.refs_0_.refs_6_
  3.1 3.1 collective-permute-start.2
  6.2 2.6 collective-permute-start.3
  10.6 1.6 collective-permute-start
  13.5 5.5 %collective-permute-done = bf16[144,768]{1,0:T(8,128)(2,1)S(1)} collective-permute-done((bf16[144,768]{1,0:T(8,128)(2,1)S(1)}, bf16[144,768]{1,0:T(8,128)(2,1)S(1)}, u32[]{:S(2)}, u32[]{:S(2)}) %collective-permute-start) | collective-permute-done | bytes 221216 | tf_op jit(solution)/shard_map/ppermute | solution.py:547
  19.9 1.6 collective-permute-start.1
  22.4 1.9 collective-permute-done.3.refs_1_.refs_7_
  24.7 2.7 collective-permute-start.4
  27.8 9.4 %collective-permute-done.5 = bf16[192,768]{1,0:T(8,128)(2,1)S(1)} collective-permute-done((bf16[192,768]{1,0:T(8,128)(2,1)S(1)}, bf16[192,768]{1,0:T(8,128)(2,1)S(1)}, u32[]{:S(2)}, u32[]{:S(2)}) %collective-permute-start.5) | collective-permute-done | bytes 294944 | tf_op jit(solution)/shard_map/ppermute | solution.py:547
  38.7 1.9 collective-permute-start.8
  41.4 1.6 collective-permute-start.10
  42.9 1.6 collective-permute-start.9
  45.3 8.0 %attention_forward.2 = (bf16[512,768]{1,0:T(8,128)(2,1)S(1)}, f32[512,768]{1,0:T(8,128)S(1)}, bf16[9,1024,64]{2,1,0:T(8,128)(2,1)S(1)}, bf16[1024,192]{1,0:T(8,1...) custom-call(s32[1]{0:T(128)} %bitcast.refs_0_, ...), custom_call_target="tpu_custom_call" | custom-call | flops 1610612736 | bytes 8497412 | tf_op jit(solution)/shard_map/attention_forward/pallas_call | solution.py:840
  53.5 2.3 collective-permute-done.11
  56.8 1.6 collective-permute-start.13
  58.4 1.6 collective-permute-start.14
  60.0 1.5 collective-permute-start.15
  61.5 14.1 %collective-permute-done.12.across_ref = bf16[512,768]{1,0:T(8,128)(2,1)S(1)} collective-permute-done((bf16[512,768]{1,0:T(8,128)(2,1)S(1)}, bf16[512,768]{1,0:T(8,128)(2,1)S(1)}, u32[]{:S(2)}, u32[]{:S(2)}) %collective-permute-start.12) | collective-permute-done | bytes 786464 | tf_op jit(solution)/shard_map/ppermute | solution.py:547
  76.7 2.0 collective-permute-done.15
  79.6 2.3 collective-permute-done.16.refs_1_
  81.9 4.0 %feed_forward.2 = (bf16[512,768]{1,0:T(8,128)(2,1)S(1)}, f32[512,768]{1,0:T(8,128)S(1)}) custom-call(bf16[512,768]{1,0:T(8,128)(2,1)S(1)} %get-tuple-element.218.refs_0_, bf16[512,768]{1,0:T(8,128)(2,1)S(1)} %collective-permute-done.16.refs_1_, f32[1,768]{1,0:T(1,128)S(1)} %get-tuple-element.219.refs_2_.refs_4_, ...), custom_call_target="tpu_custom_call" | custom-call | flops 2415919104 | bytes 6294528 | tf_op jit(solution)/shard_map/feed_forward/pallas_call | solution.py:840
  86.1 2.1 collective-permute-done.17
  92.5 1.9 collective-permute-start.21
  94.4 13.7 %collective-permute-done.18.across_ref = bf16[512,768]{1,0:T(8,128)(2,1)S(1)} collective-permute-done((bf16[512,768]{1,0:T(8,128)(2,1)S(1)}, bf16[512,768]{1,0:T(8,128)(2,1)S(1)}, u32[]{:S(2)}, u32[]{:S(2)}) %collective-permute-start.18) | collective-permute-done | bytes 786464 | tf_op jit(solution)/shard_map/ppermute | solution.py:547
  111.4 2.5 collective-permute-start.23
  114.2 7.3 %attention_forward.3 = (bf16[512,768]{1,0:T(8,128)(2,1)S(1)}, f32[512,768]{1,0:T(8,128)S(1)}, bf16[9,1024,64]{2,1,0:T(8,128)(2,1)S(1)}, bf16[1024,192]{1,0:T(8,128)(2,1)S(1)}, f32[3,1,1024]{2,1,0:T(1,128)S(1)}) custom-call(s32[1]{0:T(128)} %bitcast.refs_0_, bf16[512,768]{1,0:T(8,128)(2,1)S(1)} %get-tuple-element.228.refs_1_, ...), custom_call_target="tpu_custom_call" | custom-call | flops 1610612736 | bytes 6703364 | tf_op jit(solution)/shard_map/attention_forward/pallas_call | solution.py:840
  121.5 2.5 collective-permute-done.24
  125.4 1.7 collective-permute-done.25
  128.7 1.9 collective-permute-start.28
  130.5 16.3 %collective-permute-done.26.across_ref = bf16[512,768]{1,0:T(8,128)(2,1)S(1)} collective-permute-done((bf16[512,768]{1,0:T(8,128)(2,1)S(1)}, bf16[512,768]{1,0:T(8,128)(2,1)S(1)}, u32[]{:S(2)}, u32[]{:S(2)}) %collective-permute-start.26) | collective-permute-done | bytes 786464 | tf_op jit(solution)/shard_map/ppermute | solution.py:547
  148.0 2.3 collective-permute-done.30.refs_1_
  150.3 5.3 %feed_backward.2 = (bf16[512,768]{1,0:T(8,128)(2,1)S(1)}, f32[512,768]{1,0:T(8,128)S(1)}, bf16[1024,768]{1,0:T(8,128)(2,1)S(1)}, bf16[1024,768]{1,0:T(8,128)(2,1)S(1)}, f32[1,768]{1,0:T(1,128)S(1)}) custom-call(bf16[512,768]{1,0:T(8,128)(2,1)S(1)} %get-tuple-element.255.refs_0_, bf16[512,768]{1,0:T(8,128)(2,1)S(1)} %collective-permute-done.30.refs_1_, ...), custom_call_target="tpu_custom_call" | custom-call | flops 3623878656 | bytes 11016192 | tf_op jit(solution)/shard_map/feed_backward/pallas_call | solution.py:840
  161.1 1.8 collective-permute-start.33
  162.9 4.0 %feed_forward.3 = (bf16[512,768]{1,0:T(8,128)(2,1)S(1)}, f32[512,768]{1,0:T(8,128)S(1)}) custom-call(bf16[512,768]{1,0:T(8,128)(2,1)S(1)} %get-tuple-element.255.refs_0_, bf16[512,768]{1,0:T(8,128)(2,1)S(1)} %collective-permute-done.30.refs_1_, f32[1,768]{1,0:T(1,128)S(1)} %get-tuple-element.243.refs_4_.refs_2_, ...), custom_call_target="tpu_custom_call" | custom-call | flops 2415919104 | bytes 6294528 | tf_op jit(solution)/shard_map/feed_forward/pallas_call | solution.py:840
  166.9 10.9 %collective-permute-done.32.across_ref = bf16[512,768]{1,0:T(8,128)(2,1)S(1)} collective-permute-done((bf16[512,768]{1,0:T(8,128)(2,1)S(1)}, bf16[512,768]{1,0:T(8,128)(2,1)S(1)}, u32[]{:S(2)}, u32[]{:S(2)}) %collective-permute-start.32) | collective-permute-done | bytes 786464 | tf_op jit(solution)/shard_map/ppermute | solution.py:547
  177.8 1.5 norm_back_near.3
  179.7 1.7 collective-permute-start.36
  181.8 10.0 %attention_backward.2 = (bf16[512,768]{1,0:T(8,128)(2,1)S(1)}, f32[512,768]{1,0:T(8,128)S(1)}, bf16[1024,576]{1,0:T(8,128)(2,1)S(1)}, f32[1,576]{1,0:T(1,128)S(1)}) custom-call(s32[1]{0:T(128)} %bitcast.refs_0_, bf16[512,768]{1,0:T(8,128)(2,1)S(1)} %get-tuple-element.258.refs_1_, bf16[512,768]{1,0:T(8,128)(2,1)S(1)} %collective-permute-done.35.refs_2_, ...), custom_call_target="tpu_custom_call" | custom-call | flops 4026531840 | bytes 7489796 | tf_op jit(solution)/shard_map/attention_backward/pallas_call | solution.py:840
  195.9 2.7 collective-permute-start.40
  199.1 15.0 %collective-permute-done.38.across_ref = bf16[512,768]{1,0:T(8,128)(2,1)S(1)} collective-permute-done((bf16[512,768]{1,0:T(8,128)(2,1)S(1)}, bf16[512,768]{1,0:T(8,128)(2,1)S(1)}, u32[]{:S(2)}, u32[]{:S(2)}) %collective-permute-start.38) | collective-permute-done | bytes 786464 | tf_op jit(solution)/shard_map/ppermute | solution.py:547
  215.6 2.6 collective-permute-done.39
  218.2 2.3 collective-permute-done.42.refs_3_
  220.5 5.1 %feed_backward.3 = (bf16[512,768]{1,0:T(8,128)(2,1)S(1)}, f32[512,768]{1,0:T(8,128)S(1)}, bf16[1024,768]{1,0:T(8,128)(2,1)S(1)}, bf16[1024,768]{1,0:T(8,128)(2,1)S(1)}, f32[1,768]{1,0:T(1,128)S(1)}) custom-call(bf16[512,768]{1,0:T(8,128)(2,1)S(1)} %get-tuple-element.218.refs_0_, bf16[512,768]{1,0:T(8,128)(2,1)S(1)} %collective-permute-done.16.refs_1_, ...), custom_call_target="tpu_custom_call" | custom-call | flops 3623878656 | bytes 11016192 | tf_op jit(solution)/shard_map/feed_backward/pallas_call | solution.py:840
  231.1 1.6 collective-permute-start.47
  233.0 2.1 collective-permute-start.45
  235.1 12.7 %collective-permute-done.44.across_ref = bf16[512,768]{1,0:T(8,128)(2,1)S(1)} collective-permute-done((bf16[512,768]{1,0:T(8,128)(2,1)S(1)}, bf16[512,768]{1,0:T(8,128)(2,1)S(1)}, u32[]{:S(2)}, u32[]{:S(2)}) %collective-permute-start.44) | collective-permute-done | bytes 786464 | tf_op jit(solution)/shard_map/ppermute | solution.py:547
  247.8 1.7 norm_back_near.5
  249.6 4.4 %collective-permute-done.45 = bf16[384,384]{1,0:T(8,128)(2,1)S(1)} collective-permute-done((bf16[384,384]{1,0:T(8,128)(2,1)S(1)}, bf16[384,384]{1,0:T(8,128)(2,1)S(1)}, u32[]{:S(2)}, u32[]{:S(2)}) %collective-permute-start.45) | collective-permute-done | bytes 294944 | tf_op jit(solution)/shard_map/ppermute | solution.py:547
  255.4 1.8 collective-permute-start.51
  258.0 9.6 %attention_backward.3 = (bf16[512,768]{1,0:T(8,128)(2,1)S(1)}, f32[512,768]{1,0:T(8,128)S(1)}, bf16[1024,576]{1,0:T(8,128)(2,1)S(1)}, f32[1,576]{1,0:T(1,128)S(1)}) custom-call(s32[1]{0:T(128)} %bitcast.refs_0_, bf16[512,768]{1,0:T(8,128)(2,1)S(1)} %get-tuple-element.285.refs_1_, bf16[512,768]{1,0:T(8,128)(2,1)S(1)} %collective-permute-done.48.refs_2_, ...), custom_call_target="tpu_custom_call" | custom-call | flops 4026531840 | bytes 7686404 | tf_op jit(solution)/shard_map/attention_backward/pallas_call | solution.py:840
  267.7 1.6 collective-permute-done.52.theirs_ref
  273.7 2.6 collective-permute-start.58
  276.3 1.6 finish_feed.2
  278.0 5.7 %collective-permute-done.54.refs_6_ = bf16[256,768]{1,0:T(8,128)(2,1)S(1)} collective-permute-done((bf16[256,768]{1,0:T(8,128)(2,1)S(1)}, bf16[256,768]{1,0:T(8,128)(2,1)S(1)}, u32[]{:S(2)}, u32[]{:S(2)}) %collective-permute-start.54) | collective-permute-done | bytes 393248 | tf_op jit(solution)/shard_map/ppermute | solution.py:547
  289.8 5.8 %collective-permute-done.58 = bf16[192,768]{1,0:T(8,128)(2,1)S(1)} collective-permute-done((bf16[192,768]{1,0:T(8,128)(2,1)S(1)}, bf16[192,768]{1,0:T(8,128)(2,1)S(1)}, u32[]{:S(2)}, u32[]{:S(2)}) %collective-permute-start.58) | collective-permute-done | bytes 294944 | tf_op jit(solution)/shard_map/ppermute | solution.py:547
  298.1 1.5 collective-permute-start.64
  301.8 6.0 %collective-permute-done.62 = bf16[256,768]{1,0:T(8,128)(2,1)S(1)} collective-permute-done((bf16[256,768]{1,0:T(8,128)(2,1)S(1)}, bf16[256,768]{1,0:T(8,128)(2,1)S(1)}, u32[]{:S(2)}, u32[]{:S(2)}) %collective-permute-start.62) | collective-permute-done | bytes 393248 | tf_op jit(solution)/shard_map/ppermute | solution.py:547
  308.7 7.0 %collective-permute-done.63 = bf16[192,384]{1,0:T(8,128)(2,1)S(1)} collective-permute-done((bf16[192,384]{1,0:T(8,128)(2,1)S(1)}, bf16[192,384]{1,0:T(8,128)(2,1)S(1)}, u32[]{:S(2)}, u32[]{:S(2)}) %collective-permute-start.63) | collective-permute-done | bytes 147488 | tf_op jit(solution)/shard_map/ppermute | solution.py:547
  315.7 1.6 collective-permute-start.65
  318.7 1.6 finish_attend.2
  320.4 1.6 finish_feed.3
  322.6 1.7 collective-permute-start.69
  324.3 1.6 collective-permute-done.66
  326.0 1.6 finish_attend.3
  (223 shorter events, 64.1 us)
Async XLA Ops:
  3.1 24.7 %collective-permute-start.2 = (bf16[224,768]{1,0:T(8,128)(2,1)}, bf16[224,768]{1,0:T(8,128)(2,1)S(1)}, u32[]{:S(2)}, u32[]{:S(2)}) collective-permute-start(bf16[224,768]{1,0:T(8,128)(2,1)} %prepare_first.1.refs_0_.refs_6_), channel_id=1, source_target_pairs={{0,8},{8,0},{16,24},{24,16},{1,9},{9,1},{17,25},{25,17},{2,10},{10... | collective-permute-start | bytes 1032200 | tf_op jit(solution)/shard_map/ppermute | solution.py:547
  6.2 18.1 %collective-permute-start.3 = (bf16[224,768]{1,0:T(8,128)(2,1)}, bf16[224,768]{1,0:T(8,128)(2,1)S(1)}, u32[]{:S(2)}, u32[]{:S(2)}) collective-permute-start(bf16[224,768]{1,0:T(8,128)(2,1)} %prepare_first.1.refs_0_.refs_6_), channel_id=1, source_target_pairs={{0,16},{8,24},{16,0},{24,8},{1,17},{9,25},{17,1},{25,9},{2,18},{10... | collective-permute-start | bytes 1032200 | tf_op jit(solution)/shard_map/ppermute | solution.py:547
  10.6 8.4 %collective-permute-start = (bf16[144,768]{1,0:T(8,128)(2,1)S(1)}, bf16[144,768]{1,0:T(8,128)(2,1)S(1)}, u32[]{:S(2)}, u32[]{:S(2)}) collective-permute-start(bf16[144,768]{1,0:T(8,128)(2,1)S(1)} %fusion.83), channel_id=1, source_target_pairs={{0,4},{4,0},{1,5},{5,1},{2,6},{6,2},{3,7},{7,3},{8,12},{12,8},{9,1... | collective-permute-start | bytes 663560 | tf_op jit(solution)/shard_map/ppermute | solution.py:547
  12.2 15.6 %collective-permute-start.6 = (bf16[128,768]{1,0:T(8,128)(2,1)S(1)}, bf16[128,768]{1,0:T(8,128)(2,1)S(1)}, u32[]{:S(2)}, u32[]{:S(2)}) collective-permute-start(bf16[128,768]{1,0:T(8,128)(2,1)S(1)} %get-tuple-element.371), channel_id=1, source_target_pairs={{0,4},{4,0},{1,5},{5,1},{2,6},{6,2},{3,7},{7,3},{8,12},{12,8},{9,1... | collective-permute-start | bytes 589832 | tf_op jit(solution)/shard_map/ppermute | solution.py:547
  19.9 7.8 %collective-permute-start.1 = (bf16[256,768]{1,0:T(8,128)(2,1)S(1)}, bf16[256,768]{1,0:T(8,128)(2,1)S(1)}, u32[]{:S(2)}, u32[]{:S(2)}) collective-permute-start(bf16[256,768]{1,0:T(8,128)(2,1)S(1)} %convolution_convert_fusion.2), channel_id=1, source_target_pairs={{0,2},{1,3},{2,0},{3,1},{4,6},{5,7},{6,4},{7,5},{8,10},{9,11},{10,... | collective-permute-start | bytes 1179656 | tf_op jit(solution)/shard_map/ppermute | solution.py:547
  24.3 12.9 %collective-permute-start.5 = (bf16[192,768]{1,0:T(8,128)(2,1)S(1)}, bf16[192,768]{1,0:T(8,128)(2,1)S(1)}, u32[]{:S(2)}, u32[]{:S(2)}) collective-permute-start(bf16[192,768]{1,0:T(8,128)(2,1)S(1)} %get-tuple-element.365), channel_id=1, source_target_pairs={{0,16},{8,24},{16,0},{24,8},{1,17},{9,25},{17,1},{25,9},{2,18},{10... | collective-permute-start | bytes 884744 | tf_op jit(solution)/shard_map/ppermute | solution.py:547
  24.7 13.5 %collective-permute-start.4 = (bf16[224,768]{1,0:T(8,128)(2,1)S(1)}, bf16[224,768]{1,0:T(8,128)(2,1)S(1)}, u32[]{:S(2)}, u32[]{:S(2)}) collective-permute-start(bf16[224,768]{1,0:T(8,128)(2,1)S(1)} %collective-permute-done.3.refs_1_.refs_7_), channel_id=1, source_target_pairs={{0,8},{8,0},{16,24},{24,16},{1,9},{9,1},{17,25},{25,17},{2,10},{10... | collective-permute-start | bytes 1032200 | tf_op jit(solution)/shard_map/ppermute | solution.py:547
  38.6 6.8 %collective-permute-start.7 = (bf16[512,768]{1,0:T(8,128)(2,1)S(1)}, bf16[512,768]{1,0:T(8,128)(2,1)S(1)}, u32[]{:S(2)}, u32[]{:S(2)}) collective-permute-start(bf16[512,768]{1,0:T(8,128)(2,1)S(1)} %norm_only.1.refs_1_), channel_id=1, source_target_pairs={{0,1},{1,0},{2,3},{3,2},{4,5},{5,4},{6,7},{7,6},{8,9},{9,8},{10,11... | collective-permute-start | bytes 2359304 | tf_op jit(solution)/shard_map/ppermute | solution.py:547
  38.7 14.6 %collective-permute-start.8 = (bf16[384,384]{1,0:T(8,128)(2,1)S(1)}, bf16[384,384]{1,0:T(8,128)(2,1)S(1)}, u32[]{:S(2)}, u32[]{:S(2)}) collective-permute-start(bf16[384,384]{1,0:T(8,128)(2,1)S(1)} %pad_maximum_fusion.10), channel_id=1, source_target_pairs={{0,8},{8,0},{16,24},{24,16},{1,9},{9,1},{17,25},{25,17},{2,10},{10... | collective-permute-start | bytes 884744 | tf_op jit(solution)/shard_map/ppermute | solution.py:547
  41.4 12.0 %collective-permute-start.10 = (bf16[256,768]{1,0:T(8,128)(2,1)S(1)}, bf16[256,768]{1,0:T(8,128)(2,1)S(1)}, u32[]{:S(2)}, u32[]{:S(2)}) collective-permute-start(bf16[256,768]{1,0:T(8,128)(2,1)S(1)} %convolution_convert_fusion.1), channel_id=1, source_target_pairs={{0,2},{1,3},{2,0},{3,1},{4,6},{5,7},{6,4},{7,5},{8,10},{9,11},{10,... | collective-permute-start | bytes 1179656 | tf_op jit(solution)/shard_map/ppermute | solution.py:547
  42.9 10.4 %collective-permute-start.9 = (bf16[192,384]{1,0:T(8,128)(2,1)S(1)}, bf16[192,384]{1,0:T(8,128)(2,1)S(1)}, u32[]{:S(2)}, u32[]{:S(2)}) collective-permute-start(bf16[192,384]{1,0:T(8,128)(2,1)S(1)} %get-tuple-element.366), channel_id=1, source_target_pairs={{0,16},{8,24},{16,0},{24,8},{1,17},{9,25},{17,1},{25,9},{2,18},{10... | collective-permute-start | bytes 442376 | tf_op jit(solution)/shard_map/ppermute | solution.py:547
  53.4 2.4 collective-permute-start.11
  56.0 19.6 %collective-permute-start.12 = (bf16[512,768]{1,0:T(8,128)(2,1)S(1)}, bf16[512,768]{1,0:T(8,128)(2,1)S(1)}, u32[]{:S(2)}, u32[]{:S(2)}) collective-permute-start(bf16[512,768]{1,0:T(8,128)(2,1)S(1)} %add_convert_fusion.5.partial_ref), channel_id=1, source_target_pairs={{0,2},{1,3},{2,0},{3,1},{4,6},{5,7},{6,4},{7,5},{8,10},{9,11},{10,... | collective-permute-start | bytes 2359304 | tf_op jit(solution)/shard_map/ppermute | solution.py:547
  56.8 21.9 %collective-permute-start.13 = (bf16[768,384]{1,0:T(8,128)(2,1)S(1)}, bf16[768,384]{1,0:T(8,128)(2,1)S(1)}, u32[]{:S(2)}, u32[]{:S(2)}) collective-permute-start(bf16[768,384]{1,0:T(8,128)(2,1)S(1)} %pad_maximum_fusion.4.refs_3_.refs_5_), channel_id=1, source_target_pairs={{0,4},{4,0},{1,5},{5,1},{2,6},{6,2},{3,7},{7,3},{8,12},{12,8},{9,1... | collective-permute-start | bytes 1769480 | tf_op jit(solution)/shard_map/ppermute | solution.py:547
  58.4 21.2 %collective-permute-start.14 = (bf16[384,768]{1,0:T(8,128)(2,1)S(1)}, bf16[384,768]{1,0:T(8,128)(2,1)S(1)}, u32[]{:S(2)}, u32[]{:S(2)}) collective-permute-start(bf16[384,768]{1,0:T(8,128)(2,1)S(1)} %maximum_maximum_fusion.refs_5_.refs_7_), channel_id=1, source_target_pairs={{0,8},{8,0},{16,24},{24,16},{1,9},{9,1},{17,25},{25,17},{2,10},{10... | collective-permute-start | bytes 1769480 | tf_op jit(solution)/shard_map/ppermute | solution.py:547
  60.0 18.6 %collective-permute-start.15 = (bf16[192,768]{1,0:T(8,128)(2,1)S(1)}, bf16[192,768]{1,0:T(8,128)(2,1)S(1)}, u32[]{:S(2)}, u32[]{:S(2)}) collective-permute-start(bf16[192,768]{1,0:T(8,128)(2,1)S(1)} %prepare_attend.1), channel_id=1, source_target_pairs={{0,16},{8,24},{16,0},{24,8},{1,17},{9,25},{17,1},{25,9},{2,18},{10... | collective-permute-start | bytes 884744 | tf_op jit(solution)/shard_map/ppermute | solution.py:547
  88.4 19.6 %collective-permute-start.18 = (bf16[512,768]{1,0:T(8,128)(2,1)S(1)}, bf16[512,768]{1,0:T(8,128)(2,1)S(1)}, u32[]{:S(2)}, u32[]{:S(2)}) collective-permute-start(bf16[512,768]{1,0:T(8,128)(2,1)S(1)} %add_convert_fusion.4.partial_ref), channel_id=1, source_target_pairs={{0,2},{1,3},{2,0},{3,1},{4,6},{5,7},{6,4},{7,5},{8,10},{9,11},{10,... | collective-permute-start | bytes 2359304 | tf_op jit(solution)/shard_map/ppermute | solution.py:547
  89.8 21.5 %collective-permute-start.19 = (bf16[384,768]{1,0:T(8,128)(2,1)S(1)}, bf16[384,768]{1,0:T(8,128)(2,1)S(1)}, u32[]{:S(2)}, u32[]{:S(2)}) collective-permute-start(bf16[384,768]{1,0:T(8,128)(2,1)S(1)} %constant_dynamic-update-slice_fusion.refs_5_.refs_6_), channel_id=1, source_target_pairs={{0,8},{8,0},{16,24},{24,16},{1,9},{9,1},{17,25},{25,17},{2,10},{10... | collective-permute-start | bytes 1769480 | tf_op jit(solution)/shard_map/ppermute | solution.py:547
  91.4 17.7 %collective-permute-start.20 = (bf16[192,384]{1,0:T(8,128)(2,1)S(1)}, bf16[192,384]{1,0:T(8,128)(2,1)S(1)}, u32[]{:S(2)}, u32[]{:S(2)}) collective-permute-start(bf16[192,384]{1,0:T(8,128)(2,1)S(1)} %get-tuple-element.363), channel_id=1, source_target_pairs={{0,16},{8,24},{16,0},{24,8},{1,17},{9,25},{17,1},{25,9},{2,18},{10... | collective-permute-start | bytes 442376 | tf_op jit(solution)/shard_map/ppermute | solution.py:547
  92.5 17.8 %collective-permute-start.21 = (bf16[192,384]{1,0:T(8,128)(2,1)S(1)}, bf16[192,384]{1,0:T(8,128)(2,1)S(1)}, u32[]{:S(2)}, u32[]{:S(2)}) collective-permute-start(bf16[192,384]{1,0:T(8,128)(2,1)S(1)} %get-tuple-element.362), channel_id=1, source_target_pairs={{0,16},{8,24},{16,0},{24,8},{1,17},{9,25},{17,1},{25,9},{2,18},{10... | collective-permute-start | bytes 442376 | tf_op jit(solution)/shard_map/ppermute | solution.py:547
  111.3 2.9 collective-permute-start.22
  111.4 13.3 %collective-permute-start.23 = (bf16[384,384]{1,0:T(8,128)(2,1)S(1)}, bf16[384,384]{1,0:T(8,128)(2,1)S(1)}, u32[]{:S(2)}, u32[]{:S(2)}) collective-permute-start(bf16[384,384]{1,0:T(8,128)(2,1)S(1)} %pad_maximum_fusion.11), channel_id=1, source_target_pairs={{0,8},{8,0},{16,24},{24,16},{1,9},{9,1},{17,25},{25,17},{2,10},{10... | collective-permute-start | bytes 884744 | tf_op jit(solution)/shard_map/ppermute | solution.py:547
  113.9 10.1 %collective-permute-start.24 = (bf16[192,384]{1,0:T(8,128)(2,1)S(1)}, bf16[192,384]{1,0:T(8,128)(2,1)S(1)}, u32[]{:S(2)}, u32[]{:S(2)}) collective-permute-start(bf16[192,384]{1,0:T(8,128)(2,1)S(1)} %get-tuple-element.360), channel_id=1, source_target_pairs={{0,16},{8,24},{16,0},{24,8},{1,17},{9,25},{17,1},{25,9},{2,18},{10... | collective-permute-start | bytes 442376 | tf_op jit(solution)/shard_map/ppermute | solution.py:547
  124.8 23.1 %collective-permute-start.29 = (bf16[512,768]{1,0:T(8,128)(2,1)S(1)}, bf16[512,768]{1,0:T(8,128)(2,1)S(1)}, u32[]{:S(2)}, u32[]{:S(2)}) collective-permute-start(bf16[512,768]{1,0:T(8,128)(2,1)S(1)} %pad_maximum_fusion.1.refs_2_.skip_ref), channel_id=1, source_target_pairs={{0,1},{1,0},{2,3},{3,2},{4,5},{5,4},{6,7},{7,6},{8,9},{9,8},{10,11... | collective-permute-start | bytes 2359304 | tf_op jit(solution)/shard_map/ppermute | solution.py:547
  127.2 19.6 %collective-permute-start.26 = (bf16[512,768]{1,0:T(8,128)(2,1)S(1)}, bf16[512,768]{1,0:T(8,128)(2,1)S(1)}, u32[]{:S(2)}, u32[]{:S(2)}) collective-permute-start(bf16[512,768]{1,0:T(8,128)(2,1)S(1)} %add_convert_fusion.3.partial_ref), channel_id=1, source_target_pairs={{0,2},{1,3},{2,0},{3,1},{4,6},{5,7},{6,4},{7,5},{8,10},{9,11},{10,... | collective-permute-start | bytes 2359304 | tf_op jit(solution)/shard_map/ppermute | solution.py:547
  128.1 19.9 %collective-permute-start.27 = (bf16[768,384]{1,0:T(8,128)(2,1)S(1)}, bf16[768,384]{1,0:T(8,128)(2,1)S(1)}, u32[]{:S(2)}, u32[]{:S(2)}) collective-permute-start(bf16[768,384]{1,0:T(8,128)(2,1)S(1)} %pad_maximum_fusion.5.refs_5_.refs_3_), channel_id=1, source_target_pairs={{0,4},{4,0},{1,5},{5,1},{2,6},{6,2},{3,7},{7,3},{8,12},{12,8},{9,1... | collective-permute-start | bytes 1769480 | tf_op jit(solution)/shard_map/ppermute | solution.py:547
  128.7 19.2 %collective-permute-start.28 = (bf16[384,768]{1,0:T(8,128)(2,1)S(1)}, bf16[384,768]{1,0:T(8,128)(2,1)S(1)}, u32[]{:S(2)}, u32[]{:S(2)}) collective-permute-start(bf16[384,768]{1,0:T(8,128)(2,1)S(1)} %maximum_maximum_fusion.1.refs_7_.refs_5_), channel_id=1, source_target_pairs={{0,8},{8,0},{16,24},{24,16},{1,9},{9,1},{17,25},{25,17},{2,10},{10... | collective-permute-start | bytes 1769480 | tf_op jit(solution)/shard_map/ppermute | solution.py:547
  148.0 2.4 collective-permute-start.30
  158.2 19.6 %collective-permute-start.32 = (bf16[512,768]{1,0:T(8,128)(2,1)S(1)}, bf16[512,768]{1,0:T(8,128)(2,1)S(1)}, u32[]{:S(2)}, u32[]{:S(2)}) collective-permute-start(bf16[512,768]{1,0:T(8,128)(2,1)S(1)} %add_convert_fusion.2.partial_ref), channel_id=1, source_target_pairs={{0,2},{1,3},{2,0},{3,1},{4,6},{5,7},{6,4},{7,5},{8,10},{9,11},{10,... | collective-permute-start | bytes 2359304 | tf_op jit(solution)/shard_map/ppermute | solution.py:547
  160.5 18.9 %collective-permute-start.34 = (bf16[768,384]{1,0:T(8,128)(2,1)S(1)}, bf16[768,384]{1,0:T(8,128)(2,1)S(1)}, u32[]{:S(2)}, u32[]{:S(2)}) collective-permute-start(bf16[768,384]{1,0:T(8,128)(2,1)S(1)} %slice.339), channel_id=1, source_target_pairs={{0,4},{4,0},{1,5},{5,1},{2,6},{6,2},{3,7},{7,3},{8,12},{12,8},{9,1... | collective-permute-start | bytes 1769480 | tf_op jit(solution)/shard_map/ppermute | solution.py:547
  161.1 18.3 %collective-permute-start.33 = (bf16[384,768]{1,0:T(8,128)(2,1)S(1)}, bf16[384,768]{1,0:T(8,128)(2,1)S(1)}, u32[]{:S(2)}, u32[]{:S(2)}) collective-permute-start(bf16[384,768]{1,0:T(8,128)(2,1)S(1)} %slice.278), channel_id=1, source_target_pairs={{0,8},{8,0},{16,24},{24,16},{1,9},{9,1},{17,25},{25,17},{2,10},{10... | collective-permute-start | bytes 1769480 | tf_op jit(solution)/shard_map/ppermute | solution.py:547
  179.4 2.4 collective-permute-start.35
  179.7 12.1 %collective-permute-start.36 = (bf16[384,384]{1,0:T(8,128)(2,1)S(1)}, bf16[384,384]{1,0:T(8,128)(2,1)S(1)}, u32[]{:S(2)}, u32[]{:S(2)}) collective-permute-start(bf16[384,384]{1,0:T(8,128)(2,1)S(1)} %slice.448), channel_id=1, source_target_pairs={{0,8},{8,0},{16,24},{24,16},{1,9},{9,1},{17,25},{25,17},{2,10},{10... | collective-permute-start | bytes 884744 | tf_op jit(solution)/shard_map/ppermute | solution.py:547
  194.3 19.8 %collective-permute-start.38 = (bf16[512,768]{1,0:T(8,128)(2,1)S(1)}, bf16[512,768]{1,0:T(8,128)(2,1)S(1)}, u32[]{:S(2)}, u32[]{:S(2)}) collective-permute-start(bf16[512,768]{1,0:T(8,128)(2,1)S(1)} %add_convert_fusion.1.partial_ref), channel_id=1, source_target_pairs={{0,2},{1,3},{2,0},{3,1},{4,6},{5,7},{6,4},{7,5},{8,10},{9,11},{10,... | collective-permute-start | bytes 2359304 | tf_op jit(solution)/shard_map/ppermute | solution.py:547
  195.3 22.9 %collective-permute-start.41 = (bf16[768,384]{1,0:T(8,128)(2,1)S(1)}, bf16[768,384]{1,0:T(8,128)(2,1)S(1)}, u32[]{:S(2)}, u32[]{:S(2)}) collective-permute-start(bf16[768,384]{1,0:T(8,128)(2,1)S(1)} %broadcast_select_fusion.1), channel_id=1, source_target_pairs={{0,4},{4,0},{1,5},{5,1},{2,6},{6,2},{3,7},{7,3},{8,12},{12,8},{9,1... | collective-permute-start | bytes 1769480 | tf_op jit(solution)/shard_map/ppermute | solution.py:547
  195.9 22.3 %collective-permute-start.40 = (bf16[192,768]{1,0:T(8,128)(2,1)S(1)}, bf16[192,768]{1,0:T(8,128)(2,1)S(1)}, u32[]{:S(2)}, u32[]{:S(2)}) collective-permute-start(bf16[192,768]{1,0:T(8,128)(2,1)S(1)} %slice.447), channel_id=1, source_target_pairs={{0,16},{8,24},{16,0},{24,8},{1,17},{9,25},{17,1},{25,9},{2,18},{10... | collective-permute-start | bytes 884744 | tf_op jit(solution)/shard_map/ppermute | solution.py:547
  198.7 19.5 %collective-permute-start.39 = (bf16[192,384]{1,0:T(8,128)(2,1)S(1)}, bf16[192,384]{1,0:T(8,128)(2,1)S(1)}, u32[]{:S(2)}, u32[]{:S(2)}) collective-permute-start(bf16[192,384]{1,0:T(8,128)(2,1)S(1)} %slice.452), channel_id=1, source_target_pairs={{0,16},{8,24},{16,0},{24,8},{1,17},{9,25},{17,1},{25,9},{2,18},{10... | collective-permute-start | bytes 442376 | tf_op jit(solution)/shard_map/ppermute | solution.py:547
  225.6 2.4 collective-permute-start.43
  228.2 19.6 %collective-permute-start.44 = (bf16[512,768]{1,0:T(8,128)(2,1)S(1)}, bf16[512,768]{1,0:T(8,128)(2,1)S(1)}, u32[]{:S(2)}, u32[]{:S(2)}) collective-permute-start(bf16[512,768]{1,0:T(8,128)(2,1)S(1)} %add_convert_fusion.partial_ref), channel_id=1, source_target_pairs={{0,2},{1,3},{2,0},{3,1},{4,6},{5,7},{6,4},{7,5},{8,10},{9,11},{10,... | collective-permute-start | bytes 2359304 | tf_op jit(solution)/shard_map/ppermute | solution.py:547
  231.1 18.4 %collective-permute-start.47 = (bf16[768,384]{1,0:T(8,128)(2,1)S(1)}, bf16[768,384]{1,0:T(8,128)(2,1)S(1)}, u32[]{:S(2)}, u32[]{:S(2)}) collective-permute-start(bf16[768,384]{1,0:T(8,128)(2,1)S(1)} %slice.347), channel_id=1, source_target_pairs={{0,4},{4,0},{1,5},{5,1},{2,6},{6,2},{3,7},{7,3},{8,12},{12,8},{9,1... | collective-permute-start | bytes 1769480 | tf_op jit(solution)/shard_map/ppermute | solution.py:547
  232.8 21.2 %collective-permute-start.46 = (bf16[384,768]{1,0:T(8,128)(2,1)S(1)}, bf16[384,768]{1,0:T(8,128)(2,1)S(1)}, u32[]{:S(2)}, u32[]{:S(2)}) collective-permute-start(bf16[384,768]{1,0:T(8,128)(2,1)S(1)} %slice.289), channel_id=1, source_target_pairs={{0,8},{8,0},{16,24},{24,16},{1,9},{9,1},{17,25},{25,17},{2,10},{10... | collective-permute-start | bytes 1769480 | tf_op jit(solution)/shard_map/ppermute | solution.py:547
  232.9 56.6 %collective-permute-start.60 = (bf16[512,768]{1,0:T(8,128)(2,1)S(1)}, bf16[512,768]{1,0:T(8,128)(2,1)S(1)}, u32[]{:S(2)}, u32[]{:S(2)}) collective-permute-start(bf16[512,768]{1,0:T(8,128)(2,1)S(1)} %get-tuple-element.307), channel_id=1, source_target_pairs={{0,1},{1,0},{2,3},{3,2},{4,5},{5,4},{6,7},{7,6},{8,9},{9,8},{10,11... | collective-permute-start | bytes 2359304 | tf_op jit(solution)/shard_map/ppermute | solution.py:547
  233.0 21.0 %collective-permute-start.45 = (bf16[384,384]{1,0:T(8,128)(2,1)S(1)}, bf16[384,384]{1,0:T(8,128)(2,1)S(1)}, u32[]{:S(2)}, u32[]{:S(2)}) collective-permute-start(bf16[384,384]{1,0:T(8,128)(2,1)S(1)} %slice.446), channel_id=1, source_target_pairs={{0,8},{8,0},{16,24},{24,16},{1,9},{9,1},{17,25},{25,17},{2,10},{10... | collective-permute-start | bytes 884744 | tf_op jit(solution)/shard_map/ppermute | solution.py:547
  253.9 4.1 %collective-permute-start.48 = (bf16[512,768]{1,0:T(8,128)(2,1)S(1)}, bf16[512,768]{1,0:T(8,128)(2,1)S(1)}, u32[]{:S(2)}, u32[]{:S(2)}) collective-permute-start(bf16[512,768]{1,0:T(8,128)(2,1)S(1)} %get-tuple-element.285.refs_1_), channel_id=1, source_target_pairs={{0,1},{1,0},{2,3},{3,2},{4,5},{5,4},{6,7},{7,6},{8,9},{9,8},{10,11... | collective-permute-start | bytes 2359304 | tf_op jit(solution)/shard_map/ppermute | solution.py:547
  254.0 13.5 %collective-permute-start.50 = (bf16[192,384]{1,0:T(8,128)(2,1)S(1)}, bf16[192,384]{1,0:T(8,128)(2,1)S(1)}, u32[]{:S(2)}, u32[]{:S(2)}) collective-permute-start(bf16[192,384]{1,0:T(8,128)(2,1)S(1)} %slice.451), channel_id=1, source_target_pairs={{0,16},{8,24},{16,0},{24,8},{1,17},{9,25},{17,1},{25,9},{2,18},{10... | collective-permute-start | bytes 442376 | tf_op jit(solution)/shard_map/ppermute | solution.py:547
  255.4 12.4 %collective-permute-start.51 = (bf16[384,384]{1,0:T(8,128)(2,1)S(1)}, bf16[384,384]{1,0:T(8,128)(2,1)S(1)}, u32[]{:S(2)}, u32[]{:S(2)}) collective-permute-start(bf16[384,384]{1,0:T(8,128)(2,1)S(1)} %slice.445), channel_id=1, source_target_pairs={{0,8},{8,0},{16,24},{24,16},{1,9},{9,1},{17,25},{25,17},{2,10},{10... | collective-permute-start | bytes 884744 | tf_op jit(solution)/shard_map/ppermute | solution.py:547
  257.3 12.1 %collective-permute-start.52 = (bf16[192,1152]{1,0:T(8,128)(2,1)S(1)}, bf16[192,1152]{1,0:T(8,128)(2,1)S(1)}, u32[]{:S(2)}, u32[]{:S(2)}) collective-permute-start(bf16[192,1152]{1,0:T(8,128)(2,1)S(1)} %get-tuple-element.379), channel_id=1, source_target_pairs={{0,4},{4,0},{1,5},{5,1},{2,6},{6,2},{3,7},{7,3},{8,12},{12,8},{9,1... | collective-permute-start | bytes 1327112 | tf_op jit(solution)/shard_map/ppermute | solution.py:547
  269.4 2.9 collective-permute-start.53
  271.7 15.8 %collective-permute-start.49 = (bf16[768,384]{1,0:T(8,128)(2,1)S(1)}, bf16[768,384]{1,0:T(8,128)(2,1)S(1)}, u32[]{:S(2)}, u32[]{:S(2)}) collective-permute-start(bf16[768,384]{1,0:T(8,128)(2,1)S(1)} %broadcast_select_fusion), channel_id=1, source_target_pairs={{0,4},{4,0},{1,5},{5,1},{2,6},{6,2},{3,7},{7,3},{8,12},{12,8},{9,1... | collective-permute-start | bytes 1769480 | tf_op jit(solution)/shard_map/ppermute | solution.py:547
  272.4 11.3 %collective-permute-start.54 = (bf16[256,768]{1,0:T(8,128)(2,1)S(1)}, bf16[256,768]{1,0:T(8,128)(2,1)S(1)}, u32[]{:S(2)}, u32[]{:S(2)}) collective-permute-start(bf16[256,768]{1,0:T(8,128)(2,1)S(1)} %add_convert_fusion.8), channel_id=1, source_target_pairs={{0,2},{1,3},{2,0},{3,1},{4,6},{5,7},{6,4},{7,5},{8,10},{9,11},{10,... | collective-permute-start | bytes 1179656 | tf_op jit(solution)/shard_map/ppermute | solution.py:547
  273.3 16.5 %collective-permute-start.57 = (bf16[192,384]{1,0:T(8,128)(2,1)S(1)}, bf16[192,384]{1,0:T(8,128)(2,1)S(1)}, u32[]{:S(2)}, u32[]{:S(2)}) collective-permute-start(bf16[192,384]{1,0:T(8,128)(2,1)S(1)} %slice.450), channel_id=1, source_target_pairs={{0,16},{8,24},{16,0},{24,8},{1,17},{9,25},{17,1},{25,9},{2,18},{10... | collective-permute-start | bytes 442376 | tf_op jit(solution)/shard_map/ppermute | solution.py:547
  273.7 21.8 %collective-permute-start.58 = (bf16[192,768]{1,0:T(8,128)(2,1)S(1)}, bf16[192,768]{1,0:T(8,128)(2,1)S(1)}, u32[]{:S(2)}, u32[]{:S(2)}) collective-permute-start(bf16[192,768]{1,0:T(8,128)(2,1)S(1)} %slice.443), channel_id=1, source_target_pairs={{0,16},{8,24},{16,0},{24,8},{1,17},{9,25},{17,1},{25,9},{2,18},{10... | collective-permute-start | bytes 884744 | tf_op jit(solution)/shard_map/ppermute | solution.py:547
  285.2 3.1 collective-permute-start.55
  287.5 8.0 %collective-permute-start.61 = (bf16[128,768]{1,0:T(8,128)(2,1)S(1)}, bf16[128,768]{1,0:T(8,128)(2,1)S(1)}, u32[]{:S(2)}, u32[]{:S(2)}) collective-permute-start(bf16[128,768]{1,0:T(8,128)(2,1)S(1)} %slice_select_fusion.1), channel_id=1, source_target_pairs={{0,4},{4,0},{1,5},{5,1},{2,6},{6,2},{3,7},{7,3},{8,12},{12,8},{9,1... | collective-permute-start | bytes 589832 | tf_op jit(solution)/shard_map/ppermute | solution.py:547
  288.3 7.3 %collective-permute-start.59 = (f32[16,768]{1,0:T(8,128)S(1)}, f32[16,768]{1,0:T(8,128)S(1)}, u32[]{:S(2)}, u32[]{:S(2)}) collective-permute-start(f32[16,768]{1,0:T(8,128)S(1)} %add.142), channel_id=1, source_target_pairs={{0,2},{1,3},{2,0},{3,1},{4,6},{5,7},{6,4},{7,5},{8,10},{9,11},{10,... | collective-permute-start | bytes 147464 | tf_op jit(solution)/shard_map/ppermute | solution.py:547
  289.4 12.3 %collective-permute-start.56 = (bf16[384,384]{1,0:T(8,128)(2,1)S(1)}, bf16[384,384]{1,0:T(8,128)(2,1)S(1)}, u32[]{:S(2)}, u32[]{:S(2)}) collective-permute-start(bf16[384,384]{1,0:T(8,128)(2,1)S(1)} %slice.444), channel_id=1, source_target_pairs={{0,8},{8,0},{16,24},{24,16},{1,9},{9,1},{17,25},{25,17},{2,10},{10... | collective-permute-start | bytes 884744 | tf_op jit(solution)/shard_map/ppermute | solution.py:547
  296.7 11.0 %collective-permute-start.62 = (bf16[256,768]{1,0:T(8,128)(2,1)S(1)}, bf16[256,768]{1,0:T(8,128)(2,1)S(1)}, u32[]{:S(2)}, u32[]{:S(2)}) collective-permute-start(bf16[256,768]{1,0:T(8,128)(2,1)S(1)} %add_convert_fusion.7), channel_id=1, source_target_pairs={{0,2},{1,3},{2,0},{3,1},{4,6},{5,7},{6,4},{7,5},{8,10},{9,11},{10,... | collective-permute-start | bytes 1179656 | tf_op jit(solution)/shard_map/ppermute | solution.py:547
  298.1 10.7 %collective-permute-start.64 = (f32[256,256]{1,0:T(8,128)S(1)}, f32[256,256]{1,0:T(8,128)S(1)}, u32[]{:S(2)}, u32[]{:S(2)}) collective-permute-start(f32[256,256]{1,0:T(8,128)S(1)} %pack_grads.1), channel_id=1, source_target_pairs={{0,4},{4,0},{1,5},{5,1},{2,6},{6,2},{3,7},{7,3},{8,12},{12,8},{9,1... | collective-permute-start | bytes 786440 | tf_op jit(solution)/shard_map/ppermute | solution.py:547
  299.6 19.0 %collective-permute-start.68 = (bf16[192,1536]{1,0:T(8,128)(2,1)S(1)}, bf16[192,1536]{1,0:T(8,128)(2,1)S(1)}, u32[]{:S(2)}, u32[]{:S(2)}) collective-permute-start(bf16[192,1536]{1,0:T(8,128)(2,1)S(1)} %pad_maximum_fusion.7), channel_id=1, source_target_pairs={{0,4},{4,0},{1,5},{5,1},{2,6},{6,2},{3,7},{7,3},{8,12},{12,8},{9,1... | collective-permute-start | bytes 1769480 | tf_op jit(solution)/shard_map/ppermute | solution.py:547
  307.8 7.9 %collective-permute-start.63 = (bf16[192,384]{1,0:T(8,128)(2,1)S(1)}, bf16[192,384]{1,0:T(8,128)(2,1)S(1)}, u32[]{:S(2)}, u32[]{:S(2)}) collective-permute-start(bf16[192,384]{1,0:T(8,128)(2,1)S(1)} %slice.449), channel_id=1, source_target_pairs={{0,16},{8,24},{16,0},{24,8},{1,17},{9,25},{17,1},{25,9},{2,18},{10... | collective-permute-start | bytes 442376 | tf_op jit(solution)/shard_map/ppermute | solution.py:547
  315.7 8.6 %collective-permute-start.65 = (bf16[192,384]{1,0:T(8,128)(2,1)S(1)}, bf16[192,384]{1,0:T(8,128)(2,1)S(1)}, u32[]{:S(2)}, u32[]{:S(2)}) collective-permute-start(bf16[192,384]{1,0:T(8,128)(2,1)S(1)} %fusion.81.refs_0_), channel_id=1, source_target_pairs={{0,4},{4,0},{1,5},{5,1},{2,6},{6,2},{3,7},{7,3},{8,12},{12,8},{9,1... | collective-permute-start | bytes 442376 | tf_op jit(solution)/shard_map/ppermute | solution.py:547
  317.4 5.2 %collective-permute-start.67 = (f32[128,256]{1,0:T(8,128)S(1)}, f32[128,256]{1,0:T(8,128)S(1)}, u32[]{:S(2)}, u32[]{:S(2)}) collective-permute-start(f32[128,256]{1,0:T(8,128)S(1)} %slice.370), channel_id=1, source_target_pairs={{0,8},{8,0},{16,24},{24,16},{1,9},{9,1},{17,25},{25,17},{2,10},{10... | collective-permute-start | bytes 393224 | tf_op jit(solution)/shard_map/ppermute | solution.py:547
  317.5 8.4 %collective-permute-start.66 = (bf16[128,768]{1,0:T(8,128)(2,1)S(1)}, bf16[128,768]{1,0:T(8,128)(2,1)S(1)}, u32[]{:S(2)}, u32[]{:S(2)}) collective-permute-start(bf16[128,768]{1,0:T(8,128)(2,1)S(1)} %get-tuple-element.369), channel_id=1, source_target_pairs={{0,4},{4,0},{1,5},{5,1},{2,6},{6,2},{3,7},{7,3},{8,12},{12,8},{9,1... | collective-permute-start | bytes 589832 | tf_op jit(solution)/shard_map/ppermute | solution.py:547
  322.6 5.9 %collective-permute-start.69 = (f32[64,256]{1,0:T(8,128)S(1)}, f32[64,256]{1,0:T(8,128)S(1)}, u32[]{:S(2)}, u32[]{:S(2)}) collective-permute-start(f32[64,256]{1,0:T(8,128)S(1)} %slice.372), channel_id=1, source_target_pairs={{0,16},{8,24},{16,0},{24,8},{1,17},{9,25},{17,1},{25,9},{2,18},{10... | collective-permute-start | bytes 196616 | tf_op jit(solution)/shard_map/ppermute | solution.py:547
  (16 other events, 168.5 us)

commit v2 on v1

--- a/solution.py
+++ b/solution.py
@@ -932,37 +932,24 @@
     return value, slope
 
 
-def split_parts(weight):
-    size = min(weight.shape[1], 768)
-    return [slice(at, at + size) for at in range(0, weight.shape[1], size)]
-
-
-def feed_forward_kernel(
-    count, near_ref, far_ref, bias_ref, *refs
-):
-    sent_ref, kept_ref, expand_ref, reduce_ref = refs[-4:]
+def feed_forward_kernel(count, piece, bias_ref, *refs):
+    out, expand_ref, reduce_ref = refs[-3:]
     join(refs[:count], expand_ref)
-    join(refs[count:-4], reduce_ref)
-    parts = split_parts(expand_ref)
-    for piece, out in ((far_ref, sent_ref), (near_ref, kept_ref)):
-
-        def step(i, carry):
-            at = pl.ds(pl.multiple_of(i * CHUNK, CHUNK), CHUNK)
-            rows = piece[at, :]
-            total = None
-            for columns in parts:
-                hidden = jnp.dot(rows, expand_ref[:, columns], preferred_element_type=F32)
-                active = gelu_tanh(hidden + bias_ref[:, columns]).astype(BF16)
-                product = dot_across(active, reduce_ref[:, columns])
-                total = product if total is None else total + product
-            out[at, :] = total.astype(out.dtype)
-            return carry
-
-        lax.fori_loop(0, piece.shape[0] // CHUNK, step, 0)
-
-
-def feed_forward(near, far, expand, reduce, bias):
-    half, features = near.shape
+    join(refs[count:-3], reduce_ref)
+
+    def step(i, carry):
+        at = pl.ds(pl.multiple_of(i * CHUNK, CHUNK), CHUNK)
+        hidden = jnp.dot(piece[at, :], expand_ref[...], preferred_element_type=F32)
+        active = gelu_tanh(hidden + bias_ref[...]).astype(BF16)
+        out[at, :] = dot_across(active, reduce_ref[...]).astype(out.dtype)
+        return carry
+
+    lax.fori_loop(0, piece.shape[0] // CHUNK, step, 0)
+
+
+def feed_rows(piece, weights, kind):
+    expand, reduce, bias = weights
+    rows, features = piece.shape
     hidden = bias.shape[1]
 
     def body(*refs):
@@ -971,61 +958,43 @@
     return call(
         body,
         "feed_forward",
-        (near, far, bias) + tuple(expand) + tuple(reduce),
-        (shaped(half, features, BF16), shaped(half, features, F32)),
+        (piece, bias) + tuple(expand) + tuple(reduce),
+        (shaped(rows, features, kind),),
         [pltpu.VMEM((features, hidden), BF16), pltpu.VMEM((features, hidden), BF16)],
-        8 * half * features * hidden,
-        2 * half * hidden,
-    )
-
-
-def feed_backward_kernel(
-    count,
-    near_ref,
-    far_ref,
-    near_grad,
-    far_grad,
-    bias_ref,
-    *refs,
-):
-    sent_ref, kept_ref, active_ref, hidden_ref, sum_ref, expand_ref, reduce_ref = refs[-7:]
+        4 * rows * features * hidden,
+        rows * hidden,
+    )[0]
+
+
+def feed_forward(near, far, expand, reduce, bias):
+    weights = expand, reduce, bias
+    return feed_rows(far, weights, BF16), feed_rows(near, weights, F32)
+
+
+def feed_backward_kernel(count, piece, grads, bias_ref, *refs):
+    out, active_ref, hidden_ref, sum_ref, expand_ref, reduce_ref = refs[-6:]
     join(refs[:count], expand_ref)
-    join(refs[count:-7], reduce_ref)
-    parts = split_parts(expand_ref)
-    half = near_ref.shape[0]
+    join(refs[count:-6], reduce_ref)
     sum_ref[...] = jnp.zeros_like(sum_ref)
-    for piece, grads, out, base in (
-        (far_ref, far_grad, sent_ref, half),
-        (near_ref, near_grad, kept_ref, 0),
-    ):
-
-        def step(i, carry):
-            place = pl.multiple_of(i * CHUNK, CHUNK)
-            at = pl.ds(place, CHUNK)
-            whole = pl.ds(pl.multiple_of(base + place, CHUNK), CHUNK)
-            rows = piece[at, :]
-            grad_rows = grads[at, :]
-            total = None
-            for columns in parts:
-                hidden = jnp.dot(rows, expand_ref[:, columns], preferred_element_type=F32)
-                value, slope = gelu_both(hidden + bias_ref[:, columns])
-                active_ref[whole, columns] = value.astype(BF16)
-                grad_active = jnp.dot(
-                    grad_rows, reduce_ref[:, columns], preferred_element_type=F32
-                )
-                grad_hidden = (grad_active * slope).astype(BF16)
-                hidden_ref[whole, columns] = grad_hidden
-                sum_ref[:, columns] += jnp.sum(grad_hidden.astype(F32), axis=0, keepdims=True)
-                product = dot_across(grad_hidden, expand_ref[:, columns])
-                total = product if total is None else total + product
-            out[at, :] = total.astype(out.dtype)
-            return carry
-
-        lax.fori_loop(0, half // CHUNK, step, 0)
-
-
-def feed_backward(near, far, near_grad, far_grad, expand, reduce, bias):
-    half, features = near.shape
+
+    def step(i, carry):
+        at = pl.ds(pl.multiple_of(i * CHUNK, CHUNK), CHUNK)
+        hidden = jnp.dot(piece[at, :], expand_ref[...], preferred_element_type=F32)
+        value, slope = gelu_both(hidden + bias_ref[...])
+        active_ref[at, :] = value.astype(BF16)
+        grad_active = jnp.dot(grads[at, :], reduce_ref[...], preferred_element_type=F32)
+        grad_hidden = (grad_active * slope).astype(BF16)
+        hidden_ref[at, :] = grad_hidden
+        sum_ref[...] += jnp.sum(grad_hidden.astype(F32), axis=0, keepdims=True)
+        out[at, :] = dot_across(grad_hidden, expand_ref[...]).astype(out.dtype)
+        return carry
+
+    lax.fori_loop(0, piece.shape[0] // CHUNK, step, 0)
+
+
+def feed_back_rows(piece, grads, weights, kind):
+    expand, reduce, bias = weights
+    rows, features = piece.shape
     hidden = bias.shape[1]
 
     def body(*refs):
@@ -1034,17 +1003,29 @@
     return call(
         body,
         "feed_backward",
-        (near, far, near_grad, far_grad, bias) + tuple(expand) + tuple(reduce),
+        (piece, grads, bias) + tuple(expand) + tuple(reduce),
         (
-            shaped(half, features, BF16),
-            shaped(half, features, F32),
-            shaped(2 * half, hidden, BF16),
-            shaped(2 * half, hidden, BF16),
+            shaped(rows, features, kind),
+            shaped(rows, hidden, BF16),
+            shaped(rows, hidden, BF16),
             shaped(1, hidden, F32),
         ),
         [pltpu.VMEM((features, hidden), BF16), pltpu.VMEM((features, hidden), BF16)],
-        12 * half * features * hidden,
-        2 * half * hidden,
+        6 * rows * features * hidden,
+        rows * hidden,
+    )
+
+
+def feed_backward(near, far, near_grad, far_grad, expand, reduce, bias):
+    weights = expand, reduce, bias
+    sent, far_active, far_hidden, far_sum = feed_back_rows(far, far_grad, weights, BF16)
+    kept, active, hidden, sums = feed_back_rows(near, near_grad, weights, F32)
+    return (
+        sent,
+        kept,
+        jnp.concatenate([active, far_active], axis=0),
+        jnp.concatenate([hidden, far_hidden], axis=0),
+        sums + far_sum,
     )
 
 
@@ -1243,7 +1224,7 @@
 
 
 ROWS = 64
-SPARE = ROWS // 2
+SPARE = ROWS // 4
 
 
 def turn(value):
@@ -1326,9 +1307,10 @@
         merged_ref, output_ref = part[-2:]
         pieces = [merged_ref[k] for k in range(3)] + [turn(output_ref[...]).astype(BF16)]
         out[:local, :] = jnp.concatenate(pieces, axis=1)
-        out[local:, :256] = small[:SPARE, :].astype(BF16)
-        out[local:, 256:512] = small[SPARE:, :].astype(BF16)
-        out[local:, 512:] = jnp.zeros((SPARE, 4 * local - 512), BF16)
+        for i in range(4):
+            out[local:, local * i : local * (i + 1)] = small[
+                SPARE * i : SPARE * (i + 1), :local
+            ].astype(BF16)
 
     return pl.pallas_call(
         body,
@@ -1350,9 +1332,9 @@
     def body(place_ref, *refs):
         pieces, outs, pieces_ref = refs[:4], refs[4:-1], refs[-1]
         for k in range(4):
-            for i in range(2):
-                pieces_ref[k * ROWS + i * SPARE : k * ROWS + (i + 1) * SPARE, :] = pieces[k][
-                    local:, 256 * i : 256 * (i + 1)
+            for i in range(4):
+                pieces_ref[k * ROWS + i * SPARE : k * ROWS + (i + 1) * SPARE, :local] = pieces[k][
+                    local:, local * i : local * (i + 1)
                 ].astype(F32)
         y, z = place_ref[0], place_ref[1]
         for b in range(2):
@@ -1608,8 +1590,10 @@
     p = blocks[0]
     attend = prepare_first(place, p[2], p[4], small)
     inputs, attend = pin(inputs, attend)
-    far, near = cross_far(attend), cross_near(attend)
+    far = cross_far(attend)
     sent_rows = jnp.where(y_index == 0, inputs[1], inputs[0])
+    sent_rows, late = pin(sent_rows, attend)
+    near = cross_near(late)
     sent_docs = jnp.where(y_index == 0, segments[1:2], segments[0:1]).astype(BF16)
     sent_docs = jnp.pad(sent_docs, ((0, 15), (0, features - sent_docs.shape[1])))
     moved = cross_y(stacked(sent_rows, sent_docs))
@@ -1761,7 +1745,7 @@
     sent, kept, grad_qkv, qkv_sum_s = attention_backward(
         near_grad, far_grad, attend_s, context, saved_s, doc_max
     )
-    sent, a_moved, fe_moved, theirs_t, feed_r = pin(sent, a_moved, fe_moved, theirs_t, feed_r)
+    sent, a_moved, fe_moved, feed_r = pin(sent, a_moved, fe_moved, feed_r)
     mine_at, feed_e = keep_rows(part_a, a_moved), keep_rows(feed_e, fe_moved)
     fr_moved, fe_moved = send_rows(feed_r, cross_far), send_rows(feed_e, cross_far)
     arrived = cross_core(sent)
@@ -1793,7 +1777,7 @@
         return jnp.where(y_index == 0, jnp.stack([kept, received]), jnp.stack([received, kept]))
 
     grad_moved = swapped(input_grad.astype(BF16))
-    y_moved, sums_moved = pin(y_moved, sums_moved)
+    y_moved, sums_moved, theirs_t = pin(y_moved, sums_moved, theirs_t)
     grad_a = grad_a.astype(F32) + y_moved.astype(F32)
     y_moved = send_rows(grad_a, cross_near)
     sums = sums + sums_moved
@@ -1813,17 +1797,17 @@
         params[9].shape,
     )
     mine_s = beside(keep_rows(feed_e, fe_moved), keep_rows(feed_r, fr_moved), mine_at).astype(BF16)
-    pack, mine_s = pin(pack, mine_s)
     pack_moved = cross_y(pack)
+    expand_grad_t, reduce_grad_t = finish_feed(mine_t, theirs_t, place, half)
+    y_moved, mine_s = pin(y_moved, mine_s)
     theirs_s = cross_y(
         beside(
             mine_s[:, :half], mine_s[:, 2 * half : 3 * half], mine_s[:, half : 2 * half], mine_s[:, 3 * half :]
         )
     )
-    expand_grad_t, reduce_grad_t = finish_feed(mine_t, theirs_t, place, half)
-    y_moved, final_across, expand_grad_t = pin(y_moved, final_across, expand_grad_t)
     grad_a = keep_rows(grad_a, y_moved)
     y_moved = send_rows(grad_a, cross_far)
+    final_across, expand_grad_t = pin(final_across, expand_grad_t)
     rows = 2 * tokens
     final = middle_t[:rows] + gains_t[5:6] + final_kept[:rows] + final_across.astype(F32)
     final = final + final_arrived[:rows].astype(F32)
@@ -1837,15 +1821,17 @@
     merged_grad_t, output_grad_t = finish_attend(
         (), mine_s[:, 3 * half :], theirs_s[:, 3 * half :], place
     )
-    pack_near, output_grad_t = pin(pack_near, output_grad_t)
+    expand_grad_s, reduce_grad_s = finish_feed(
+        mine_s[:, : 3 * half], theirs_s[:, : 3 * half], place, half
+    )
+    pack_near, pack = pin(pack_near, pack)
     pack = pack[: 2 * ROWS] + pack_near
     pack_far = cross_far(pack[ROWS:])
-    theirs_a, final_moved = pin(theirs_a, final_moved)
+    theirs_a, final_moved, pack_far, output_grad_t, expand_grad_s = pin(
+        theirs_a, final_moved, pack_far, output_grad_t, expand_grad_s
+    )
     grad_moved = grad_moved.astype(F32)
     merged_grad_s, output_grad_s = finish_attend((), mine_a, theirs_a, place)
-    expand_grad_s, reduce_grad_s = finish_feed(
-        mine_s[:, : 3 * half], theirs_s[:, : 3 * half], place, half
-    )
     vectors = unpack_grads(pack, pack_far, local, params[3].shape, params[9].shape)
     outputs = [restore(final, final_moved), restore(input_grad, grad_moved)]
     for vector, merged, output, expand, reduce in (

time: 334 us -> 331 us (level)
  waiting for transfers between devices: 161 us -> 153 us
  starting transfers between devices: 68.2 us -> 71.9 us
    ppermute x70, waiting for transfers between devices: 161 us -> 153 us  [swap(): return row_major(lax.ppermute(row_major(value), axis, route))]
    ppermute x70, starting transfers between devices: 68.2 us -> 71.9 us  [swap(): return row_major(lax.ppermute(row_major(value), axis, route))]
    pallas_call x8 -> x12, Pallas kernels: 53.3 us -> 53.9 us  [call(): pl.pallas_call(body, out_shape=tuple(outputs), in_specs=[SMEM if v.ndim =...]
  transfers between devices with their start and end apart: 70 -> 70, of which waited for: 41 -> 37; matrix products, arithmetic and copies ran while one was open for 7% -> 6% of each run, Pallas kernels for 18% -> 19%
where the time goes in v2:
time: 331 us; the launch traced here: 326 us
  waiting for transfers between devices  153 us (46%)
  Pallas kernels  76.2 us (23%)
  starting transfers between devices  71.9 us (22%)
  matrix products  13.7 us (4%)
  other arithmetic  8.13 us (2%)
    ppermute x70, waiting for transfers between devices, swap(): return row_major(lax.ppermute(row_major(value), axis, route))  153 us
    ppermute x70, starting transfers between devices, swap(): return row_major(lax.ppermute(row_major(value), axis, route))  71.9 us
    pallas_call x12, Pallas kernels, call(): pl.pallas_call(body, out_shape=tuple(outputs), in_specs=[SMEM if v.ndim =...  53.9 us
    dot_general x8, matrix products, dot_down(): lax.dot_general(left, right, (((0,), (0,)), ((), ())), preferred_element_...  9.98 us
    pallas_call x8, Pallas kernels, row_call(): pl.pallas_call(body, grid=(1,), out_shape=tuple(outputs), in_specs=specs,...  9.77 us
  transfers between devices with their start and end apart: 70, of which 37 were waited for; matrix products, arithmetic and copies ran while one was open for 6% of the time, Pallas kernels for 19%

profile of v2, /device:TPU:0, one launch (start us, length us, event | category | flops | bytes accessed | tf_op | source)
XLA Modules:
  0.0 326.2 jit_solution(16832145087763961068)
XLA Ops:
  0.7 2.4 prepare_first.1.refs_0_.refs_6_
  3.1 4.1 %collective-permute-start.3 = (bf16[208,768]{1,0:T(8,128)(2,1)}, bf16[208,768]{1,0:T(8,128)(2,1)S(1)}, u32[]{:S(2)}, u32[]{:S(2)}) collective-permute-start(bf16[208,768]{1,0:T(8,128)(2,1)} %prepare_first.1.refs_0_.refs_6_), channel_id=1, source_target_pairs={{0,16},{8,24},{16,0},{24,8},{1,17},{9,25},{17,1},{25,9},{2,18},{10... | collective-permute-start | bytes 958472 | tf_op jit(solution)/shard_map/ppermute | solution.py:547
  9.0 1.6 collective-permute-start
  10.6 1.6 collective-permute-start.2
  13.5 3.9 %collective-permute-done = bf16[144,768]{1,0:T(8,128)(2,1)S(1)} collective-permute-done((bf16[144,768]{1,0:T(8,128)(2,1)S(1)}, bf16[144,768]{1,0:T(8,128)(2,1)S(1)}, u32[]{:S(2)}, u32[]{:S(2)}) %collective-permute-start) | collective-permute-done | bytes 221216 | tf_op jit(solution)/shard_map/ppermute | solution.py:547
  18.3 1.6 collective-permute-start.1
  22.0 4.1 %collective-permute-start.4 = (bf16[208,768]{1,0:T(8,128)(2,1)S(1)}, bf16[208,768]{1,0:T(8,128)(2,1)S(1)}, u32[]{:S(2)}, u32[]{:S(2)}) collective-permute-start(bf16[208,768]{1,0:T(8,128)(2,1)S(1)} %collective-permute-done.3.refs_1_.refs_7_), channel_id=1, source_target_pairs={{0,8},{8,0},{16,24},{24,16},{1,9},{9,1},{17,25},{25,17},{2,10},{10... | collective-permute-start | bytes 958472 | tf_op jit(solution)/shard_map/ppermute | solution.py:547
  27.1 10.4 %collective-permute-done.5 = bf16[192,768]{1,0:T(8,128)(2,1)S(1)} collective-permute-done((bf16[192,768]{1,0:T(8,128)(2,1)S(1)}, bf16[192,768]{1,0:T(8,128)(2,1)S(1)}, u32[]{:S(2)}, u32[]{:S(2)}) %collective-permute-start.5) | collective-permute-done | bytes 294944 | tf_op jit(solution)/shard_map/ppermute | solution.py:547
  39.9 1.6 collective-permute-start.10
  41.5 3.5 %collective-permute-start.9 = (bf16[192,384]{1,0:T(8,128)(2,1)S(1)}, bf16[192,384]{1,0:T(8,128)(2,1)S(1)}, u32[]{:S(2)}, u32[]{:S(2)}) collective-permute-start(bf16[192,384]{1,0:T(8,128)(2,1)S(1)} %get-tuple-element.378), channel_id=1, source_target_pairs={{0,16},{8,24},{16,0},{24,8},{1,17},{9,25},{17,1},{25,9},{2,18},{10... | collective-permute-start | bytes 442376 | tf_op jit(solution)/shard_map/ppermute | solution.py:547
  45.8 8.0 %attention_forward.2 = (bf16[512,768]{1,0:T(8,128)(2,1)S(1)}, f32[512,768]{1,0:T(8,128)S(1)}, bf16[9,1024,64]{2,1,0:T(8,128)(2,1)S(1)}, bf16[1024,192]{1,0:T(8,1...) custom-call(s32[1]{0:T(128)} %bitcast.refs_0_, ...), custom_call_target="tpu_custom_call" | custom-call | flops 1610612736 | bytes 8399108 | tf_op jit(solution)/shard_map/attention_forward/pallas_call | solution.py:840
  53.9 2.3 collective-permute-done.11
  57.6 1.6 collective-permute-start.13
  59.2 1.7 collective-permute-start.15
  60.9 15.1 %collective-permute-done.12.across_ref = bf16[512,768]{1,0:T(8,128)(2,1)S(1)} collective-permute-done((bf16[512,768]{1,0:T(8,128)(2,1)S(1)}, bf16[512,768]{1,0:T(8,128)(2,1)S(1)}, u32[]{:S(2)}, u32[]{:S(2)}) %collective-permute-start.12) | collective-permute-done | bytes 786464 | tf_op jit(solution)/shard_map/ppermute | solution.py:547
  78.6 2.3 collective-permute-done.16.refs_0_
  80.8 2.1 feed_forward.5
  83.1 2.1 feed_forward.4
  85.4 1.5 collective-permute-start.18
  88.7 2.1 collective-permute-start.21
  90.8 14.4 %collective-permute-done.18.across_ref = bf16[512,768]{1,0:T(8,128)(2,1)S(1)} collective-permute-done((bf16[512,768]{1,0:T(8,128)(2,1)S(1)}, bf16[512,768]{1,0:T(8,128)(2,1)S(1)}, u32[]{:S(2)}, u32[]{:S(2)}) %collective-permute-start.18) | collective-permute-done | bytes 786464 | tf_op jit(solution)/shard_map/ppermute | solution.py:547
  106.9 1.8 collective-permute-done.19.refs_6_.refs_7_
  111.0 7.3 %attention_forward.3 = (bf16[512,768]{1,0:T(8,128)(2,1)S(1)}, f32[512,768]{1,0:T(8,128)S(1)}, bf16[9,1024,64]{2,1,0:T(8,128)(2,1)S(1)}, bf16[1024,192]{1,0:T(8,128)(2,1)S(1)}, f32[3,1,1024]{2,1,0:T(1,128)S(1)}) custom-call(s32[1]{0:T(128)} %bitcast.refs_0_, bf16[512,768]{1,0:T(8,128)(2,1)S(1)} %get-tuple-element.234.refs_1_, ...), custom_call_target="tpu_custom_call" | custom-call | flops 1610612736 | bytes 6703364 | tf_op jit(solution)/shard_map/attention_forward/pallas_call | solution.py:840
  118.3 1.8 collective-permute-done.24
  122.0 1.7 collective-permute-done.25
  124.7 2.5 collective-permute-start.28
  127.3 1.6 collective-permute-start.27
  128.8 14.7 %collective-permute-done.26.across_ref = bf16[512,768]{1,0:T(8,128)(2,1)S(1)} collective-permute-done((bf16[512,768]{1,0:T(8,128)(2,1)S(1)}, bf16[512,768]{1,0:T(8,128)(2,1)S(1)}, u32[]{:S(2)}, u32[]{:S(2)}) %collective-permute-start.26) | collective-permute-done | bytes 786464 | tf_op jit(solution)/shard_map/ppermute | solution.py:547
  144.7 2.3 collective-permute-done.30.refs_0_
  147.0 2.8 feed_backward.5
  150.0 2.7 feed_backward.4
  156.5 1.6 collective-permute-start.34
  158.1 2.6 collective-permute-start.33
  160.8 2.0 feed_forward.7
  162.8 2.1 feed_forward.6
  164.9 9.4 %collective-permute-done.32.across_ref = bf16[512,768]{1,0:T(8,128)(2,1)S(1)} collective-permute-done((bf16[512,768]{1,0:T(8,128)(2,1)S(1)}, bf16[512,768]{1,0:T(8,128)(2,1)S(1)}, u32[]{:S(2)}, u32[]{:S(2)}) %collective-permute-start.32) | collective-permute-done | bytes 786464 | tf_op jit(solution)/shard_map/ppermute | solution.py:547
  176.1 1.7 collective-permute-start.36
  178.2 10.0 %attention_backward.2 = (bf16[512,768]{1,0:T(8,128)(2,1)S(1)}, f32[512,768]{1,0:T(8,128)S(1)}, bf16[1024,576]{1,0:T(8,128)(2,1)S(1)}, f32[1,576]{1,0:T(1,128)S(1)}) custom-call(s32[1]{0:T(128)} %bitcast.refs_0_, bf16[512,768]{1,0:T(8,128)(2,1)S(1)} %get-tuple-element.264.refs_1_, bf16[512,768]{1,0:T(8,128)(2,1)S(1)} %collective-permute-done.35.refs_2_, ...), custom_call_target="tpu_custom_call" | custom-call | flops 4026531840 | bytes 7489796 | tf_op jit(solution)/shard_map/attention_backward/pallas_call | solution.py:840
  192.3 1.6 collective-permute-start.41
  197.1 13.4 %collective-permute-done.38.across_ref = bf16[512,768]{1,0:T(8,128)(2,1)S(1)} collective-permute-done((bf16[512,768]{1,0:T(8,128)(2,1)S(1)}, bf16[512,768]{1,0:T(8,128)(2,1)S(1)}, u32[]{:S(2)}, u32[]{:S(2)}) %collective-permute-start.38) | collective-permute-done | bytes 786464 | tf_op jit(solution)/shard_map/ppermute | solution.py:547
  212.0 4.2 %collective-permute-done.39 = bf16[192,384]{1,0:T(8,128)(2,1)S(1)} collective-permute-done((bf16[192,384]{1,0:T(8,128)(2,1)S(1)}, bf16[192,384]{1,0:T(8,128)(2,1)S(1)}, u32[]{:S(2)}, u32[]{:S(2)}) %collective-permute-start.39) | collective-permute-done | bytes 147488 | tf_op jit(solution)/shard_map/ppermute | solution.py:547
  216.2 2.3 collective-permute-done.42.refs_1_
  218.5 2.7 feed_backward.7
  221.3 2.6 feed_backward.6
  229.3 2.1 collective-permute-start.45
  231.4 14.5 %collective-permute-done.44.across_ref = bf16[512,768]{1,0:T(8,128)(2,1)S(1)} collective-permute-done((bf16[512,768]{1,0:T(8,128)(2,1)S(1)}, bf16[512,768]{1,0:T(8,128)(2,1)S(1)}, u32[]{:S(2)}, u32[]{:S(2)}) %collective-permute-start.44) | collective-permute-done | bytes 786464 | tf_op jit(solution)/shard_map/ppermute | solution.py:547
  245.9 1.7 norm_back_near.5
  247.6 2.8 collective-permute-done.45
  250.6 1.6 collective-permute-start.55
  252.8 2.1 collective-permute-start.50
  255.0 9.5 %attention_backward.3 = (bf16[512,768]{1,0:T(8,128)(2,1)S(1)}, f32[512,768]{1,0:T(8,128)S(1)}, bf16[1024,576]{1,0:T(8,128)(2,1)S(1)}, f32[1,576]{1,0:T(1,128)S(1)}) custom-call(s32[1]{0:T(128)} %bitcast.refs_0_, bf16[512,768]{1,0:T(8,128)(2,1)S(1)} %get-tuple-element.293.refs_1_, bf16[512,768]{1,0:T(8,128)(2,1)S(1)} %collective-permute-done.48.refs_2_, ...), custom_call_target="tpu_custom_call" | custom-call | flops 4026531840 | bytes 7588100 | tf_op jit(solution)/shard_map/attention_backward/pallas_call | solution.py:840
  270.8 8.6 %collective-permute-done.53.refs_6_ = bf16[256,768]{1,0:T(8,128)(2,1)S(1)} collective-permute-done((bf16[256,768]{1,0:T(8,128)(2,1)S(1)}, bf16[256,768]{1,0:T(8,128)(2,1)S(1)}, u32[]{:S(2)}, u32[]{:S(2)}) %collective-permute-start.53) | collective-permute-done | bytes 393248 | tf_op jit(solution)/shard_map/ppermute | solution.py:547
  286.8 1.6 finish_feed.2
  289.6 3.2 collective-permute-done.57
  294.9 1.6 collective-permute-start.63
  296.6 2.4 collective-permute-done.56
  299.1 1.6 collective-permute-start.69
  300.9 3.2 collective-permute-done.64
  304.9 4.5 %collective-permute-done.62 = bf16[192,384]{1,0:T(8,128)(2,1)S(1)} collective-permute-done((bf16[192,384]{1,0:T(8,128)(2,1)S(1)}, bf16[192,384]{1,0:T(8,128)(2,1)S(1)}, u32[]{:S(2)}, u32[]{:S(2)}) %collective-permute-start.62) | collective-permute-done | bytes 147488 | tf_op jit(solution)/shard_map/ppermute | solution.py:547
  311.8 3.2 collective-permute-done.67
  316.6 1.6 finish_attend.2
  318.3 1.6 finish_feed.3
  319.9 3.0 collective-permute-done.65.refs_1_
  322.9 1.6 finish_attend.3
  (229 shorter events, 69.3 us)
Async XLA Ops:
  3.1 18.8 %collective-permute-start.3 = (bf16[208,768]{1,0:T(8,128)(2,1)}, bf16[208,768]{1,0:T(8,128)(2,1)S(1)}, u32[]{:S(2)}, u32[]{:S(2)}) collective-permute-start(bf16[208,768]{1,0:T(8,128)(2,1)} %prepare_first.1.refs_0_.refs_6_), channel_id=1, source_target_pairs={{0,16},{8,24},{16,0},{24,8},{1,17},{9,25},{17,1},{25,9},{2,18},{10... | collective-permute-start | bytes 958472 | tf_op jit(solution)/shard_map/ppermute | solution.py:547
  9.0 8.4 %collective-permute-start = (bf16[144,768]{1,0:T(8,128)(2,1)S(1)}, bf16[144,768]{1,0:T(8,128)(2,1)S(1)}, u32[]{:S(2)}, u32[]{:S(2)}) collective-permute-start(bf16[144,768]{1,0:T(8,128)(2,1)S(1)} %fusion.103), channel_id=1, source_target_pairs={{0,4},{4,0},{1,5},{5,1},{2,6},{6,2},{3,7},{7,3},{8,12},{12,8},{9,1... | collective-permute-start | bytes 663560 | tf_op jit(solution)/shard_map/ppermute | solution.py:547
  10.6 16.5 %collective-permute-start.2 = (bf16[208,768]{1,0:T(8,128)(2,1)}, bf16[208,768]{1,0:T(8,128)(2,1)S(1)}, u32[]{:S(2)}, u32[]{:S(2)}) collective-permute-start(bf16[208,768]{1,0:T(8,128)(2,1)} %prepare_first.1.refs_0_.refs_6_), channel_id=1, source_target_pairs={{0,8},{8,0},{16,24},{24,16},{1,9},{9,1},{17,25},{25,17},{2,10},{10... | collective-permute-start | bytes 958472 | tf_op jit(solution)/shard_map/ppermute | solution.py:547
  12.2 14.4 %collective-permute-start.6 = (bf16[128,768]{1,0:T(8,128)(2,1)S(1)}, bf16[128,768]{1,0:T(8,128)(2,1)S(1)}, u32[]{:S(2)}, u32[]{:S(2)}) collective-permute-start(bf16[128,768]{1,0:T(8,128)(2,1)S(1)} %get-tuple-element.383), channel_id=1, source_target_pairs={{0,4},{4,0},{1,5},{5,1},{2,6},{6,2},{3,7},{7,3},{8,12},{12,8},{9,1... | collective-permute-start | bytes 589832 | tf_op jit(solution)/shard_map/ppermute | solution.py:547
  18.3 8.3 %collective-permute-start.1 = (bf16[256,768]{1,0:T(8,128)(2,1)S(1)}, bf16[256,768]{1,0:T(8,128)(2,1)S(1)}, u32[]{:S(2)}, u32[]{:S(2)}) collective-permute-start(bf16[256,768]{1,0:T(8,128)(2,1)S(1)} %convolution_convert_fusion.2), channel_id=1, source_target_pairs={{0,2},{1,3},{2,0},{3,1},{4,6},{5,7},{6,4},{7,5},{8,10},{9,11},{10,... | collective-permute-start | bytes 1179656 | tf_op jit(solution)/shard_map/ppermute | solution.py:547
  21.9 15.6 %collective-permute-start.5 = (bf16[192,768]{1,0:T(8,128)(2,1)S(1)}, bf16[192,768]{1,0:T(8,128)(2,1)S(1)}, u32[]{:S(2)}, u32[]{:S(2)}) collective-permute-start(bf16[192,768]{1,0:T(8,128)(2,1)S(1)} %get-tuple-element.377), channel_id=1, source_target_pairs={{0,16},{8,24},{16,0},{24,8},{1,17},{9,25},{17,1},{25,9},{2,18},{10... | collective-permute-start | bytes 884744 | tf_op jit(solution)/shard_map/ppermute | solution.py:547
  22.0 16.4 %collective-permute-start.4 = (bf16[208,768]{1,0:T(8,128)(2,1)S(1)}, bf16[208,768]{1,0:T(8,128)(2,1)S(1)}, u32[]{:S(2)}, u32[]{:S(2)}) collective-permute-start(bf16[208,768]{1,0:T(8,128)(2,1)S(1)} %collective-permute-done.3.refs_1_.refs_7_), channel_id=1, source_target_pairs={{0,8},{8,0},{16,24},{24,16},{1,9},{9,1},{17,25},{25,17},{2,10},{10... | collective-permute-start | bytes 958472 | tf_op jit(solution)/shard_map/ppermute | solution.py:547
  38.8 7.0 %collective-permute-start.7 = (bf16[512,768]{1,0:T(8,128)(2,1)S(1)}, bf16[512,768]{1,0:T(8,128)(2,1)S(1)}, u32[]{:S(2)}, u32[]{:S(2)}) collective-permute-start(bf16[512,768]{1,0:T(8,128)(2,1)S(1)} %norm_only.1.refs_1_), channel_id=1, source_target_pairs={{0,1},{1,0},{2,3},{3,2},{4,5},{5,4},{6,7},{7,6},{8,9},{9,8},{10,11... | collective-permute-start | bytes 2359304 | tf_op jit(solution)/shard_map/ppermute | solution.py:547
  39.0 14.8 %collective-permute-start.8 = (bf16[384,384]{1,0:T(8,128)(2,1)S(1)}, bf16[384,384]{1,0:T(8,128)(2,1)S(1)}, u32[]{:S(2)}, u32[]{:S(2)}) collective-permute-start(bf16[384,384]{1,0:T(8,128)(2,1)S(1)} %pad_maximum_fusion.10), channel_id=1, source_target_pairs={{0,8},{8,0},{16,24},{24,16},{1,9},{9,1},{17,25},{25,17},{2,10},{10... | collective-permute-start | bytes 884744 | tf_op jit(solution)/shard_map/ppermute | solution.py:547
  39.9 14.0 %collective-permute-start.10 = (bf16[256,768]{1,0:T(8,128)(2,1)S(1)}, bf16[256,768]{1,0:T(8,128)(2,1)S(1)}, u32[]{:S(2)}, u32[]{:S(2)}) collective-permute-start(bf16[256,768]{1,0:T(8,128)(2,1)S(1)} %convolution_convert_fusion.1), channel_id=1, source_target_pairs={{0,2},{1,3},{2,0},{3,1},{4,6},{5,7},{6,4},{7,5},{8,10},{9,11},{10,... | collective-permute-start | bytes 1179656 | tf_op jit(solution)/shard_map/ppermute | solution.py:547
  41.5 12.4 %collective-permute-start.9 = (bf16[192,384]{1,0:T(8,128)(2,1)S(1)}, bf16[192,384]{1,0:T(8,128)(2,1)S(1)}, u32[]{:S(2)}, u32[]{:S(2)}) collective-permute-start(bf16[192,384]{1,0:T(8,128)(2,1)S(1)} %get-tuple-element.378), channel_id=1, source_target_pairs={{0,16},{8,24},{16,0},{24,8},{1,17},{9,25},{17,1},{25,9},{2,18},{10... | collective-permute-start | bytes 442376 | tf_op jit(solution)/shard_map/ppermute | solution.py:547
  53.9 2.4 collective-permute-start.11
  56.4 19.6 %collective-permute-start.12 = (bf16[512,768]{1,0:T(8,128)(2,1)S(1)}, bf16[512,768]{1,0:T(8,128)(2,1)S(1)}, u32[]{:S(2)}, u32[]{:S(2)}) collective-permute-start(bf16[512,768]{1,0:T(8,128)(2,1)S(1)} %add_convert_fusion.5.partial_ref), channel_id=1, source_target_pairs={{0,2},{1,3},{2,0},{3,1},{4,6},{5,7},{6,4},{7,5},{8,10},{9,11},{10,... | collective-permute-start | bytes 2359304 | tf_op jit(solution)/shard_map/ppermute | solution.py:547
  57.1 21.5 %collective-permute-start.14 = (bf16[384,768]{1,0:T(8,128)(2,1)S(1)}, bf16[384,768]{1,0:T(8,128)(2,1)S(1)}, u32[]{:S(2)}, u32[]{:S(2)}) collective-permute-start(bf16[384,768]{1,0:T(8,128)(2,1)S(1)} %maximum_maximum_fusion.refs_4_.refs_5_), channel_id=1, source_target_pairs={{0,8},{8,0},{16,24},{24,16},{1,9},{9,1},{17,25},{25,17},{2,10},{10... | collective-permute-start | bytes 1769480 | tf_op jit(solution)/shard_map/ppermute | solution.py:547
  57.6 20.9 %collective-permute-start.13 = (bf16[768,384]{1,0:T(8,128)(2,1)S(1)}, bf16[768,384]{1,0:T(8,128)(2,1)S(1)}, u32[]{:S(2)}, u32[]{:S(2)}) collective-permute-start(bf16[768,384]{1,0:T(8,128)(2,1)S(1)} %pad_maximum_fusion.4.refs_2_.refs_3_), channel_id=1, source_target_pairs={{0,4},{4,0},{1,5},{5,1},{2,6},{6,2},{3,7},{7,3},{8,12},{12,8},{9,1... | collective-permute-start | bytes 1769480 | tf_op jit(solution)/shard_map/ppermute | solution.py:547
  59.2 18.0 %collective-permute-start.15 = (bf16[192,768]{1,0:T(8,128)(2,1)S(1)}, bf16[192,768]{1,0:T(8,128)(2,1)S(1)}, u32[]{:S(2)}, u32[]{:S(2)}) collective-permute-start(bf16[192,768]{1,0:T(8,128)(2,1)S(1)} %prepare_attend.1), channel_id=1, source_target_pairs={{0,16},{8,24},{16,0},{24,8},{1,17},{9,25},{17,1},{25,9},{2,18},{10... | collective-permute-start | bytes 884744 | tf_op jit(solution)/shard_map/ppermute | solution.py:547
  82.9 2.4 collective-permute-start.17
  85.4 19.8 %collective-permute-start.18 = (bf16[512,768]{1,0:T(8,128)(2,1)S(1)}, bf16[512,768]{1,0:T(8,128)(2,1)S(1)}, u32[]{:S(2)}, u32[]{:S(2)}) collective-permute-start(bf16[512,768]{1,0:T(8,128)(2,1)S(1)} %add_convert_fusion.4.partial_ref), channel_id=1, source_target_pairs={{0,2},{1,3},{2,0},{3,1},{4,6},{5,7},{6,4},{7,5},{8,10},{9,11},{10,... | collective-permute-start | bytes 2359304 | tf_op jit(solution)/shard_map/ppermute | solution.py:547
  87.0 21.6 %collective-permute-start.19 = (bf16[384,768]{1,0:T(8,128)(2,1)S(1)}, bf16[384,768]{1,0:T(8,128)(2,1)S(1)}, u32[]{:S(2)}, u32[]{:S(2)}) collective-permute-start(bf16[384,768]{1,0:T(8,128)(2,1)S(1)} %constant_dynamic-update-slice_fusion.refs_5_.refs_6_), channel_id=1, source_target_pairs={{0,8},{8,0},{16,24},{24,16},{1,9},{9,1},{17,25},{25,17},{2,10},{10... | collective-permute-start | bytes 1769480 | tf_op jit(solution)/shard_map/ppermute | solution.py:547
  87.9 18.5 %collective-permute-start.20 = (bf16[192,384]{1,0:T(8,128)(2,1)S(1)}, bf16[192,384]{1,0:T(8,128)(2,1)S(1)}, u32[]{:S(2)}, u32[]{:S(2)}) collective-permute-start(bf16[192,384]{1,0:T(8,128)(2,1)S(1)} %get-tuple-element.375), channel_id=1, source_target_pairs={{0,16},{8,24},{16,0},{24,8},{1,17},{9,25},{17,1},{25,9},{2,18},{10... | collective-permute-start | bytes 442376 | tf_op jit(solution)/shard_map/ppermute | solution.py:547
  88.7 18.2 %collective-permute-start.21 = (bf16[192,384]{1,0:T(8,128)(2,1)S(1)}, bf16[192,384]{1,0:T(8,128)(2,1)S(1)}, u32[]{:S(2)}, u32[]{:S(2)}) collective-permute-start(bf16[192,384]{1,0:T(8,128)(2,1)S(1)} %get-tuple-element.374), channel_id=1, source_target_pairs={{0,16},{8,24},{16,0},{24,8},{1,17},{9,25},{17,1},{25,9},{2,18},{10... | collective-permute-start | bytes 442376 | tf_op jit(solution)/shard_map/ppermute | solution.py:547
  108.8 12.6 %collective-permute-start.23 = (bf16[384,384]{1,0:T(8,128)(2,1)S(1)}, bf16[384,384]{1,0:T(8,128)(2,1)S(1)}, u32[]{:S(2)}, u32[]{:S(2)}) collective-permute-start(bf16[384,384]{1,0:T(8,128)(2,1)S(1)} %pad_maximum_fusion.11), channel_id=1, source_target_pairs={{0,8},{8,0},{16,24},{24,16},{1,9},{9,1},{17,25},{25,17},{2,10},{10... | collective-permute-start | bytes 884744 | tf_op jit(solution)/shard_map/ppermute | solution.py:547
  110.0 10.1 %collective-permute-start.24 = (bf16[192,384]{1,0:T(8,128)(2,1)S(1)}, bf16[192,384]{1,0:T(8,128)(2,1)S(1)}, u32[]{:S(2)}, u32[]{:S(2)}) collective-permute-start(bf16[192,384]{1,0:T(8,128)(2,1)S(1)} %get-tuple-element.372), channel_id=1, source_target_pairs={{0,16},{8,24},{16,0},{24,8},{1,17},{9,25},{17,1},{25,9},{2,18},{10... | collective-permute-start | bytes 442376 | tf_op jit(solution)/shard_map/ppermute | solution.py:547
  121.5 23.1 %collective-permute-start.29 = (bf16[512,768]{1,0:T(8,128)(2,1)S(1)}, bf16[512,768]{1,0:T(8,128)(2,1)S(1)}, u32[]{:S(2)}, u32[]{:S(2)}) collective-permute-start(bf16[512,768]{1,0:T(8,128)(2,1)S(1)} %pad_maximum_fusion.1.refs_1_.skip_ref), channel_id=1, source_target_pairs={{0,1},{1,0},{2,3},{3,2},{4,5},{5,4},{6,7},{7,6},{8,9},{9,8},{10,11... | collective-permute-start | bytes 2359304 | tf_op jit(solution)/shard_map/ppermute | solution.py:547
  123.9 19.6 %collective-permute-start.26 = (bf16[512,768]{1,0:T(8,128)(2,1)S(1)}, bf16[512,768]{1,0:T(8,128)(2,1)S(1)}, u32[]{:S(2)}, u32[]{:S(2)}) collective-permute-start(bf16[512,768]{1,0:T(8,128)(2,1)S(1)} %add_convert_fusion.3.partial_ref), channel_id=1, source_target_pairs={{0,2},{1,3},{2,0},{3,1},{4,6},{5,7},{6,4},{7,5},{8,10},{9,11},{10,... | collective-permute-start | bytes 2359304 | tf_op jit(solution)/shard_map/ppermute | solution.py:547
  124.7 19.9 %collective-permute-start.28 = (bf16[384,768]{1,0:T(8,128)(2,1)S(1)}, bf16[384,768]{1,0:T(8,128)(2,1)S(1)}, u32[]{:S(2)}, u32[]{:S(2)}) collective-permute-start(bf16[384,768]{1,0:T(8,128)(2,1)S(1)} %maximum_maximum_fusion.1.refs_5_.refs_4_), channel_id=1, source_target_pairs={{0,8},{8,0},{16,24},{24,16},{1,9},{9,1},{17,25},{25,17},{2,10},{10... | collective-permute-start | bytes 1769480 | tf_op jit(solution)/shard_map/ppermute | solution.py:547
  127.3 17.4 %collective-permute-start.27 = (bf16[768,384]{1,0:T(8,128)(2,1)S(1)}, bf16[768,384]{1,0:T(8,128)(2,1)S(1)}, u32[]{:S(2)}, u32[]{:S(2)}) collective-permute-start(bf16[768,384]{1,0:T(8,128)(2,1)S(1)} %pad_maximum_fusion.5.refs_3_.refs_2_), channel_id=1, source_target_pairs={{0,4},{4,0},{1,5},{5,1},{2,6},{6,2},{3,7},{7,3},{8,12},{12,8},{9,1... | collective-permute-start | bytes 1769480 | tf_op jit(solution)/shard_map/ppermute | solution.py:547
  144.6 2.4 collective-permute-start.30
  149.8 4.3 %collective-permute-start.31 = (bf16[512,768]{1,0:T(8,128)(2,1)S(1)}, bf16[512,768]{1,0:T(8,128)(2,1)S(1)}, u32[]{:S(2)}, u32[]{:S(2)}) collective-permute-start(bf16[512,768]{1,0:T(8,128)(2,1)S(1)} %get-tuple-element.255), channel_id=1, source_target_pairs={{0,1},{1,0},{2,3},{3,2},{4,5},{5,4},{6,7},{7,6},{8,9},{9,8},{10,11... | collective-permute-start | bytes 2359304 | tf_op jit(solution)/shard_map/ppermute | solution.py:547
  154.4 19.9 %collective-permute-start.32 = (bf16[512,768]{1,0:T(8,128)(2,1)S(1)}, bf16[512,768]{1,0:T(8,128)(2,1)S(1)}, u32[]{:S(2)}, u32[]{:S(2)}) collective-permute-start(bf16[512,768]{1,0:T(8,128)(2,1)S(1)} %add_convert_fusion.2.partial_ref), channel_id=1, source_target_pairs={{0,2},{1,3},{2,0},{3,1},{4,6},{5,7},{6,4},{7,5},{8,10},{9,11},{10,... | collective-permute-start | bytes 2359304 | tf_op jit(solution)/shard_map/ppermute | solution.py:547
  156.5 19.3 %collective-permute-start.34 = (bf16[768,384]{1,0:T(8,128)(2,1)S(1)}, bf16[768,384]{1,0:T(8,128)(2,1)S(1)}, u32[]{:S(2)}, u32[]{:S(2)}) collective-permute-start(bf16[768,384]{1,0:T(8,128)(2,1)S(1)} %slice.339), channel_id=1, source_target_pairs={{0,4},{4,0},{1,5},{5,1},{2,6},{6,2},{3,7},{7,3},{8,12},{12,8},{9,1... | collective-permute-start | bytes 1769480 | tf_op jit(solution)/shard_map/ppermute | solution.py:547
  158.1 17.7 %collective-permute-start.33 = (bf16[384,768]{1,0:T(8,128)(2,1)S(1)}, bf16[384,768]{1,0:T(8,128)(2,1)S(1)}, u32[]{:S(2)}, u32[]{:S(2)}) collective-permute-start(bf16[384,768]{1,0:T(8,128)(2,1)S(1)} %slice.278), channel_id=1, source_target_pairs={{0,8},{8,0},{16,24},{24,16},{1,9},{9,1},{17,25},{25,17},{2,10},{10... | collective-permute-start | bytes 1769480 | tf_op jit(solution)/shard_map/ppermute | solution.py:547
  176.1 12.0 %collective-permute-start.36 = (bf16[384,384]{1,0:T(8,128)(2,1)S(1)}, bf16[384,384]{1,0:T(8,128)(2,1)S(1)}, u32[]{:S(2)}, u32[]{:S(2)}) collective-permute-start(bf16[384,384]{1,0:T(8,128)(2,1)S(1)} %slice.447), channel_id=1, source_target_pairs={{0,8},{8,0},{16,24},{24,16},{1,9},{9,1},{17,25},{25,17},{2,10},{10... | collective-permute-start | bytes 884744 | tf_op jit(solution)/shard_map/ppermute | solution.py:547
  190.7 19.8 %collective-permute-start.38 = (bf16[512,768]{1,0:T(8,128)(2,1)S(1)}, bf16[512,768]{1,0:T(8,128)(2,1)S(1)}, u32[]{:S(2)}, u32[]{:S(2)}) collective-permute-start(bf16[512,768]{1,0:T(8,128)(2,1)S(1)} %add_convert_fusion.1.partial_ref), channel_id=1, source_target_pairs={{0,2},{1,3},{2,0},{3,1},{4,6},{5,7},{6,4},{7,5},{8,10},{9,11},{10,... | collective-permute-start | bytes 2359304 | tf_op jit(solution)/shard_map/ppermute | solution.py:547
  192.3 23.9 %collective-permute-start.41 = (bf16[768,384]{1,0:T(8,128)(2,1)S(1)}, bf16[768,384]{1,0:T(8,128)(2,1)S(1)}, u32[]{:S(2)}, u32[]{:S(2)}) collective-permute-start(bf16[768,384]{1,0:T(8,128)(2,1)S(1)} %broadcast_select_fusion.1), channel_id=1, source_target_pairs={{0,4},{4,0},{1,5},{5,1},{2,6},{6,2},{3,7},{7,3},{8,12},{12,8},{9,1... | collective-permute-start | bytes 1769480 | tf_op jit(solution)/shard_map/ppermute | solution.py:547
  193.9 22.2 %collective-permute-start.40 = (bf16[192,768]{1,0:T(8,128)(2,1)S(1)}, bf16[192,768]{1,0:T(8,128)(2,1)S(1)}, u32[]{:S(2)}, u32[]{:S(2)}) collective-permute-start(bf16[192,768]{1,0:T(8,128)(2,1)S(1)} %slice.446), channel_id=1, source_target_pairs={{0,16},{8,24},{16,0},{24,8},{1,17},{9,25},{17,1},{25,9},{2,18},{10... | collective-permute-start | bytes 884744 | tf_op jit(solution)/shard_map/ppermute | solution.py:547
  195.5 20.6 %collective-permute-start.39 = (bf16[192,384]{1,0:T(8,128)(2,1)S(1)}, bf16[192,384]{1,0:T(8,128)(2,1)S(1)}, u32[]{:S(2)}, u32[]{:S(2)}) collective-permute-start(bf16[192,384]{1,0:T(8,128)(2,1)S(1)} %slice.451), channel_id=1, source_target_pairs={{0,16},{8,24},{16,0},{24,8},{1,17},{9,25},{17,1},{25,9},{2,18},{10... | collective-permute-start | bytes 442376 | tf_op jit(solution)/shard_map/ppermute | solution.py:547
  221.1 4.7 %collective-permute-start.43 = (bf16[512,768]{1,0:T(8,128)(2,1)S(1)}, bf16[512,768]{1,0:T(8,128)(2,1)S(1)}, u32[]{:S(2)}, u32[]{:S(2)}) collective-permute-start(bf16[512,768]{1,0:T(8,128)(2,1)S(1)} %get-tuple-element.284), channel_id=1, source_target_pairs={{0,1},{1,0},{2,3},{3,2},{4,5},{5,4},{6,7},{7,6},{8,9},{9,8},{10,11... | collective-permute-start | bytes 2359304 | tf_op jit(solution)/shard_map/ppermute | solution.py:547
  226.0 19.9 %collective-permute-start.44 = (bf16[512,768]{1,0:T(8,128)(2,1)S(1)}, bf16[512,768]{1,0:T(8,128)(2,1)S(1)}, u32[]{:S(2)}, u32[]{:S(2)}) collective-permute-start(bf16[512,768]{1,0:T(8,128)(2,1)S(1)} %add_convert_fusion.partial_ref), channel_id=1, source_target_pairs={{0,2},{1,3},{2,0},{3,1},{4,6},{5,7},{6,4},{7,5},{8,10},{9,11},{10,... | collective-permute-start | bytes 2359304 | tf_op jit(solution)/shard_map/ppermute | solution.py:547
  228.4 19.2 %collective-permute-start.47 = (bf16[768,384]{1,0:T(8,128)(2,1)S(1)}, bf16[768,384]{1,0:T(8,128)(2,1)S(1)}, u32[]{:S(2)}, u32[]{:S(2)}) collective-permute-start(bf16[768,384]{1,0:T(8,128)(2,1)S(1)} %slice.347), channel_id=1, source_target_pairs={{0,4},{4,0},{1,5},{5,1},{2,6},{6,2},{3,7},{7,3},{8,12},{12,8},{9,1... | collective-permute-start | bytes 1769480 | tf_op jit(solution)/shard_map/ppermute | solution.py:547
  229.0 21.4 %collective-permute-start.46 = (bf16[384,768]{1,0:T(8,128)(2,1)S(1)}, bf16[384,768]{1,0:T(8,128)(2,1)S(1)}, u32[]{:S(2)}, u32[]{:S(2)}) collective-permute-start(bf16[384,768]{1,0:T(8,128)(2,1)S(1)} %slice.289), channel_id=1, source_target_pairs={{0,8},{8,0},{16,24},{24,16},{1,9},{9,1},{17,25},{25,17},{2,10},{10... | collective-permute-start | bytes 1769480 | tf_op jit(solution)/shard_map/ppermute | solution.py:547
  229.1 59.3 %collective-permute-start.60 = (bf16[512,768]{1,0:T(8,128)(2,1)S(1)}, bf16[512,768]{1,0:T(8,128)(2,1)S(1)}, u32[]{:S(2)}, u32[]{:S(2)}) collective-permute-start(bf16[512,768]{1,0:T(8,128)(2,1)S(1)} %feed_forward.6), channel_id=1, source_target_pairs={{0,1},{1,0},{2,3},{3,2},{4,5},{5,4},{6,7},{7,6},{8,9},{9,8},{10,11... | collective-permute-start | bytes 2359304 | tf_op jit(solution)/shard_map/ppermute | solution.py:547
  229.3 21.2 %collective-permute-start.45 = (bf16[384,384]{1,0:T(8,128)(2,1)S(1)}, bf16[384,384]{1,0:T(8,128)(2,1)S(1)}, u32[]{:S(2)}, u32[]{:S(2)}) collective-permute-start(bf16[384,384]{1,0:T(8,128)(2,1)S(1)} %slice.445), channel_id=1, source_target_pairs={{0,8},{8,0},{16,24},{24,16},{1,9},{9,1},{17,25},{25,17},{2,10},{10... | collective-permute-start | bytes 884744 | tf_op jit(solution)/shard_map/ppermute | solution.py:547
  250.6 31.7 %collective-permute-start.55 = (bf16[192,1152]{1,0:T(8,128)(2,1)S(1)}, bf16[192,1152]{1,0:T(8,128)(2,1)S(1)}, u32[]{:S(2)}, u32[]{:S(2)}) collective-permute-start(bf16[192,1152]{1,0:T(8,128)(2,1)S(1)} %get-tuple-element.391), channel_id=1, source_target_pairs={{0,4},{4,0},{1,5},{5,1},{2,6},{6,2},{3,7},{7,3},{8,12},{12,8},{9,1... | collective-permute-start | bytes 1327112 | tf_op jit(solution)/shard_map/ppermute | solution.py:547
  252.2 2.8 collective-permute-start.48
  252.4 12.6 %collective-permute-start.51 = (bf16[384,384]{1,0:T(8,128)(2,1)S(1)}, bf16[384,384]{1,0:T(8,128)(2,1)S(1)}, u32[]{:S(2)}, u32[]{:S(2)}) collective-permute-start(bf16[384,384]{1,0:T(8,128)(2,1)S(1)} %slice.444), channel_id=1, source_target_pairs={{0,8},{8,0},{16,24},{24,16},{1,9},{9,1},{17,25},{25,17},{2,10},{10... | collective-permute-start | bytes 884744 | tf_op jit(solution)/shard_map/ppermute | solution.py:547
  252.8 11.8 %collective-permute-start.50 = (bf16[192,384]{1,0:T(8,128)(2,1)S(1)}, bf16[192,384]{1,0:T(8,128)(2,1)S(1)}, u32[]{:S(2)}, u32[]{:S(2)}) collective-permute-start(bf16[192,384]{1,0:T(8,128)(2,1)S(1)} %slice.450), channel_id=1, source_target_pairs={{0,16},{8,24},{16,0},{24,8},{1,17},{9,25},{17,1},{25,9},{2,18},{10... | collective-permute-start | bytes 442376 | tf_op jit(solution)/shard_map/ppermute | solution.py:547
  265.0 2.9 collective-permute-start.52
  267.4 16.2 %collective-permute-start.49 = (bf16[768,384]{1,0:T(8,128)(2,1)S(1)}, bf16[768,384]{1,0:T(8,128)(2,1)S(1)}, u32[]{:S(2)}, u32[]{:S(2)}) collective-permute-start(bf16[768,384]{1,0:T(8,128)(2,1)S(1)} %broadcast_select_fusion), channel_id=1, source_target_pairs={{0,4},{4,0},{1,5},{5,1},{2,6},{6,2},{3,7},{7,3},{8,12},{12,8},{9,1... | collective-permute-start | bytes 1769480 | tf_op jit(solution)/shard_map/ppermute | solution.py:547
  268.0 11.3 %collective-permute-start.53 = (bf16[256,768]{1,0:T(8,128)(2,1)S(1)}, bf16[256,768]{1,0:T(8,128)(2,1)S(1)}, u32[]{:S(2)}, u32[]{:S(2)}) collective-permute-start(bf16[256,768]{1,0:T(8,128)(2,1)S(1)} %add_convert_fusion.8), channel_id=1, source_target_pairs={{0,2},{1,3},{2,0},{3,1},{4,6},{5,7},{6,4},{7,5},{8,10},{9,11},{10,... | collective-permute-start | bytes 1179656 | tf_op jit(solution)/shard_map/ppermute | solution.py:547
  269.5 23.3 %collective-permute-start.58 = (bf16[192,768]{1,0:T(8,128)(2,1)S(1)}, bf16[192,768]{1,0:T(8,128)(2,1)S(1)}, u32[]{:S(2)}, u32[]{:S(2)}) collective-permute-start(bf16[192,768]{1,0:T(8,128)(2,1)S(1)} %slice.442), channel_id=1, source_target_pairs={{0,16},{8,24},{16,0},{24,8},{1,17},{9,25},{17,1},{25,9},{2,18},{10... | collective-permute-start | bytes 884744 | tf_op jit(solution)/shard_map/ppermute | solution.py:547
  280.8 4.3 %collective-permute-start.54 = (f32[16,768]{1,0:T(8,128)S(1)}, f32[16,768]{1,0:T(8,128)S(1)}, u32[]{:S(2)}, u32[]{:S(2)}) collective-permute-start(f32[16,768]{1,0:T(8,128)S(1)} %get-tuple-element.306), channel_id=1, source_target_pairs={{0,1},{1,0},{2,3},{3,2},{4,5},{5,4},{6,7},{7,6},{8,9},{9,8},{10,11... | collective-permute-start | bytes 147464 | tf_op jit(solution)/shard_map/ppermute | solution.py:547
  282.3 10.5 %collective-permute-start.57 = (bf16[192,384]{1,0:T(8,128)(2,1)S(1)}, bf16[192,384]{1,0:T(8,128)(2,1)S(1)}, u32[]{:S(2)}, u32[]{:S(2)}) collective-permute-start(bf16[192,384]{1,0:T(8,128)(2,1)S(1)} %slice.449), channel_id=1, source_target_pairs={{0,16},{8,24},{16,0},{24,8},{1,17},{9,25},{17,1},{25,9},{2,18},{10... | collective-permute-start | bytes 442376 | tf_op jit(solution)/shard_map/ppermute | solution.py:547
  283.6 9.2 %collective-permute-start.61 = (bf16[128,768]{1,0:T(8,128)(2,1)S(1)}, bf16[128,768]{1,0:T(8,128)(2,1)S(1)}, u32[]{:S(2)}, u32[]{:S(2)}) collective-permute-start(bf16[128,768]{1,0:T(8,128)(2,1)S(1)} %slice_select_fusion.1), channel_id=1, source_target_pairs={{0,4},{4,0},{1,5},{5,1},{2,6},{6,2},{3,7},{7,3},{8,12},{12,8},{9,1... | collective-permute-start | bytes 589832 | tf_op jit(solution)/shard_map/ppermute | solution.py:547
  285.1 7.7 %collective-permute-start.59 = (f32[16,768]{1,0:T(8,128)S(1)}, f32[16,768]{1,0:T(8,128)S(1)}, u32[]{:S(2)}, u32[]{:S(2)}) collective-permute-start(f32[16,768]{1,0:T(8,128)S(1)} %add.148), channel_id=1, source_target_pairs={{0,2},{1,3},{2,0},{3,1},{4,6},{5,7},{6,4},{7,5},{8,10},{9,11},{10,... | collective-permute-start | bytes 147464 | tf_op jit(solution)/shard_map/ppermute | solution.py:547
  288.4 10.5 %collective-permute-start.56 = (bf16[384,384]{1,0:T(8,128)(2,1)S(1)}, bf16[384,384]{1,0:T(8,128)(2,1)S(1)}, u32[]{:S(2)}, u32[]{:S(2)}) collective-permute-start(bf16[384,384]{1,0:T(8,128)(2,1)S(1)} %slice.443), channel_id=1, source_target_pairs={{0,8},{8,0},{16,24},{24,16},{1,9},{9,1},{17,25},{25,17},{2,10},{10... | collective-permute-start | bytes 884744 | tf_op jit(solution)/shard_map/ppermute | solution.py:547
  293.0 11.1 %collective-permute-start.64 = (bf16[256,768]{1,0:T(8,128)(2,1)S(1)}, bf16[256,768]{1,0:T(8,128)(2,1)S(1)}, u32[]{:S(2)}, u32[]{:S(2)}) collective-permute-start(bf16[256,768]{1,0:T(8,128)(2,1)S(1)} %add_convert_fusion.7), channel_id=1, source_target_pairs={{0,2},{1,3},{2,0},{3,1},{4,6},{5,7},{6,4},{7,5},{8,10},{9,11},{10,... | collective-permute-start | bytes 1179656 | tf_op jit(solution)/shard_map/ppermute | solution.py:547
  294.9 10.0 %collective-permute-start.63 = (f32[256,256]{1,0:T(8,128)S(1)}, f32[256,256]{1,0:T(8,128)S(1)}, u32[]{:S(2)}, u32[]{:S(2)}) collective-permute-start(f32[256,256]{1,0:T(8,128)S(1)} %pack_grads.1), channel_id=1, source_target_pairs={{0,4},{4,0},{1,5},{5,1},{2,6},{6,2},{3,7},{7,3},{8,12},{12,8},{9,1... | collective-permute-start | bytes 786440 | tf_op jit(solution)/shard_map/ppermute | solution.py:547
  299.1 17.5 %collective-permute-start.69 = (bf16[192,1536]{1,0:T(8,128)(2,1)S(1)}, bf16[192,1536]{1,0:T(8,128)(2,1)S(1)}, u32[]{:S(2)}, u32[]{:S(2)}) collective-permute-start(bf16[192,1536]{1,0:T(8,128)(2,1)S(1)} %pad_maximum_fusion.7), channel_id=1, source_target_pairs={{0,4},{4,0},{1,5},{5,1},{2,6},{6,2},{3,7},{7,3},{8,12},{12,8},{9,1... | collective-permute-start | bytes 1769480 | tf_op jit(solution)/shard_map/ppermute | solution.py:547
  300.8 8.6 %collective-permute-start.62 = (bf16[192,384]{1,0:T(8,128)(2,1)S(1)}, bf16[192,384]{1,0:T(8,128)(2,1)S(1)}, u32[]{:S(2)}, u32[]{:S(2)}) collective-permute-start(bf16[192,384]{1,0:T(8,128)(2,1)S(1)} %slice.448), channel_id=1, source_target_pairs={{0,16},{8,24},{16,0},{24,8},{1,17},{9,25},{17,1},{25,9},{2,18},{10... | collective-permute-start | bytes 442376 | tf_op jit(solution)/shard_map/ppermute | solution.py:547
  309.5 5.5 %collective-permute-start.67 = (f32[128,256]{1,0:T(8,128)S(1)}, f32[128,256]{1,0:T(8,128)S(1)}, u32[]{:S(2)}, u32[]{:S(2)}) collective-permute-start(f32[128,256]{1,0:T(8,128)S(1)} %slice.367), channel_id=1, source_target_pairs={{0,8},{8,0},{16,24},{24,16},{1,9},{9,1},{17,25},{25,17},{2,10},{10... | collective-permute-start | bytes 393224 | tf_op jit(solution)/shard_map/ppermute | solution.py:547
  309.6 13.4 %collective-permute-start.66 = (bf16[128,768]{1,0:T(8,128)(2,1)S(1)}, bf16[128,768]{1,0:T(8,128)(2,1)S(1)}, u32[]{:S(2)}, u32[]{:S(2)}) collective-permute-start(bf16[128,768]{1,0:T(8,128)(2,1)S(1)} %get-tuple-element.381), channel_id=1, source_target_pairs={{0,4},{4,0},{1,5},{5,1},{2,6},{6,2},{3,7},{7,3},{8,12},{12,8},{9,1... | collective-permute-start | bytes 589832 | tf_op jit(solution)/shard_map/ppermute | solution.py:547
  310.3 12.6 %collective-permute-start.65 = (bf16[192,384]{1,0:T(8,128)(2,1)S(1)}, bf16[192,384]{1,0:T(8,128)(2,1)S(1)}, u32[]{:S(2)}, u32[]{:S(2)}) collective-permute-start(bf16[192,384]{1,0:T(8,128)(2,1)S(1)} %fusion.101.refs_0_), channel_id=1, source_target_pairs={{0,4},{4,0},{1,5},{5,1},{2,6},{6,2},{3,7},{7,3},{8,12},{12,8},{9,1... | collective-permute-start | bytes 442376 | tf_op jit(solution)/shard_map/ppermute | solution.py:547
  315.0 8.0 %collective-permute-start.68 = (f32[64,256]{1,0:T(8,128)S(1)}, f32[64,256]{1,0:T(8,128)S(1)}, u32[]{:S(2)}, u32[]{:S(2)}) collective-permute-start(f32[64,256]{1,0:T(8,128)S(1)} %slice.368), channel_id=1, source_target_pairs={{0,16},{8,24},{16,0},{24,8},{1,17},{9,25},{17,1},{25,9},{2,18},{10... | collective-permute-start | bytes 196616 | tf_op jit(solution)/shard_map/ppermute | solution.py:547
  (16 other events, 168.0 us)

commit v3 on v2

--- a/solution.py
+++ b/solution.py
@@ -937,14 +937,11 @@
     join(refs[:count], expand_ref)
     join(refs[count:-3], reduce_ref)
 
-    def step(i, carry):
-        at = pl.ds(pl.multiple_of(i * CHUNK, CHUNK), CHUNK)
+    for first in range(0, piece.shape[0], CHUNK):
+        at = slice(first, first + CHUNK)
         hidden = jnp.dot(piece[at, :], expand_ref[...], preferred_element_type=F32)
         active = gelu_tanh(hidden + bias_ref[...]).astype(BF16)
         out[at, :] = dot_across(active, reduce_ref[...]).astype(out.dtype)
-        return carry
-
-    lax.fori_loop(0, piece.shape[0] // CHUNK, step, 0)
 
 
 def feed_rows(piece, weights, kind):
@@ -977,8 +974,8 @@
     join(refs[count:-6], reduce_ref)
     sum_ref[...] = jnp.zeros_like(sum_ref)
 
-    def step(i, carry):
-        at = pl.ds(pl.multiple_of(i * CHUNK, CHUNK), CHUNK)
+    for first in range(0, piece.shape[0], CHUNK):
+        at = slice(first, first + CHUNK)
         hidden = jnp.dot(piece[at, :], expand_ref[...], preferred_element_type=F32)
         value, slope = gelu_both(hidden + bias_ref[...])
         active_ref[at, :] = value.astype(BF16)
@@ -987,9 +984,6 @@
         hidden_ref[at, :] = grad_hidden
         sum_ref[...] += jnp.sum(grad_hidden.astype(F32), axis=0, keepdims=True)
         out[at, :] = dot_across(grad_hidden, expand_ref[...]).astype(out.dtype)
-        return carry
-
-    lax.fori_loop(0, piece.shape[0] // CHUNK, step, 0)
 
 
 def feed_back_rows(piece, grads, weights, kind):
@@ -1783,9 +1777,7 @@
     sums = sums + sums_moved
     sums_moved = cross_x(sums)
     final_arrived = cross_core(final_sent)
-    fe_moved, fr_moved, mine_at, sums_moved, final_arrived, grad_moved = pin(
-        fe_moved, fr_moved, mine_at, sums_moved, final_arrived, grad_moved
-    )
+    sums_moved, final_arrived, grad_moved = pin(sums_moved, final_arrived, grad_moved)
     final_across = cross_x(halves_added(final_kept, final_arrived))
     pack = pack_grads(
         sums + sums_moved,
@@ -1796,15 +1788,16 @@
         params[3].shape,
         params[9].shape,
     )
+    pack_moved = cross_y(pack)
+    fe_moved, fr_moved, mine_at, pack = pin(fe_moved, fr_moved, mine_at, pack)
     mine_s = beside(keep_rows(feed_e, fe_moved), keep_rows(feed_r, fr_moved), mine_at).astype(BF16)
-    pack_moved = cross_y(pack)
-    expand_grad_t, reduce_grad_t = finish_feed(mine_t, theirs_t, place, half)
-    y_moved, mine_s = pin(y_moved, mine_s)
     theirs_s = cross_y(
         beside(
             mine_s[:, :half], mine_s[:, 2 * half : 3 * half], mine_s[:, half : 2 * half], mine_s[:, 3 * half :]
         )
     )
+    late, _ = pin(mine_t, mine_s)
+    expand_grad_t, reduce_grad_t = finish_feed(late, theirs_t, place, half)
     grad_a = keep_rows(grad_a, y_moved)
     y_moved = send_rows(grad_a, cross_far)
     final_across, expand_grad_t = pin(final_across, expand_grad_t)
@@ -1827,13 +1820,14 @@
     pack_near, pack = pin(pack_near, pack)
     pack = pack[: 2 * ROWS] + pack_near
     pack_far = cross_far(pack[ROWS:])
-    theirs_a, final_moved, pack_far, output_grad_t, expand_grad_s = pin(
-        theirs_a, final_moved, pack_far, output_grad_t, expand_grad_s
-    )
-    grad_moved = grad_moved.astype(F32)
+    vectors = unpack_grads(pack, pack_far, local, params[3].shape, params[9].shape)
+    final = restore(final, final_moved)
+    theirs_a, final, first, output_grad_t, expand_grad_s = pin(
+        theirs_a, final, vectors[0], output_grad_t, expand_grad_s
+    )
+    vectors[0] = first
     merged_grad_s, output_grad_s = finish_attend((), mine_a, theirs_a, place)
-    vectors = unpack_grads(pack, pack_far, local, params[3].shape, params[9].shape)
-    outputs = [restore(final, final_moved), restore(input_grad, grad_moved)]
+    outputs = [final, restore(input_grad, grad_moved.astype(F32))]
     for vector, merged, output, expand, reduce in (
         (vectors[:8], merged_grad_s, output_grad_s, expand_grad_s, reduce_grad_s),
         (vectors[8:], merged_grad_t, output_grad_t, expand_grad_t, reduce_grad_t),

time: 331 us -> 327 us (0.988)
  transfers between devices with their start and end apart: 70 -> 70, of which waited for: 37 -> 37; matrix products, arithmetic and copies ran while one was open for 6% -> 7% of each run, Pallas kernels for 19% -> 20%
where the time goes in v3:
time: 327 us; the launch traced here: 322 us
  waiting for transfers between devices  151 us (46%)
  Pallas kernels  74.7 us (23%)
  starting transfers between devices  70.9 us (22%)
  matrix products  13.6 us (4%)
  other arithmetic  8.08 us (2%)
    ppermute x70, waiting for transfers between devices, swap(): return row_major(lax.ppermute(row_major(value), axis, route))  151 us
    ppermute x70, starting transfers between devices, swap(): return row_major(lax.ppermute(row_major(value), axis, route))  70.9 us
    pallas_call x12, Pallas kernels, call(): pl.pallas_call(body, out_shape=tuple(outputs), in_specs=[SMEM if v.ndim =...  51.8 us
    pallas_call x8, Pallas kernels, row_call(): pl.pallas_call(body, grid=(1,), out_shape=tuple(outputs), in_specs=specs,...  10.4 us
    dot_general x8, matrix products, dot_down(): lax.dot_general(left, right, (((0,), (0,)), ((), ())), preferred_element_...  9.97 us
  transfers between devices with their start and end apart: 70, of which 37 were waited for; matrix products, arithmetic and copies ran while one was open for 7% of the time, Pallas kernels for 20%

profile of v3, /device:TPU:0, one launch (start us, length us, event | category | flops | bytes accessed | tf_op | source)
XLA Modules:
  0.0 321.8 jit_solution(12160481223918174425)
XLA Ops:
  0.7 2.4 prepare_first.1.refs_0_.refs_6_
  3.1 4.1 %collective-permute-start.3 = (bf16[208,768]{1,0:T(8,128)(2,1)}, bf16[208,768]{1,0:T(8,128)(2,1)S(1)}, u32[]{:S(2)}, u32[]{:S(2)}) collective-permute-start(bf16[208,768]{1,0:T(8,128)(2,1)} %prepare_first.1.refs_0_.refs_6_), channel_id=1, source_target_pairs={{0,16},{8,24},{16,0},{24,8},{1,17},{9,25},{17,1},{25,9},{2,18},{10... | collective-permute-start | bytes 958472 | tf_op jit(solution)/shard_map/ppermute | solution.py:547
  9.0 1.6 collective-permute-start
  10.6 1.6 collective-permute-start.2
  13.5 3.9 %collective-permute-done = bf16[144,768]{1,0:T(8,128)(2,1)S(1)} collective-permute-done((bf16[144,768]{1,0:T(8,128)(2,1)S(1)}, bf16[144,768]{1,0:T(8,128)(2,1)S(1)}, u32[]{:S(2)}, u32[]{:S(2)}) %collective-permute-start) | collective-permute-done | bytes 221216 | tf_op jit(solution)/shard_map/ppermute | solution.py:547
  18.3 1.6 collective-permute-start.1
  22.0 4.1 %collective-permute-start.4 = (bf16[208,768]{1,0:T(8,128)(2,1)S(1)}, bf16[208,768]{1,0:T(8,128)(2,1)S(1)}, u32[]{:S(2)}, u32[]{:S(2)}) collective-permute-start(bf16[208,768]{1,0:T(8,128)(2,1)S(1)} %collective-permute-done.3.refs_1_.refs_7_), channel_id=1, source_target_pairs={{0,8},{8,0},{16,24},{24,16},{1,9},{9,1},{17,25},{25,17},{2,10},{10... | collective-permute-start | bytes 958472 | tf_op jit(solution)/shard_map/ppermute | solution.py:547
  27.1 10.4 %collective-permute-done.5 = bf16[192,768]{1,0:T(8,128)(2,1)S(1)} collective-permute-done((bf16[192,768]{1,0:T(8,128)(2,1)S(1)}, bf16[192,768]{1,0:T(8,128)(2,1)S(1)}, u32[]{:S(2)}, u32[]{:S(2)}) %collective-permute-start.5) | collective-permute-done | bytes 294944 | tf_op jit(solution)/shard_map/ppermute | solution.py:547
  39.9 1.6 collective-permute-start.10
  41.5 3.5 %collective-permute-start.9 = (bf16[192,384]{1,0:T(8,128)(2,1)S(1)}, bf16[192,384]{1,0:T(8,128)(2,1)S(1)}, u32[]{:S(2)}, u32[]{:S(2)}) collective-permute-start(bf16[192,384]{1,0:T(8,128)(2,1)S(1)} %get-tuple-element.372), channel_id=1, source_target_pairs={{0,16},{8,24},{16,0},{24,8},{1,17},{9,25},{17,1},{25,9},{2,18},{10... | collective-permute-start | bytes 442376 | tf_op jit(solution)/shard_map/ppermute | solution.py:547
  45.8 7.8 %attention_forward.2 = (bf16[512,768]{1,0:T(8,128)(2,1)S(1)}, f32[512,768]{1,0:T(8,128)S(1)}, bf16[9,1024,64]{2,1,0:T(8,128)(2,1)S(1)}, bf16[1024,192]{1,0:T(8,1...) custom-call(s32[1]{0:T(128)} %bitcast.refs_0_, ...), custom_call_target="tpu_custom_call" | custom-call | flops 1610612736 | bytes 8399108 | tf_op jit(solution)/shard_map/attention_forward/pallas_call | solution.py:840
  53.7 2.3 collective-permute-done.11
  57.6 1.6 collective-permute-start.13
  59.2 1.7 collective-permute-start.15
  60.9 14.9 %collective-permute-done.12.across_ref = bf16[512,768]{1,0:T(8,128)(2,1)S(1)} collective-permute-done((bf16[512,768]{1,0:T(8,128)(2,1)S(1)}, bf16[512,768]{1,0:T(8,128)(2,1)S(1)}, u32[]{:S(2)}, u32[]{:S(2)}) %collective-permute-start.12) | collective-permute-done | bytes 786464 | tf_op jit(solution)/shard_map/ppermute | solution.py:547
  78.3 2.3 collective-permute-done.16.refs_0_
  80.6 1.7 feed_forward.5
  82.4 1.7 feed_forward.4
  84.8 1.6 collective-permute-start.18
  88.1 2.4 collective-permute-start.21
  90.4 14.0 %collective-permute-done.18.across_ref = bf16[512,768]{1,0:T(8,128)(2,1)S(1)} collective-permute-done((bf16[512,768]{1,0:T(8,128)(2,1)S(1)}, bf16[512,768]{1,0:T(8,128)(2,1)S(1)}, u32[]{:S(2)}, u32[]{:S(2)}) %collective-permute-start.18) | collective-permute-done | bytes 786464 | tf_op jit(solution)/shard_map/ppermute | solution.py:547
  106.3 1.5 collective-permute-done.19.refs_6_.refs_7_
  110.2 7.3 %attention_forward.3 = (bf16[512,768]{1,0:T(8,128)(2,1)S(1)}, f32[512,768]{1,0:T(8,128)S(1)}, bf16[9,1024,64]{2,1,0:T(8,128)(2,1)S(1)}, bf16[1024,192]{1,0:T(8,128)(2,1)S(1)}, f32[3,1,1024]{2,1,0:T(1,128)S(1)}) custom-call(s32[1]{0:T(128)} %bitcast.refs_0_, bf16[512,768]{1,0:T(8,128)(2,1)S(1)} %get-tuple-element.233.refs_1_, ...), custom_call_target="tpu_custom_call" | custom-call | flops 1610612736 | bytes 6703364 | tf_op jit(solution)/shard_map/attention_forward/pallas_call | solution.py:840
  117.5 1.8 collective-permute-done.24
  121.2 1.7 collective-permute-done.25
  123.9 2.7 collective-permute-start.28
  126.7 1.6 collective-permute-start.27
  128.3 14.5 %collective-permute-done.26.across_ref = bf16[512,768]{1,0:T(8,128)(2,1)S(1)} collective-permute-done((bf16[512,768]{1,0:T(8,128)(2,1)S(1)}, bf16[512,768]{1,0:T(8,128)(2,1)S(1)}, u32[]{:S(2)}, u32[]{:S(2)}) %collective-permute-start.26) | collective-permute-done | bytes 786464 | tf_op jit(solution)/shard_map/ppermute | solution.py:547
  144.3 2.3 collective-permute-done.30.refs_0_
  146.6 2.7 feed_backward.5
  149.5 2.7 feed_backward.4
  156.1 1.6 collective-permute-start.34
  157.7 2.7 collective-permute-start.33
  160.4 1.6 feed_forward.7
  162.1 1.6 feed_forward.6
  163.7 10.0 %collective-permute-done.32.across_ref = bf16[512,768]{1,0:T(8,128)(2,1)S(1)} collective-permute-done((bf16[512,768]{1,0:T(8,128)(2,1)S(1)}, bf16[512,768]{1,0:T(8,128)(2,1)S(1)}, u32[]{:S(2)}, u32[]{:S(2)}) %collective-permute-start.32) | collective-permute-done | bytes 786464 | tf_op jit(solution)/shard_map/ppermute | solution.py:547
  173.7 1.7 norm_back_near.3
  175.7 1.9 collective-permute-start.36
  177.8 9.6 %attention_backward.2 = (bf16[512,768]{1,0:T(8,128)(2,1)S(1)}, f32[512,768]{1,0:T(8,128)S(1)}, bf16[1024,576]{1,0:T(8,128)(2,1)S(1)}, f32[1,576]{1,0:T(1,128)S(1)}) custom-call(s32[1]{0:T(128)} %bitcast.refs_0_, bf16[512,768]{1,0:T(8,128)(2,1)S(1)} %get-tuple-element.263.refs_1_, bf16[512,768]{1,0:T(8,128)(2,1)S(1)} %collective-permute-done.35.refs_2_, ...), custom_call_target="tpu_custom_call" | custom-call | flops 4026531840 | bytes 7489796 | tf_op jit(solution)/shard_map/attention_backward/pallas_call | solution.py:840
  189.9 1.6 collective-permute-start.38
  191.8 1.6 collective-permute-start.41
  193.4 1.5 collective-permute-start.40
  196.5 13.2 %collective-permute-done.38.across_ref = bf16[512,768]{1,0:T(8,128)(2,1)S(1)} collective-permute-done((bf16[512,768]{1,0:T(8,128)(2,1)S(1)}, bf16[512,768]{1,0:T(8,128)(2,1)S(1)}, u32[]{:S(2)}, u32[]{:S(2)}) %collective-permute-start.38) | collective-permute-done | bytes 786464 | tf_op jit(solution)/shard_map/ppermute | solution.py:547
  209.7 1.7 norm_back_near.4
  211.4 4.2 %collective-permute-done.39 = bf16[192,384]{1,0:T(8,128)(2,1)S(1)} collective-permute-done((bf16[192,384]{1,0:T(8,128)(2,1)S(1)}, bf16[192,384]{1,0:T(8,128)(2,1)S(1)}, u32[]{:S(2)}, u32[]{:S(2)}) %collective-permute-start.39) | collective-permute-done | bytes 147488 | tf_op jit(solution)/shard_map/ppermute | solution.py:547
  215.6 2.3 collective-permute-done.42.refs_1_
  217.9 2.7 feed_backward.7
  220.8 2.7 feed_backward.6
  228.5 2.1 collective-permute-start.45
  230.7 14.7 %collective-permute-done.44.across_ref = bf16[512,768]{1,0:T(8,128)(2,1)S(1)} collective-permute-done((bf16[512,768]{1,0:T(8,128)(2,1)S(1)}, bf16[512,768]{1,0:T(8,128)(2,1)S(1)}, u32[]{:S(2)}, u32[]{:S(2)}) %collective-permute-start.44) | collective-permute-done | bytes 786464 | tf_op jit(solution)/shard_map/ppermute | solution.py:547
  246.9 2.8 collective-permute-done.45
  250.3 2.0 collective-permute-start.50
  252.4 1.6 collective-permute-start.55
  254.1 9.8 %attention_backward.3 = (bf16[512,768]{1,0:T(8,128)(2,1)S(1)}, f32[512,768]{1,0:T(8,128)S(1)}, bf16[1024,576]{1,0:T(8,128)(2,1)S(1)}, f32[1,576]{1,0:T(1,128)S(1)}) custom-call(s32[1]{0:T(128)} %bitcast.refs_0_, bf16[512,768]{1,0:T(8,128)(2,1)S(1)} %get-tuple-element.292.refs_1_, bf16[512,768]{1,0:T(8,128)(2,1)S(1)} %collective-permute-done.48.refs_2_, ...), custom_call_target="tpu_custom_call" | custom-call | flops 4026531840 | bytes 7588100 | tf_op jit(solution)/shard_map/attention_backward/pallas_call | solution.py:840
  270.2 7.7 %collective-permute-done.53.refs_6_ = bf16[256,768]{1,0:T(8,128)(2,1)S(1)} collective-permute-done((bf16[256,768]{1,0:T(8,128)(2,1)S(1)}, bf16[256,768]{1,0:T(8,128)(2,1)S(1)}, u32[]{:S(2)}, u32[]{:S(2)}) %collective-permute-start.53) | collective-permute-done | bytes 393248 | tf_op jit(solution)/shard_map/ppermute | solution.py:547
  281.9 1.7 collective-permute-done.49
  285.2 1.6 finish_feed.2
  293.8 3.7 %collective-permute-done.56 = bf16[384,384]{1,0:T(8,128)(2,1)S(1)} collective-permute-done((bf16[384,384]{1,0:T(8,128)(2,1)S(1)}, bf16[384,384]{1,0:T(8,128)(2,1)S(1)}, u32[]{:S(2)}, u32[]{:S(2)}) %collective-permute-start.56) | collective-permute-done | bytes 294944 | tf_op jit(solution)/shard_map/ppermute | solution.py:547
  297.9 5.8 %collective-permute-done.62 = bf16[256,768]{1,0:T(8,128)(2,1)S(1)} collective-permute-done((bf16[256,768]{1,0:T(8,128)(2,1)S(1)}, bf16[256,768]{1,0:T(8,128)(2,1)S(1)}, u32[]{:S(2)}, u32[]{:S(2)}) %collective-permute-start.62) | collective-permute-done | bytes 393248 | tf_op jit(solution)/shard_map/ppermute | solution.py:547
  304.5 2.5 collective-permute-done.57
  309.3 3.2 collective-permute-done.67
  314.1 1.6 finish_attend.2
  315.8 1.6 finish_feed.3
  319.7 1.6 finish_attend.3
  (228 shorter events, 68.3 us)
Async XLA Ops:
  3.1 18.8 %collective-permute-start.3 = (bf16[208,768]{1,0:T(8,128)(2,1)}, bf16[208,768]{1,0:T(8,128)(2,1)S(1)}, u32[]{:S(2)}, u32[]{:S(2)}) collective-permute-start(bf16[208,768]{1,0:T(8,128)(2,1)} %prepare_first.1.refs_0_.refs_6_), channel_id=1, source_target_pairs={{0,16},{8,24},{16,0},{24,8},{1,17},{9,25},{17,1},{25,9},{2,18},{10... | collective-permute-start | bytes 958472 | tf_op jit(solution)/shard_map/ppermute | solution.py:547
  9.0 8.4 %collective-permute-start = (bf16[144,768]{1,0:T(8,128)(2,1)S(1)}, bf16[144,768]{1,0:T(8,128)(2,1)S(1)}, u32[]{:S(2)}, u32[]{:S(2)}) collective-permute-start(bf16[144,768]{1,0:T(8,128)(2,1)S(1)} %fusion.103), channel_id=1, source_target_pairs={{0,4},{4,0},{1,5},{5,1},{2,6},{6,2},{3,7},{7,3},{8,12},{12,8},{9,1... | collective-permute-start | bytes 663560 | tf_op jit(solution)/shard_map/ppermute | solution.py:547
  10.6 16.5 %collective-permute-start.2 = (bf16[208,768]{1,0:T(8,128)(2,1)}, bf16[208,768]{1,0:T(8,128)(2,1)S(1)}, u32[]{:S(2)}, u32[]{:S(2)}) collective-permute-start(bf16[208,768]{1,0:T(8,128)(2,1)} %prepare_first.1.refs_0_.refs_6_), channel_id=1, source_target_pairs={{0,8},{8,0},{16,24},{24,16},{1,9},{9,1},{17,25},{25,17},{2,10},{10... | collective-permute-start | bytes 958472 | tf_op jit(solution)/shard_map/ppermute | solution.py:547
  12.2 14.4 %collective-permute-start.6 = (bf16[128,768]{1,0:T(8,128)(2,1)S(1)}, bf16[128,768]{1,0:T(8,128)(2,1)S(1)}, u32[]{:S(2)}, u32[]{:S(2)}) collective-permute-start(bf16[128,768]{1,0:T(8,128)(2,1)S(1)} %get-tuple-element.377), channel_id=1, source_target_pairs={{0,4},{4,0},{1,5},{5,1},{2,6},{6,2},{3,7},{7,3},{8,12},{12,8},{9,1... | collective-permute-start | bytes 589832 | tf_op jit(solution)/shard_map/ppermute | solution.py:547
  18.3 8.3 %collective-permute-start.1 = (bf16[256,768]{1,0:T(8,128)(2,1)S(1)}, bf16[256,768]{1,0:T(8,128)(2,1)S(1)}, u32[]{:S(2)}, u32[]{:S(2)}) collective-permute-start(bf16[256,768]{1,0:T(8,128)(2,1)S(1)} %convolution_convert_fusion.2), channel_id=1, source_target_pairs={{0,2},{1,3},{2,0},{3,1},{4,6},{5,7},{6,4},{7,5},{8,10},{9,11},{10,... | collective-permute-start | bytes 1179656 | tf_op jit(solution)/shard_map/ppermute | solution.py:547
  21.9 15.6 %collective-permute-start.5 = (bf16[192,768]{1,0:T(8,128)(2,1)S(1)}, bf16[192,768]{1,0:T(8,128)(2,1)S(1)}, u32[]{:S(2)}, u32[]{:S(2)}) collective-permute-start(bf16[192,768]{1,0:T(8,128)(2,1)S(1)} %get-tuple-element.371), channel_id=1, source_target_pairs={{0,16},{8,24},{16,0},{24,8},{1,17},{9,25},{17,1},{25,9},{2,18},{10... | collective-permute-start | bytes 884744 | tf_op jit(solution)/shard_map/ppermute | solution.py:547
  22.0 16.4 %collective-permute-start.4 = (bf16[208,768]{1,0:T(8,128)(2,1)S(1)}, bf16[208,768]{1,0:T(8,128)(2,1)S(1)}, u32[]{:S(2)}, u32[]{:S(2)}) collective-permute-start(bf16[208,768]{1,0:T(8,128)(2,1)S(1)} %collective-permute-done.3.refs_1_.refs_7_), channel_id=1, source_target_pairs={{0,8},{8,0},{16,24},{24,16},{1,9},{9,1},{17,25},{25,17},{2,10},{10... | collective-permute-start | bytes 958472 | tf_op jit(solution)/shard_map/ppermute | solution.py:547
  38.8 7.0 %collective-permute-start.7 = (bf16[512,768]{1,0:T(8,128)(2,1)S(1)}, bf16[512,768]{1,0:T(8,128)(2,1)S(1)}, u32[]{:S(2)}, u32[]{:S(2)}) collective-permute-start(bf16[512,768]{1,0:T(8,128)(2,1)S(1)} %norm_only.1.refs_1_), channel_id=1, source_target_pairs={{0,1},{1,0},{2,3},{3,2},{4,5},{5,4},{6,7},{7,6},{8,9},{9,8},{10,11... | collective-permute-start | bytes 2359304 | tf_op jit(solution)/shard_map/ppermute | solution.py:547
  39.0 14.6 %collective-permute-start.8 = (bf16[384,384]{1,0:T(8,128)(2,1)S(1)}, bf16[384,384]{1,0:T(8,128)(2,1)S(1)}, u32[]{:S(2)}, u32[]{:S(2)}) collective-permute-start(bf16[384,384]{1,0:T(8,128)(2,1)S(1)} %pad_maximum_fusion.10), channel_id=1, source_target_pairs={{0,8},{8,0},{16,24},{24,16},{1,9},{9,1},{17,25},{25,17},{2,10},{10... | collective-permute-start | bytes 884744 | tf_op jit(solution)/shard_map/ppermute | solution.py:547
  39.9 13.8 %collective-permute-start.10 = (bf16[256,768]{1,0:T(8,128)(2,1)S(1)}, bf16[256,768]{1,0:T(8,128)(2,1)S(1)}, u32[]{:S(2)}, u32[]{:S(2)}) collective-permute-start(bf16[256,768]{1,0:T(8,128)(2,1)S(1)} %convolution_convert_fusion.1), channel_id=1, source_target_pairs={{0,2},{1,3},{2,0},{3,1},{4,6},{5,7},{6,4},{7,5},{8,10},{9,11},{10,... | collective-permute-start | bytes 1179656 | tf_op jit(solution)/shard_map/ppermute | solution.py:547
  41.5 12.1 %collective-permute-start.9 = (bf16[192,384]{1,0:T(8,128)(2,1)S(1)}, bf16[192,384]{1,0:T(8,128)(2,1)S(1)}, u32[]{:S(2)}, u32[]{:S(2)}) collective-permute-start(bf16[192,384]{1,0:T(8,128)(2,1)S(1)} %get-tuple-element.372), channel_id=1, source_target_pairs={{0,16},{8,24},{16,0},{24,8},{1,17},{9,25},{17,1},{25,9},{2,18},{10... | collective-permute-start | bytes 442376 | tf_op jit(solution)/shard_map/ppermute | solution.py:547
  53.6 2.4 collective-permute-start.11
  56.2 19.6 %collective-permute-start.12 = (bf16[512,768]{1,0:T(8,128)(2,1)S(1)}, bf16[512,768]{1,0:T(8,128)(2,1)S(1)}, u32[]{:S(2)}, u32[]{:S(2)}) collective-permute-start(bf16[512,768]{1,0:T(8,128)(2,1)S(1)} %add_convert_fusion.5.partial_ref), channel_id=1, source_target_pairs={{0,2},{1,3},{2,0},{3,1},{4,6},{5,7},{6,4},{7,5},{8,10},{9,11},{10,... | collective-permute-start | bytes 2359304 | tf_op jit(solution)/shard_map/ppermute | solution.py:547
  56.8 21.5 %collective-permute-start.14 = (bf16[384,768]{1,0:T(8,128)(2,1)S(1)}, bf16[384,768]{1,0:T(8,128)(2,1)S(1)}, u32[]{:S(2)}, u32[]{:S(2)}) collective-permute-start(bf16[384,768]{1,0:T(8,128)(2,1)S(1)} %maximum_maximum_fusion.refs_4_.refs_5_), channel_id=1, source_target_pairs={{0,8},{8,0},{16,24},{24,16},{1,9},{9,1},{17,25},{25,17},{2,10},{10... | collective-permute-start | bytes 1769480 | tf_op jit(solution)/shard_map/ppermute | solution.py:547
  57.6 20.7 %collective-permute-start.13 = (bf16[768,384]{1,0:T(8,128)(2,1)S(1)}, bf16[768,384]{1,0:T(8,128)(2,1)S(1)}, u32[]{:S(2)}, u32[]{:S(2)}) collective-permute-start(bf16[768,384]{1,0:T(8,128)(2,1)S(1)} %pad_maximum_fusion.4.refs_2_.refs_3_), channel_id=1, source_target_pairs={{0,4},{4,0},{1,5},{5,1},{2,6},{6,2},{3,7},{7,3},{8,12},{12,8},{9,1... | collective-permute-start | bytes 1769480 | tf_op jit(solution)/shard_map/ppermute | solution.py:547
  59.2 17.7 %collective-permute-start.15 = (bf16[192,768]{1,0:T(8,128)(2,1)S(1)}, bf16[192,768]{1,0:T(8,128)(2,1)S(1)}, u32[]{:S(2)}, u32[]{:S(2)}) collective-permute-start(bf16[192,768]{1,0:T(8,128)(2,1)S(1)} %prepare_attend.1), channel_id=1, source_target_pairs={{0,16},{8,24},{16,0},{24,8},{1,17},{9,25},{17,1},{25,9},{2,18},{10... | collective-permute-start | bytes 884744 | tf_op jit(solution)/shard_map/ppermute | solution.py:547
  82.2 2.4 collective-permute-start.17
  84.8 19.6 %collective-permute-start.18 = (bf16[512,768]{1,0:T(8,128)(2,1)S(1)}, bf16[512,768]{1,0:T(8,128)(2,1)S(1)}, u32[]{:S(2)}, u32[]{:S(2)}) collective-permute-start(bf16[512,768]{1,0:T(8,128)(2,1)S(1)} %add_convert_fusion.4.partial_ref), channel_id=1, source_target_pairs={{0,2},{1,3},{2,0},{3,1},{4,6},{5,7},{6,4},{7,5},{8,10},{9,11},{10,... | collective-permute-start | bytes 2359304 | tf_op jit(solution)/shard_map/ppermute | solution.py:547
  86.4 21.5 %collective-permute-start.19 = (bf16[384,768]{1,0:T(8,128)(2,1)S(1)}, bf16[384,768]{1,0:T(8,128)(2,1)S(1)}, u32[]{:S(2)}, u32[]{:S(2)}) collective-permute-start(bf16[384,768]{1,0:T(8,128)(2,1)S(1)} %constant_dynamic-update-slice_fusion.refs_5_.refs_6_), channel_id=1, source_target_pairs={{0,8},{8,0},{16,24},{24,16},{1,9},{9,1},{17,25},{25,17},{2,10},{10... | collective-permute-start | bytes 1769480 | tf_op jit(solution)/shard_map/ppermute | solution.py:547
  87.5 18.0 %collective-permute-start.20 = (bf16[192,384]{1,0:T(8,128)(2,1)S(1)}, bf16[192,384]{1,0:T(8,128)(2,1)S(1)}, u32[]{:S(2)}, u32[]{:S(2)}) collective-permute-start(bf16[192,384]{1,0:T(8,128)(2,1)S(1)} %get-tuple-element.369), channel_id=1, source_target_pairs={{0,16},{8,24},{16,0},{24,8},{1,17},{9,25},{17,1},{25,9},{2,18},{10... | collective-permute-start | bytes 442376 | tf_op jit(solution)/shard_map/ppermute | solution.py:547
  88.1 18.3 %collective-permute-start.21 = (bf16[192,384]{1,0:T(8,128)(2,1)S(1)}, bf16[192,384]{1,0:T(8,128)(2,1)S(1)}, u32[]{:S(2)}, u32[]{:S(2)}) collective-permute-start(bf16[192,384]{1,0:T(8,128)(2,1)S(1)} %get-tuple-element.368), channel_id=1, source_target_pairs={{0,16},{8,24},{16,0},{24,8},{1,17},{9,25},{17,1},{25,9},{2,18},{10... | collective-permute-start | bytes 442376 | tf_op jit(solution)/shard_map/ppermute | solution.py:547
  107.9 12.6 %collective-permute-start.23 = (bf16[384,384]{1,0:T(8,128)(2,1)S(1)}, bf16[384,384]{1,0:T(8,128)(2,1)S(1)}, u32[]{:S(2)}, u32[]{:S(2)}) collective-permute-start(bf16[384,384]{1,0:T(8,128)(2,1)S(1)} %pad_maximum_fusion.11), channel_id=1, source_target_pairs={{0,8},{8,0},{16,24},{24,16},{1,9},{9,1},{17,25},{25,17},{2,10},{10... | collective-permute-start | bytes 884744 | tf_op jit(solution)/shard_map/ppermute | solution.py:547
  109.2 10.1 %collective-permute-start.24 = (bf16[192,384]{1,0:T(8,128)(2,1)S(1)}, bf16[192,384]{1,0:T(8,128)(2,1)S(1)}, u32[]{:S(2)}, u32[]{:S(2)}) collective-permute-start(bf16[192,384]{1,0:T(8,128)(2,1)S(1)} %get-tuple-element.366), channel_id=1, source_target_pairs={{0,16},{8,24},{16,0},{24,8},{1,17},{9,25},{17,1},{25,9},{2,18},{10... | collective-permute-start | bytes 442376 | tf_op jit(solution)/shard_map/ppermute | solution.py:547
  120.7 23.5 %collective-permute-start.29 = (bf16[512,768]{1,0:T(8,128)(2,1)S(1)}, bf16[512,768]{1,0:T(8,128)(2,1)S(1)}, u32[]{:S(2)}, u32[]{:S(2)}) collective-permute-start(bf16[512,768]{1,0:T(8,128)(2,1)S(1)} %pad_maximum_fusion.1.refs_1_.skip_ref), channel_id=1, source_target_pairs={{0,1},{1,0},{2,3},{3,2},{4,5},{5,4},{6,7},{7,6},{8,9},{9,8},{10,11... | collective-permute-start | bytes 2359304 | tf_op jit(solution)/shard_map/ppermute | solution.py:547
  123.1 19.6 %collective-permute-start.26 = (bf16[512,768]{1,0:T(8,128)(2,1)S(1)}, bf16[512,768]{1,0:T(8,128)(2,1)S(1)}, u32[]{:S(2)}, u32[]{:S(2)}) collective-permute-start(bf16[512,768]{1,0:T(8,128)(2,1)S(1)} %add_convert_fusion.3.partial_ref), channel_id=1, source_target_pairs={{0,2},{1,3},{2,0},{3,1},{4,6},{5,7},{6,4},{7,5},{8,10},{9,11},{10,... | collective-permute-start | bytes 2359304 | tf_op jit(solution)/shard_map/ppermute | solution.py:547
  123.9 20.3 %collective-permute-start.28 = (bf16[384,768]{1,0:T(8,128)(2,1)S(1)}, bf16[384,768]{1,0:T(8,128)(2,1)S(1)}, u32[]{:S(2)}, u32[]{:S(2)}) collective-permute-start(bf16[384,768]{1,0:T(8,128)(2,1)S(1)} %maximum_maximum_fusion.1.refs_5_.refs_4_), channel_id=1, source_target_pairs={{0,8},{8,0},{16,24},{24,16},{1,9},{9,1},{17,25},{25,17},{2,10},{10... | collective-permute-start | bytes 1769480 | tf_op jit(solution)/shard_map/ppermute | solution.py:547
  126.7 17.5 %collective-permute-start.27 = (bf16[768,384]{1,0:T(8,128)(2,1)S(1)}, bf16[768,384]{1,0:T(8,128)(2,1)S(1)}, u32[]{:S(2)}, u32[]{:S(2)}) collective-permute-start(bf16[768,384]{1,0:T(8,128)(2,1)S(1)} %pad_maximum_fusion.5.refs_3_.refs_2_), channel_id=1, source_target_pairs={{0,4},{4,0},{1,5},{5,1},{2,6},{6,2},{3,7},{7,3},{8,12},{12,8},{9,1... | collective-permute-start | bytes 1769480 | tf_op jit(solution)/shard_map/ppermute | solution.py:547
  149.3 4.4 %collective-permute-start.31 = (bf16[512,768]{1,0:T(8,128)(2,1)S(1)}, bf16[512,768]{1,0:T(8,128)(2,1)S(1)}, u32[]{:S(2)}, u32[]{:S(2)}) collective-permute-start(bf16[512,768]{1,0:T(8,128)(2,1)S(1)} %get-tuple-element.254), channel_id=1, source_target_pairs={{0,1},{1,0},{2,3},{3,2},{4,5},{5,4},{6,7},{7,6},{8,9},{9,8},{10,11... | collective-permute-start | bytes 2359304 | tf_op jit(solution)/shard_map/ppermute | solution.py:547
  153.8 19.9 %collective-permute-start.32 = (bf16[512,768]{1,0:T(8,128)(2,1)S(1)}, bf16[512,768]{1,0:T(8,128)(2,1)S(1)}, u32[]{:S(2)}, u32[]{:S(2)}) collective-permute-start(bf16[512,768]{1,0:T(8,128)(2,1)S(1)} %add_convert_fusion.2.partial_ref), channel_id=1, source_target_pairs={{0,2},{1,3},{2,0},{3,1},{4,6},{5,7},{6,4},{7,5},{8,10},{9,11},{10,... | collective-permute-start | bytes 2359304 | tf_op jit(solution)/shard_map/ppermute | solution.py:547
  156.1 19.3 %collective-permute-start.34 = (bf16[768,384]{1,0:T(8,128)(2,1)S(1)}, bf16[768,384]{1,0:T(8,128)(2,1)S(1)}, u32[]{:S(2)}, u32[]{:S(2)}) collective-permute-start(bf16[768,384]{1,0:T(8,128)(2,1)S(1)} %slice.339), channel_id=1, source_target_pairs={{0,4},{4,0},{1,5},{5,1},{2,6},{6,2},{3,7},{7,3},{8,12},{12,8},{9,1... | collective-permute-start | bytes 1769480 | tf_op jit(solution)/shard_map/ppermute | solution.py:547
  157.7 17.7 %collective-permute-start.33 = (bf16[384,768]{1,0:T(8,128)(2,1)S(1)}, bf16[384,768]{1,0:T(8,128)(2,1)S(1)}, u32[]{:S(2)}, u32[]{:S(2)}) collective-permute-start(bf16[384,768]{1,0:T(8,128)(2,1)S(1)} %slice.279), channel_id=1, source_target_pairs={{0,8},{8,0},{16,24},{24,16},{1,9},{9,1},{17,25},{25,17},{2,10},{10... | collective-permute-start | bytes 1769480 | tf_op jit(solution)/shard_map/ppermute | solution.py:547
  175.4 2.4 collective-permute-start.35
  175.7 11.7 %collective-permute-start.36 = (bf16[384,384]{1,0:T(8,128)(2,1)S(1)}, bf16[384,384]{1,0:T(8,128)(2,1)S(1)}, u32[]{:S(2)}, u32[]{:S(2)}) collective-permute-start(bf16[384,384]{1,0:T(8,128)(2,1)S(1)} %slice.450), channel_id=1, source_target_pairs={{0,8},{8,0},{16,24},{24,16},{1,9},{9,1},{17,25},{25,17},{2,10},{10... | collective-permute-start | bytes 884744 | tf_op jit(solution)/shard_map/ppermute | solution.py:547
  187.4 2.4 collective-permute-start.37
  189.9 19.8 %collective-permute-start.38 = (bf16[512,768]{1,0:T(8,128)(2,1)S(1)}, bf16[512,768]{1,0:T(8,128)(2,1)S(1)}, u32[]{:S(2)}, u32[]{:S(2)}) collective-permute-start(bf16[512,768]{1,0:T(8,128)(2,1)S(1)} %add_convert_fusion.1.partial_ref), channel_id=1, source_target_pairs={{0,2},{1,3},{2,0},{3,1},{4,6},{5,7},{6,4},{7,5},{8,10},{9,11},{10,... | collective-permute-start | bytes 2359304 | tf_op jit(solution)/shard_map/ppermute | solution.py:547
  191.8 23.9 %collective-permute-start.41 = (bf16[768,384]{1,0:T(8,128)(2,1)S(1)}, bf16[768,384]{1,0:T(8,128)(2,1)S(1)}, u32[]{:S(2)}, u32[]{:S(2)}) collective-permute-start(bf16[768,384]{1,0:T(8,128)(2,1)S(1)} %broadcast_select_fusion.1), channel_id=1, source_target_pairs={{0,4},{4,0},{1,5},{5,1},{2,6},{6,2},{3,7},{7,3},{8,12},{12,8},{9,1... | collective-permute-start | bytes 1769480 | tf_op jit(solution)/shard_map/ppermute | solution.py:547
  193.4 22.3 %collective-permute-start.40 = (bf16[192,768]{1,0:T(8,128)(2,1)S(1)}, bf16[192,768]{1,0:T(8,128)(2,1)S(1)}, u32[]{:S(2)}, u32[]{:S(2)}) collective-permute-start(bf16[192,768]{1,0:T(8,128)(2,1)S(1)} %slice.449), channel_id=1, source_target_pairs={{0,16},{8,24},{16,0},{24,8},{1,17},{9,25},{17,1},{25,9},{2,18},{10... | collective-permute-start | bytes 884744 | tf_op jit(solution)/shard_map/ppermute | solution.py:547
  195.0 20.6 %collective-permute-start.39 = (bf16[192,384]{1,0:T(8,128)(2,1)S(1)}, bf16[192,384]{1,0:T(8,128)(2,1)S(1)}, u32[]{:S(2)}, u32[]{:S(2)}) collective-permute-start(bf16[192,384]{1,0:T(8,128)(2,1)S(1)} %slice.454), channel_id=1, source_target_pairs={{0,16},{8,24},{16,0},{24,8},{1,17},{9,25},{17,1},{25,9},{2,18},{10... | collective-permute-start | bytes 442376 | tf_op jit(solution)/shard_map/ppermute | solution.py:547
  220.6 4.7 %collective-permute-start.43 = (bf16[512,768]{1,0:T(8,128)(2,1)S(1)}, bf16[512,768]{1,0:T(8,128)(2,1)S(1)}, u32[]{:S(2)}, u32[]{:S(2)}) collective-permute-start(bf16[512,768]{1,0:T(8,128)(2,1)S(1)} %get-tuple-element.283), channel_id=1, source_target_pairs={{0,1},{1,0},{2,3},{3,2},{4,5},{5,4},{6,7},{7,6},{8,9},{9,8},{10,11... | collective-permute-start | bytes 2359304 | tf_op jit(solution)/shard_map/ppermute | solution.py:547
  225.5 19.9 %collective-permute-start.44 = (bf16[512,768]{1,0:T(8,128)(2,1)S(1)}, bf16[512,768]{1,0:T(8,128)(2,1)S(1)}, u32[]{:S(2)}, u32[]{:S(2)}) collective-permute-start(bf16[512,768]{1,0:T(8,128)(2,1)S(1)} %add_convert_fusion.partial_ref), channel_id=1, source_target_pairs={{0,2},{1,3},{2,0},{3,1},{4,6},{5,7},{6,4},{7,5},{8,10},{9,11},{10,... | collective-permute-start | bytes 2359304 | tf_op jit(solution)/shard_map/ppermute | solution.py:547
  227.6 19.3 %collective-permute-start.47 = (bf16[768,384]{1,0:T(8,128)(2,1)S(1)}, bf16[768,384]{1,0:T(8,128)(2,1)S(1)}, u32[]{:S(2)}, u32[]{:S(2)}) collective-permute-start(bf16[768,384]{1,0:T(8,128)(2,1)S(1)} %slice.347), channel_id=1, source_target_pairs={{0,4},{4,0},{1,5},{5,1},{2,6},{6,2},{3,7},{7,3},{8,12},{12,8},{9,1... | collective-permute-start | bytes 1769480 | tf_op jit(solution)/shard_map/ppermute | solution.py:547
  228.3 21.4 %collective-permute-start.46 = (bf16[384,768]{1,0:T(8,128)(2,1)S(1)}, bf16[384,768]{1,0:T(8,128)(2,1)S(1)}, u32[]{:S(2)}, u32[]{:S(2)}) collective-permute-start(bf16[384,768]{1,0:T(8,128)(2,1)S(1)} %slice.290), channel_id=1, source_target_pairs={{0,8},{8,0},{16,24},{24,16},{1,9},{9,1},{17,25},{25,17},{2,10},{10... | collective-permute-start | bytes 1769480 | tf_op jit(solution)/shard_map/ppermute | solution.py:547
  228.4 58.5 %collective-permute-start.59 = (bf16[512,768]{1,0:T(8,128)(2,1)S(1)}, bf16[512,768]{1,0:T(8,128)(2,1)S(1)}, u32[]{:S(2)}, u32[]{:S(2)}) collective-permute-start(bf16[512,768]{1,0:T(8,128)(2,1)S(1)} %feed_forward.6), channel_id=1, source_target_pairs={{0,1},{1,0},{2,3},{3,2},{4,5},{5,4},{6,7},{7,6},{8,9},{9,8},{10,11... | collective-permute-start | bytes 2359304 | tf_op jit(solution)/shard_map/ppermute | solution.py:547
  228.5 21.2 %collective-permute-start.45 = (bf16[384,384]{1,0:T(8,128)(2,1)S(1)}, bf16[384,384]{1,0:T(8,128)(2,1)S(1)}, u32[]{:S(2)}, u32[]{:S(2)}) collective-permute-start(bf16[384,384]{1,0:T(8,128)(2,1)S(1)} %slice.448), channel_id=1, source_target_pairs={{0,8},{8,0},{16,24},{24,16},{1,9},{9,1},{17,25},{25,17},{2,10},{10... | collective-permute-start | bytes 884744 | tf_op jit(solution)/shard_map/ppermute | solution.py:547
  249.8 14.1 %collective-permute-start.51 = (bf16[384,384]{1,0:T(8,128)(2,1)S(1)}, bf16[384,384]{1,0:T(8,128)(2,1)S(1)}, u32[]{:S(2)}, u32[]{:S(2)}) collective-permute-start(bf16[384,384]{1,0:T(8,128)(2,1)S(1)} %slice.447), channel_id=1, source_target_pairs={{0,8},{8,0},{16,24},{24,16},{1,9},{9,1},{17,25},{25,17},{2,10},{10... | collective-permute-start | bytes 884744 | tf_op jit(solution)/shard_map/ppermute | solution.py:547
  250.2 3.9 %collective-permute-start.48 = (bf16[512,768]{1,0:T(8,128)(2,1)S(1)}, bf16[512,768]{1,0:T(8,128)(2,1)S(1)}, u32[]{:S(2)}, u32[]{:S(2)}) collective-permute-start(bf16[512,768]{1,0:T(8,128)(2,1)S(1)} %get-tuple-element.292.refs_1_), channel_id=1, source_target_pairs={{0,1},{1,0},{2,3},{3,2},{4,5},{5,4},{6,7},{7,6},{8,9},{9,8},{10,11... | collective-permute-start | bytes 2359304 | tf_op jit(solution)/shard_map/ppermute | solution.py:547
  250.3 13.7 %collective-permute-start.50 = (bf16[192,384]{1,0:T(8,128)(2,1)S(1)}, bf16[192,384]{1,0:T(8,128)(2,1)S(1)}, u32[]{:S(2)}, u32[]{:S(2)}) collective-permute-start(bf16[192,384]{1,0:T(8,128)(2,1)S(1)} %slice.453), channel_id=1, source_target_pairs={{0,16},{8,24},{16,0},{24,8},{1,17},{9,25},{17,1},{25,9},{2,18},{10... | collective-permute-start | bytes 442376 | tf_op jit(solution)/shard_map/ppermute | solution.py:547
  252.4 28.4 %collective-permute-start.55 = (bf16[192,1152]{1,0:T(8,128)(2,1)S(1)}, bf16[192,1152]{1,0:T(8,128)(2,1)S(1)}, u32[]{:S(2)}, u32[]{:S(2)}) collective-permute-start(bf16[192,1152]{1,0:T(8,128)(2,1)S(1)} %get-tuple-element.387), channel_id=1, source_target_pairs={{0,4},{4,0},{1,5},{5,1},{2,6},{6,2},{3,7},{7,3},{8,12},{12,8},{9,1... | collective-permute-start | bytes 1327112 | tf_op jit(solution)/shard_map/ppermute | solution.py:547
  266.4 11.5 %collective-permute-start.53 = (bf16[256,768]{1,0:T(8,128)(2,1)S(1)}, bf16[256,768]{1,0:T(8,128)(2,1)S(1)}, u32[]{:S(2)}, u32[]{:S(2)}) collective-permute-start(bf16[256,768]{1,0:T(8,128)(2,1)S(1)} %add_convert_fusion.8), channel_id=1, source_target_pairs={{0,2},{1,3},{2,0},{3,1},{4,6},{5,7},{6,4},{7,5},{8,10},{9,11},{10,... | collective-permute-start | bytes 1179656 | tf_op jit(solution)/shard_map/ppermute | solution.py:547
  268.1 15.5 %collective-permute-start.49 = (bf16[768,384]{1,0:T(8,128)(2,1)S(1)}, bf16[768,384]{1,0:T(8,128)(2,1)S(1)}, u32[]{:S(2)}, u32[]{:S(2)}) collective-permute-start(bf16[768,384]{1,0:T(8,128)(2,1)S(1)} %broadcast_select_fusion), channel_id=1, source_target_pairs={{0,4},{4,0},{1,5},{5,1},{2,6},{6,2},{3,7},{7,3},{8,12},{12,8},{9,1... | collective-permute-start | bytes 1769480 | tf_op jit(solution)/shard_map/ppermute | solution.py:547
  268.7 22.5 %collective-permute-start.66 = (bf16[192,768]{1,0:T(8,128)(2,1)S(1)}, bf16[192,768]{1,0:T(8,128)(2,1)S(1)}, u32[]{:S(2)}, u32[]{:S(2)}) collective-permute-start(bf16[192,768]{1,0:T(8,128)(2,1)S(1)} %slice.445), channel_id=1, source_target_pairs={{0,16},{8,24},{16,0},{24,8},{1,17},{9,25},{17,1},{25,9},{2,18},{10... | collective-permute-start | bytes 884744 | tf_op jit(solution)/shard_map/ppermute | solution.py:547
  279.4 4.7 %collective-permute-start.54 = (f32[16,768]{1,0:T(8,128)S(1)}, f32[16,768]{1,0:T(8,128)S(1)}, u32[]{:S(2)}, u32[]{:S(2)}) collective-permute-start(f32[16,768]{1,0:T(8,128)S(1)} %get-tuple-element.305), channel_id=1, source_target_pairs={{0,1},{1,0},{2,3},{3,2},{4,5},{5,4},{6,7},{7,6},{8,9},{9,8},{10,11... | collective-permute-start | bytes 147464 | tf_op jit(solution)/shard_map/ppermute | solution.py:547
  280.8 10.4 %collective-permute-start.65 = (bf16[192,384]{1,0:T(8,128)(2,1)S(1)}, bf16[192,384]{1,0:T(8,128)(2,1)S(1)}, u32[]{:S(2)}, u32[]{:S(2)}) collective-permute-start(bf16[192,384]{1,0:T(8,128)(2,1)S(1)} %slice.451), channel_id=1, source_target_pairs={{0,16},{8,24},{16,0},{24,8},{1,17},{9,25},{17,1},{25,9},{2,18},{10... | collective-permute-start | bytes 442376 | tf_op jit(solution)/shard_map/ppermute | solution.py:547
  283.6 6.1 %collective-permute-start.60 = (bf16[128,768]{1,0:T(8,128)(2,1)S(1)}, bf16[128,768]{1,0:T(8,128)(2,1)S(1)}, u32[]{:S(2)}, u32[]{:S(2)}) collective-permute-start(bf16[128,768]{1,0:T(8,128)(2,1)S(1)} %slice_select_fusion.1), channel_id=1, source_target_pairs={{0,4},{4,0},{1,5},{5,1},{2,6},{6,2},{3,7},{7,3},{8,12},{12,8},{9,1... | collective-permute-start | bytes 589832 | tf_op jit(solution)/shard_map/ppermute | solution.py:547
  284.1 4.2 %collective-permute-start.58 = (f32[16,768]{1,0:T(8,128)S(1)}, f32[16,768]{1,0:T(8,128)S(1)}, u32[]{:S(2)}, u32[]{:S(2)}) collective-permute-start(f32[16,768]{1,0:T(8,128)S(1)} %add.147), channel_id=1, source_target_pairs={{0,2},{1,3},{2,0},{3,1},{4,6},{5,7},{6,4},{7,5},{8,10},{9,11},{10,... | collective-permute-start | bytes 147464 | tf_op jit(solution)/shard_map/ppermute | solution.py:547
  286.8 10.6 %collective-permute-start.56 = (bf16[384,384]{1,0:T(8,128)(2,1)S(1)}, bf16[384,384]{1,0:T(8,128)(2,1)S(1)}, u32[]{:S(2)}, u32[]{:S(2)}) collective-permute-start(bf16[384,384]{1,0:T(8,128)(2,1)S(1)} %slice.446), channel_id=1, source_target_pairs={{0,8},{8,0},{16,24},{24,16},{1,9},{9,1},{17,25},{25,17},{2,10},{10... | collective-permute-start | bytes 884744 | tf_op jit(solution)/shard_map/ppermute | solution.py:547
  290.5 14.0 %collective-permute-start.61 = (f32[256,256]{1,0:T(8,128)S(1)}, f32[256,256]{1,0:T(8,128)S(1)}, u32[]{:S(2)}, u32[]{:S(2)}) collective-permute-start(f32[256,256]{1,0:T(8,128)S(1)} %pack_grads.1), channel_id=1, source_target_pairs={{0,4},{4,0},{1,5},{5,1},{2,6},{6,2},{3,7},{7,3},{8,12},{12,8},{9,1... | collective-permute-start | bytes 786440 | tf_op jit(solution)/shard_map/ppermute | solution.py:547
  291.5 22.6 %collective-permute-start.69 = (bf16[192,1536]{1,0:T(8,128)(2,1)S(1)}, bf16[192,1536]{1,0:T(8,128)(2,1)S(1)}, u32[]{:S(2)}, u32[]{:S(2)}) collective-permute-start(bf16[192,1536]{1,0:T(8,128)(2,1)S(1)} %pad_maximum_fusion.6), channel_id=1, source_target_pairs={{0,4},{4,0},{1,5},{5,1},{2,6},{6,2},{3,7},{7,3},{8,12},{12,8},{9,1... | collective-permute-start | bytes 1769480 | tf_op jit(solution)/shard_map/ppermute | solution.py:547
  293.0 10.7 %collective-permute-start.62 = (bf16[256,768]{1,0:T(8,128)(2,1)S(1)}, bf16[256,768]{1,0:T(8,128)(2,1)S(1)}, u32[]{:S(2)}, u32[]{:S(2)}) collective-permute-start(bf16[256,768]{1,0:T(8,128)(2,1)S(1)} %add_convert_fusion.7), channel_id=1, source_target_pairs={{0,2},{1,3},{2,0},{3,1},{4,6},{5,7},{6,4},{7,5},{8,10},{9,11},{10,... | collective-permute-start | bytes 1179656 | tf_op jit(solution)/shard_map/ppermute | solution.py:547
  297.6 9.4 %collective-permute-start.57 = (bf16[192,384]{1,0:T(8,128)(2,1)S(1)}, bf16[192,384]{1,0:T(8,128)(2,1)S(1)}, u32[]{:S(2)}, u32[]{:S(2)}) collective-permute-start(bf16[192,384]{1,0:T(8,128)(2,1)S(1)} %slice.452), channel_id=1, source_target_pairs={{0,16},{8,24},{16,0},{24,8},{1,17},{9,25},{17,1},{25,9},{2,18},{10... | collective-permute-start | bytes 442376 | tf_op jit(solution)/shard_map/ppermute | solution.py:547
  307.0 5.5 %collective-permute-start.67 = (f32[128,256]{1,0:T(8,128)S(1)}, f32[128,256]{1,0:T(8,128)S(1)}, u32[]{:S(2)}, u32[]{:S(2)}) collective-permute-start(f32[128,256]{1,0:T(8,128)S(1)} %slice.366), channel_id=1, source_target_pairs={{0,8},{8,0},{16,24},{24,16},{1,9},{9,1},{17,25},{25,17},{2,10},{10... | collective-permute-start | bytes 393224 | tf_op jit(solution)/shard_map/ppermute | solution.py:547
  307.1 11.7 %collective-permute-start.64 = (bf16[128,768]{1,0:T(8,128)(2,1)S(1)}, bf16[128,768]{1,0:T(8,128)(2,1)S(1)}, u32[]{:S(2)}, u32[]{:S(2)}) collective-permute-start(bf16[128,768]{1,0:T(8,128)(2,1)S(1)} %get-tuple-element.375), channel_id=1, source_target_pairs={{0,4},{4,0},{1,5},{5,1},{2,6},{6,2},{3,7},{7,3},{8,12},{12,8},{9,1... | collective-permute-start | bytes 589832 | tf_op jit(solution)/shard_map/ppermute | solution.py:547
  308.6 11.1 %collective-permute-start.63 = (bf16[192,384]{1,0:T(8,128)(2,1)S(1)}, bf16[192,384]{1,0:T(8,128)(2,1)S(1)}, u32[]{:S(2)}, u32[]{:S(2)}) collective-permute-start(bf16[192,384]{1,0:T(8,128)(2,1)S(1)} %fusion.102.refs_0_), channel_id=1, source_target_pairs={{0,4},{4,0},{1,5},{5,1},{2,6},{6,2},{3,7},{7,3},{8,12},{12,8},{9,1... | collective-permute-start | bytes 442376 | tf_op jit(solution)/shard_map/ppermute | solution.py:547
  312.6 5.7 %collective-permute-start.68 = (f32[64,256]{1,0:T(8,128)S(1)}, f32[64,256]{1,0:T(8,128)S(1)}, u32[]{:S(2)}, u32[]{:S(2)}) collective-permute-start(f32[64,256]{1,0:T(8,128)S(1)} %slice.367), channel_id=1, source_target_pairs={{0,16},{8,24},{16,0},{24,8},{1,17},{9,25},{17,1},{25,9},{2,18},{10... | collective-permute-start | bytes 196616 | tf_op jit(solution)/shard_map/ppermute | solution.py:547
  (16 other events, 167.2 us)

commit v4 on v3

--- a/solution.py
+++ b/solution.py
@@ -1796,18 +1796,19 @@
             mine_s[:, :half], mine_s[:, 2 * half : 3 * half], mine_s[:, half : 2 * half], mine_s[:, 3 * half :]
         )
     )
-    late, _ = pin(mine_t, mine_s)
-    expand_grad_t, reduce_grad_t = finish_feed(late, theirs_t, place, half)
+    y_moved, theirs_t = pin(y_moved, theirs_t)
     grad_a = keep_rows(grad_a, y_moved)
     y_moved = send_rows(grad_a, cross_far)
+    grad_a, pack_moved = pin(grad_a, pack_moved)
+    pack = pack + pack_moved
+    pack_near = cross_near(pack[2 * ROWS :])
+    expand_grad_t, reduce_grad_t = finish_feed(mine_t, theirs_t, place, half)
     final_across, expand_grad_t = pin(final_across, expand_grad_t)
     rows = 2 * tokens
     final = middle_t[:rows] + gains_t[5:6] + final_kept[:rows] + final_across.astype(F32)
     final = final + final_arrived[:rows].astype(F32)
     final = times_across(final.astype(BF16), chooser, BF16)
-    y_moved, pack_moved, final = pin(y_moved, pack_moved, final)
-    pack = pack + pack_moved
-    pack_near = cross_near(pack[2 * ROWS :])
+    y_moved, pack_near, final = pin(y_moved, pack_near, final)
     mine_a = keep_rows(grad_a, y_moved).astype(BF16)
     theirs_a = cross_y(mine_a)
     final_moved = swapped(final)
@@ -1817,7 +1818,6 @@
     expand_grad_s, reduce_grad_s = finish_feed(
         mine_s[:, : 3 * half], theirs_s[:, : 3 * half], place, half
     )
-    pack_near, pack = pin(pack_near, pack)
     pack = pack[: 2 * ROWS] + pack_near
     pack_far = cross_far(pack[ROWS:])
     vectors = unpack_grads(pack, pack_far, local, params[3].shape, params[9].shape)

time: 327 us -> 325 us (level)
  waiting for transfers between devices: 151 us -> 145 us
  starting transfers between devices: 70.9 us -> 76.2 us
    ppermute x70, waiting for transfers between devices: 151 us -> 145 us  [swap(): return row_major(lax.ppermute(row_major(value), axis, route))]
    ppermute x70, starting transfers between devices: 70.9 us -> 76.2 us  [swap(): return row_major(lax.ppermute(row_major(value), axis, route))]
  transfers between devices with their start and end apart: 70 -> 70, of which waited for: 37 -> 36; matrix products, arithmetic and copies ran while one was open for 7% -> 7% of each run, Pallas kernels for 20% -> 20%
where the time goes in v4:
time: 325 us; the launch traced here: 320 us
  waiting for transfers between devices  145 us (45%)
  starting transfers between devices  76.2 us (23%)
  Pallas kernels  74.7 us (23%)
  matrix products  13.7 us (4%)
  other arithmetic  8.1 us (2%)
    ppermute x70, waiting for transfers between devices, swap(): return row_major(lax.ppermute(row_major(value), axis, route))  145 us
    ppermute x70, starting transfers between devices, swap(): return row_major(lax.ppermute(row_major(value), axis, route))  76.2 us
    pallas_call x12, Pallas kernels, call(): pl.pallas_call(body, out_shape=tuple(outputs), in_specs=[SMEM if v.ndim =...  51.8 us
    pallas_call x8, Pallas kernels, row_call(): pl.pallas_call(body, grid=(1,), out_shape=tuple(outputs), in_specs=specs,...  10.4 us
    dot_general x8, matrix products, dot_down(): lax.dot_general(left, right, (((0,), (0,)), ((), ())), preferred_element_...  9.97 us
  transfers between devices with their start and end apart: 70, of which 36 were waited for; matrix products, arithmetic and copies ran while one was open for 7% of the time, Pallas kernels for 20%

profile of v4, /device:TPU:0, one launch (start us, length us, event | category | flops | bytes accessed | tf_op | source)
XLA Modules:
  0.0 320.3 jit_solution(8729942390981459659)
XLA Ops:
  0.7 2.4 prepare_first.1.refs_0_.refs_6_
  3.1 4.1 %collective-permute-start.3 = (bf16[208,768]{1,0:T(8,128)(2,1)}, bf16[208,768]{1,0:T(8,128)(2,1)S(1)}, u32[]{:S(2)}, u32[]{:S(2)}) collective-permute-start(bf16[208,768]{1,0:T(8,128)(2,1)} %prepare_first.1.refs_0_.refs_6_), channel_id=1, source_target_pairs={{0,16},{8,24},{16,0},{24,8},{1,17},{9,25},{17,1},{25,9},{2,18},{10... | collective-permute-start | bytes 958472 | tf_op jit(solution)/shard_map/ppermute | solution.py:547
  9.0 1.6 collective-permute-start
  10.6 1.6 collective-permute-start.2
  13.5 3.9 %collective-permute-done = bf16[144,768]{1,0:T(8,128)(2,1)S(1)} collective-permute-done((bf16[144,768]{1,0:T(8,128)(2,1)S(1)}, bf16[144,768]{1,0:T(8,128)(2,1)S(1)}, u32[]{:S(2)}, u32[]{:S(2)}) %collective-permute-start) | collective-permute-done | bytes 221216 | tf_op jit(solution)/shard_map/ppermute | solution.py:547
  18.3 1.6 collective-permute-start.1
  22.0 4.1 %collective-permute-start.4 = (bf16[208,768]{1,0:T(8,128)(2,1)S(1)}, bf16[208,768]{1,0:T(8,128)(2,1)S(1)}, u32[]{:S(2)}, u32[]{:S(2)}) collective-permute-start(bf16[208,768]{1,0:T(8,128)(2,1)S(1)} %collective-permute-done.3.refs_1_.refs_7_), channel_id=1, source_target_pairs={{0,8},{8,0},{16,24},{24,16},{1,9},{9,1},{17,25},{25,17},{2,10},{10... | collective-permute-start | bytes 958472 | tf_op jit(solution)/shard_map/ppermute | solution.py:547
  27.1 10.4 %collective-permute-done.5 = bf16[192,768]{1,0:T(8,128)(2,1)S(1)} collective-permute-done((bf16[192,768]{1,0:T(8,128)(2,1)S(1)}, bf16[192,768]{1,0:T(8,128)(2,1)S(1)}, u32[]{:S(2)}, u32[]{:S(2)}) %collective-permute-start.5) | collective-permute-done | bytes 294944 | tf_op jit(solution)/shard_map/ppermute | solution.py:547
  39.9 1.6 collective-permute-start.10
  41.5 3.5 %collective-permute-start.9 = (bf16[192,384]{1,0:T(8,128)(2,1)S(1)}, bf16[192,384]{1,0:T(8,128)(2,1)S(1)}, u32[]{:S(2)}, u32[]{:S(2)}) collective-permute-start(bf16[192,384]{1,0:T(8,128)(2,1)S(1)} %get-tuple-element.376), channel_id=1, source_target_pairs={{0,16},{8,24},{16,0},{24,8},{1,17},{9,25},{17,1},{25,9},{2,18},{10... | collective-permute-start | bytes 442376 | tf_op jit(solution)/shard_map/ppermute | solution.py:547
  45.8 7.8 %attention_forward.2 = (bf16[512,768]{1,0:T(8,128)(2,1)S(1)}, f32[512,768]{1,0:T(8,128)S(1)}, bf16[9,1024,64]{2,1,0:T(8,128)(2,1)S(1)}, bf16[1024,192]{1,0:T(8,1...) custom-call(s32[1]{0:T(128)} %bitcast.refs_0_, ...), custom_call_target="tpu_custom_call" | custom-call | flops 1610612736 | bytes 8399108 | tf_op jit(solution)/shard_map/attention_forward/pallas_call | solution.py:840
  53.7 2.3 collective-permute-done.11
  57.6 1.6 collective-permute-start.13
  59.2 1.7 collective-permute-start.15
  60.9 14.9 %collective-permute-done.12.across_ref = bf16[512,768]{1,0:T(8,128)(2,1)S(1)} collective-permute-done((bf16[512,768]{1,0:T(8,128)(2,1)S(1)}, bf16[512,768]{1,0:T(8,128)(2,1)S(1)}, u32[]{:S(2)}, u32[]{:S(2)}) %collective-permute-start.12) | collective-permute-done | bytes 786464 | tf_op jit(solution)/shard_map/ppermute | solution.py:547
  78.3 2.3 collective-permute-done.16.refs_0_
  80.6 1.7 feed_forward.5
  82.4 1.7 feed_forward.4
  84.8 1.6 collective-permute-start.18
  88.1 2.4 collective-permute-start.21
  90.4 14.0 %collective-permute-done.18.across_ref = bf16[512,768]{1,0:T(8,128)(2,1)S(1)} collective-permute-done((bf16[512,768]{1,0:T(8,128)(2,1)S(1)}, bf16[512,768]{1,0:T(8,128)(2,1)S(1)}, u32[]{:S(2)}, u32[]{:S(2)}) %collective-permute-start.18) | collective-permute-done | bytes 786464 | tf_op jit(solution)/shard_map/ppermute | solution.py:547
  110.2 7.3 %attention_forward.3 = (bf16[512,768]{1,0:T(8,128)(2,1)S(1)}, f32[512,768]{1,0:T(8,128)S(1)}, bf16[9,1024,64]{2,1,0:T(8,128)(2,1)S(1)}, bf16[1024,192]{1,0:T(8,128)(2,1)S(1)}, f32[3,1,1024]{2,1,0:T(1,128)S(1)}) custom-call(s32[1]{0:T(128)} %bitcast.refs_0_, bf16[512,768]{1,0:T(8,128)(2,1)S(1)} %get-tuple-element.235.refs_1_, ...), custom_call_target="tpu_custom_call" | custom-call | flops 1610612736 | bytes 6703364 | tf_op jit(solution)/shard_map/attention_forward/pallas_call | solution.py:840
  117.5 1.8 collective-permute-done.24
  121.2 1.7 collective-permute-done.25
  123.9 2.7 collective-permute-start.28
  126.7 1.6 collective-permute-start.27
  128.3 14.5 %collective-permute-done.26.across_ref = bf16[512,768]{1,0:T(8,128)(2,1)S(1)} collective-permute-done((bf16[512,768]{1,0:T(8,128)(2,1)S(1)}, bf16[512,768]{1,0:T(8,128)(2,1)S(1)}, u32[]{:S(2)}, u32[]{:S(2)}) %collective-permute-start.26) | collective-permute-done | bytes 786464 | tf_op jit(solution)/shard_map/ppermute | solution.py:547
  144.3 2.3 collective-permute-done.30.refs_0_
  146.6 2.7 feed_backward.5
  149.5 2.7 feed_backward.4
  156.1 1.6 collective-permute-start.34
  157.7 2.7 collective-permute-start.33
  160.5 1.6 feed_forward.7
  162.1 1.6 feed_forward.6
  163.7 9.9 %collective-permute-done.32.across_ref = bf16[512,768]{1,0:T(8,128)(2,1)S(1)} collective-permute-done((bf16[512,768]{1,0:T(8,128)(2,1)S(1)}, bf16[512,768]{1,0:T(8,128)(2,1)S(1)}, u32[]{:S(2)}, u32[]{:S(2)}) %collective-permute-start.32) | collective-permute-done | bytes 786464 | tf_op jit(solution)/shard_map/ppermute | solution.py:547
  173.7 1.7 norm_back_near.3
  175.7 1.9 collective-permute-start.36
  177.8 9.6 %attention_backward.2 = (bf16[512,768]{1,0:T(8,128)(2,1)S(1)}, f32[512,768]{1,0:T(8,128)S(1)}, bf16[1024,576]{1,0:T(8,128)(2,1)S(1)}, f32[1,576]{1,0:T(1,128)S(1)}) custom-call(s32[1]{0:T(128)} %bitcast.refs_0_, bf16[512,768]{1,0:T(8,128)(2,1)S(1)} %get-tuple-element.265.refs_1_, bf16[512,768]{1,0:T(8,128)(2,1)S(1)} %collective-permute-done.35.refs_2_, ...), custom_call_target="tpu_custom_call" | custom-call | flops 4026531840 | bytes 7489796 | tf_op jit(solution)/shard_map/attention_backward/pallas_call | solution.py:840
  189.9 1.6 collective-permute-start.38
  191.8 1.6 collective-permute-start.41
  196.5 13.2 %collective-permute-done.38.across_ref = bf16[512,768]{1,0:T(8,128)(2,1)S(1)} collective-permute-done((bf16[512,768]{1,0:T(8,128)(2,1)S(1)}, bf16[512,768]{1,0:T(8,128)(2,1)S(1)}, u32[]{:S(2)}, u32[]{:S(2)}) %collective-permute-start.38) | collective-permute-done | bytes 786464 | tf_op jit(solution)/shard_map/ppermute | solution.py:547
  209.7 1.7 norm_back_near.4
  211.4 4.2 %collective-permute-done.39 = bf16[192,384]{1,0:T(8,128)(2,1)S(1)} collective-permute-done((bf16[192,384]{1,0:T(8,128)(2,1)S(1)}, bf16[192,384]{1,0:T(8,128)(2,1)S(1)}, u32[]{:S(2)}, u32[]{:S(2)}) %collective-permute-start.39) | collective-permute-done | bytes 147488 | tf_op jit(solution)/shard_map/ppermute | solution.py:547
  215.7 2.3 collective-permute-done.42.refs_1_
  217.9 2.7 feed_backward.7
  220.8 2.7 feed_backward.6
  228.5 2.1 collective-permute-start.45
  230.7 14.7 %collective-permute-done.44.across_ref = bf16[512,768]{1,0:T(8,128)(2,1)S(1)} collective-permute-done((bf16[512,768]{1,0:T(8,128)(2,1)S(1)}, bf16[512,768]{1,0:T(8,128)(2,1)S(1)}, u32[]{:S(2)}, u32[]{:S(2)}) %collective-permute-start.44) | collective-permute-done | bytes 786464 | tf_op jit(solution)/shard_map/ppermute | solution.py:547
  246.9 2.7 collective-permute-done.45
  249.8 1.6 collective-permute-start.55
  252.0 2.0 collective-permute-start.50
  254.2 9.8 %attention_backward.3 = (bf16[512,768]{1,0:T(8,128)(2,1)S(1)}, f32[512,768]{1,0:T(8,128)S(1)}, bf16[1024,576]{1,0:T(8,128)(2,1)S(1)}, f32[1,576]{1,0:T(1,128)S(1)}) custom-call(s32[1]{0:T(128)} %bitcast.refs_0_, bf16[512,768]{1,0:T(8,128)(2,1)S(1)} %get-tuple-element.294.refs_1_, bf16[512,768]{1,0:T(8,128)(2,1)S(1)} %collective-permute-done.48.refs_2_, ...), custom_call_target="tpu_custom_call" | custom-call | flops 4026531840 | bytes 7588100 | tf_op jit(solution)/shard_map/attention_backward/pallas_call | solution.py:840
  270.2 8.3 %collective-permute-done.53.refs_6_ = bf16[256,768]{1,0:T(8,128)(2,1)S(1)} collective-permute-done((bf16[256,768]{1,0:T(8,128)(2,1)S(1)}, bf16[256,768]{1,0:T(8,128)(2,1)S(1)}, u32[]{:S(2)}, u32[]{:S(2)}) %collective-permute-start.53) | collective-permute-done | bytes 393248 | tf_op jit(solution)/shard_map/ppermute | solution.py:547
  284.3 1.6 collective-permute-start.57
  290.5 1.6 collective-permute-start.60
  295.3 2.6 collective-permute-done.56
  298.1 1.6 finish_feed.2
  299.9 2.0 collective-permute-start.64
  301.9 2.8 collective-permute-done.65
  308.5 2.1 collective-permute-start.66
  311.5 1.9 collective-permute-done.68.arrived_ref
  314.1 1.6 finish_attend.2
  315.8 1.6 finish_feed.3
  318.2 1.6 finish_attend.3
  (228 shorter events, 71.7 us)
Async XLA Ops:
  3.1 18.8 %collective-permute-start.3 = (bf16[208,768]{1,0:T(8,128)(2,1)}, bf16[208,768]{1,0:T(8,128)(2,1)S(1)}, u32[]{:S(2)}, u32[]{:S(2)}) collective-permute-start(bf16[208,768]{1,0:T(8,128)(2,1)} %prepare_first.1.refs_0_.refs_6_), channel_id=1, source_target_pairs={{0,16},{8,24},{16,0},{24,8},{1,17},{9,25},{17,1},{25,9},{2,18},{10... | collective-permute-start | bytes 958472 | tf_op jit(solution)/shard_map/ppermute | solution.py:547
  9.0 8.4 %collective-permute-start = (bf16[144,768]{1,0:T(8,128)(2,1)S(1)}, bf16[144,768]{1,0:T(8,128)(2,1)S(1)}, u32[]{:S(2)}, u32[]{:S(2)}) collective-permute-start(bf16[144,768]{1,0:T(8,128)(2,1)S(1)} %fusion.102), channel_id=1, source_target_pairs={{0,4},{4,0},{1,5},{5,1},{2,6},{6,2},{3,7},{7,3},{8,12},{12,8},{9,1... | collective-permute-start | bytes 663560 | tf_op jit(solution)/shard_map/ppermute | solution.py:547
  10.6 16.5 %collective-permute-start.2 = (bf16[208,768]{1,0:T(8,128)(2,1)}, bf16[208,768]{1,0:T(8,128)(2,1)S(1)}, u32[]{:S(2)}, u32[]{:S(2)}) collective-permute-start(bf16[208,768]{1,0:T(8,128)(2,1)} %prepare_first.1.refs_0_.refs_6_), channel_id=1, source_target_pairs={{0,8},{8,0},{16,24},{24,16},{1,9},{9,1},{17,25},{25,17},{2,10},{10... | collective-permute-start | bytes 958472 | tf_op jit(solution)/shard_map/ppermute | solution.py:547
  12.2 14.4 %collective-permute-start.6 = (bf16[128,768]{1,0:T(8,128)(2,1)S(1)}, bf16[128,768]{1,0:T(8,128)(2,1)S(1)}, u32[]{:S(2)}, u32[]{:S(2)}) collective-permute-start(bf16[128,768]{1,0:T(8,128)(2,1)S(1)} %get-tuple-element.381), channel_id=1, source_target_pairs={{0,4},{4,0},{1,5},{5,1},{2,6},{6,2},{3,7},{7,3},{8,12},{12,8},{9,1... | collective-permute-start | bytes 589832 | tf_op jit(solution)/shard_map/ppermute | solution.py:547
  18.3 8.3 %collective-permute-start.1 = (bf16[256,768]{1,0:T(8,128)(2,1)S(1)}, bf16[256,768]{1,0:T(8,128)(2,1)S(1)}, u32[]{:S(2)}, u32[]{:S(2)}) collective-permute-start(bf16[256,768]{1,0:T(8,128)(2,1)S(1)} %convolution_convert_fusion.2), channel_id=1, source_target_pairs={{0,2},{1,3},{2,0},{3,1},{4,6},{5,7},{6,4},{7,5},{8,10},{9,11},{10,... | collective-permute-start | bytes 1179656 | tf_op jit(solution)/shard_map/ppermute | solution.py:547
  21.9 15.6 %collective-permute-start.5 = (bf16[192,768]{1,0:T(8,128)(2,1)S(1)}, bf16[192,768]{1,0:T(8,128)(2,1)S(1)}, u32[]{:S(2)}, u32[]{:S(2)}) collective-permute-start(bf16[192,768]{1,0:T(8,128)(2,1)S(1)} %get-tuple-element.375), channel_id=1, source_target_pairs={{0,16},{8,24},{16,0},{24,8},{1,17},{9,25},{17,1},{25,9},{2,18},{10... | collective-permute-start | bytes 884744 | tf_op jit(solution)/shard_map/ppermute | solution.py:547
  22.0 16.4 %collective-permute-start.4 = (bf16[208,768]{1,0:T(8,128)(2,1)S(1)}, bf16[208,768]{1,0:T(8,128)(2,1)S(1)}, u32[]{:S(2)}, u32[]{:S(2)}) collective-permute-start(bf16[208,768]{1,0:T(8,128)(2,1)S(1)} %collective-permute-done.3.refs_1_.refs_7_), channel_id=1, source_target_pairs={{0,8},{8,0},{16,24},{24,16},{1,9},{9,1},{17,25},{25,17},{2,10},{10... | collective-permute-start | bytes 958472 | tf_op jit(solution)/shard_map/ppermute | solution.py:547
  38.8 7.0 %collective-permute-start.7 = (bf16[512,768]{1,0:T(8,128)(2,1)S(1)}, bf16[512,768]{1,0:T(8,128)(2,1)S(1)}, u32[]{:S(2)}, u32[]{:S(2)}) collective-permute-start(bf16[512,768]{1,0:T(8,128)(2,1)S(1)} %norm_only.1.refs_1_), channel_id=1, source_target_pairs={{0,1},{1,0},{2,3},{3,2},{4,5},{5,4},{6,7},{7,6},{8,9},{9,8},{10,11... | collective-permute-start | bytes 2359304 | tf_op jit(solution)/shard_map/ppermute | solution.py:547
  39.0 14.6 %collective-permute-start.8 = (bf16[384,384]{1,0:T(8,128)(2,1)S(1)}, bf16[384,384]{1,0:T(8,128)(2,1)S(1)}, u32[]{:S(2)}, u32[]{:S(2)}) collective-permute-start(bf16[384,384]{1,0:T(8,128)(2,1)S(1)} %pad_maximum_fusion.10), channel_id=1, source_target_pairs={{0,8},{8,0},{16,24},{24,16},{1,9},{9,1},{17,25},{25,17},{2,10},{10... | collective-permute-start | bytes 884744 | tf_op jit(solution)/shard_map/ppermute | solution.py:547
  39.9 13.8 %collective-permute-start.10 = (bf16[256,768]{1,0:T(8,128)(2,1)S(1)}, bf16[256,768]{1,0:T(8,128)(2,1)S(1)}, u32[]{:S(2)}, u32[]{:S(2)}) collective-permute-start(bf16[256,768]{1,0:T(8,128)(2,1)S(1)} %convolution_convert_fusion.1), channel_id=1, source_target_pairs={{0,2},{1,3},{2,0},{3,1},{4,6},{5,7},{6,4},{7,5},{8,10},{9,11},{10,... | collective-permute-start | bytes 1179656 | tf_op jit(solution)/shard_map/ppermute | solution.py:547
  41.5 12.1 %collective-permute-start.9 = (bf16[192,384]{1,0:T(8,128)(2,1)S(1)}, bf16[192,384]{1,0:T(8,128)(2,1)S(1)}, u32[]{:S(2)}, u32[]{:S(2)}) collective-permute-start(bf16[192,384]{1,0:T(8,128)(2,1)S(1)} %get-tuple-element.376), channel_id=1, source_target_pairs={{0,16},{8,24},{16,0},{24,8},{1,17},{9,25},{17,1},{25,9},{2,18},{10... | collective-permute-start | bytes 442376 | tf_op jit(solution)/shard_map/ppermute | solution.py:547
  56.2 19.6 %collective-permute-start.12 = (bf16[512,768]{1,0:T(8,128)(2,1)S(1)}, bf16[512,768]{1,0:T(8,128)(2,1)S(1)}, u32[]{:S(2)}, u32[]{:S(2)}) collective-permute-start(bf16[512,768]{1,0:T(8,128)(2,1)S(1)} %add_convert_fusion.5.partial_ref), channel_id=1, source_target_pairs={{0,2},{1,3},{2,0},{3,1},{4,6},{5,7},{6,4},{7,5},{8,10},{9,11},{10,... | collective-permute-start | bytes 2359304 | tf_op jit(solution)/shard_map/ppermute | solution.py:547
  56.8 21.5 %collective-permute-start.14 = (bf16[384,768]{1,0:T(8,128)(2,1)S(1)}, bf16[384,768]{1,0:T(8,128)(2,1)S(1)}, u32[]{:S(2)}, u32[]{:S(2)}) collective-permute-start(bf16[384,768]{1,0:T(8,128)(2,1)S(1)} %maximum_maximum_fusion.refs_4_.refs_5_), channel_id=1, source_target_pairs={{0,8},{8,0},{16,24},{24,16},{1,9},{9,1},{17,25},{25,17},{2,10},{10... | collective-permute-start | bytes 1769480 | tf_op jit(solution)/shard_map/ppermute | solution.py:547
  57.6 20.7 %collective-permute-start.13 = (bf16[768,384]{1,0:T(8,128)(2,1)S(1)}, bf16[768,384]{1,0:T(8,128)(2,1)S(1)}, u32[]{:S(2)}, u32[]{:S(2)}) collective-permute-start(bf16[768,384]{1,0:T(8,128)(2,1)S(1)} %pad_maximum_fusion.4.refs_2_.refs_3_), channel_id=1, source_target_pairs={{0,4},{4,0},{1,5},{5,1},{2,6},{6,2},{3,7},{7,3},{8,12},{12,8},{9,1... | collective-permute-start | bytes 1769480 | tf_op jit(solution)/shard_map/ppermute | solution.py:547
  59.2 17.7 %collective-permute-start.15 = (bf16[192,768]{1,0:T(8,128)(2,1)S(1)}, bf16[192,768]{1,0:T(8,128)(2,1)S(1)}, u32[]{:S(2)}, u32[]{:S(2)}) collective-permute-start(bf16[192,768]{1,0:T(8,128)(2,1)S(1)} %prepare_attend.1), channel_id=1, source_target_pairs={{0,16},{8,24},{16,0},{24,8},{1,17},{9,25},{17,1},{25,9},{2,18},{10... | collective-permute-start | bytes 884744 | tf_op jit(solution)/shard_map/ppermute | solution.py:547
  82.2 2.4 collective-permute-start.17
  84.8 19.6 %collective-permute-start.18 = (bf16[512,768]{1,0:T(8,128)(2,1)S(1)}, bf16[512,768]{1,0:T(8,128)(2,1)S(1)}, u32[]{:S(2)}, u32[]{:S(2)}) collective-permute-start(bf16[512,768]{1,0:T(8,128)(2,1)S(1)} %add_convert_fusion.4.partial_ref), channel_id=1, source_target_pairs={{0,2},{1,3},{2,0},{3,1},{4,6},{5,7},{6,4},{7,5},{8,10},{9,11},{10,... | collective-permute-start | bytes 2359304 | tf_op jit(solution)/shard_map/ppermute | solution.py:547
  86.4 21.5 %collective-permute-start.19 = (bf16[384,768]{1,0:T(8,128)(2,1)S(1)}, bf16[384,768]{1,0:T(8,128)(2,1)S(1)}, u32[]{:S(2)}, u32[]{:S(2)}) collective-permute-start(bf16[384,768]{1,0:T(8,128)(2,1)S(1)} %constant_dynamic-update-slice_fusion.refs_5_.refs_6_), channel_id=1, source_target_pairs={{0,8},{8,0},{16,24},{24,16},{1,9},{9,1},{17,25},{25,17},{2,10},{10... | collective-permute-start | bytes 1769480 | tf_op jit(solution)/shard_map/ppermute | solution.py:547
  87.4 18.0 %collective-permute-start.20 = (bf16[192,384]{1,0:T(8,128)(2,1)S(1)}, bf16[192,384]{1,0:T(8,128)(2,1)S(1)}, u32[]{:S(2)}, u32[]{:S(2)}) collective-permute-start(bf16[192,384]{1,0:T(8,128)(2,1)S(1)} %get-tuple-element.373), channel_id=1, source_target_pairs={{0,16},{8,24},{16,0},{24,8},{1,17},{9,25},{17,1},{25,9},{2,18},{10... | collective-permute-start | bytes 442376 | tf_op jit(solution)/shard_map/ppermute | solution.py:547
  88.1 18.3 %collective-permute-start.21 = (bf16[192,384]{1,0:T(8,128)(2,1)S(1)}, bf16[192,384]{1,0:T(8,128)(2,1)S(1)}, u32[]{:S(2)}, u32[]{:S(2)}) collective-permute-start(bf16[192,384]{1,0:T(8,128)(2,1)S(1)} %get-tuple-element.372), channel_id=1, source_target_pairs={{0,16},{8,24},{16,0},{24,8},{1,17},{9,25},{17,1},{25,9},{2,18},{10... | collective-permute-start | bytes 442376 | tf_op jit(solution)/shard_map/ppermute | solution.py:547
  107.9 12.6 %collective-permute-start.23 = (bf16[384,384]{1,0:T(8,128)(2,1)S(1)}, bf16[384,384]{1,0:T(8,128)(2,1)S(1)}, u32[]{:S(2)}, u32[]{:S(2)}) collective-permute-start(bf16[384,384]{1,0:T(8,128)(2,1)S(1)} %pad_maximum_fusion.11), channel_id=1, source_target_pairs={{0,8},{8,0},{16,24},{24,16},{1,9},{9,1},{17,25},{25,17},{2,10},{10... | collective-permute-start | bytes 884744 | tf_op jit(solution)/shard_map/ppermute | solution.py:547
  109.2 10.1 %collective-permute-start.24 = (bf16[192,384]{1,0:T(8,128)(2,1)S(1)}, bf16[192,384]{1,0:T(8,128)(2,1)S(1)}, u32[]{:S(2)}, u32[]{:S(2)}) collective-permute-start(bf16[192,384]{1,0:T(8,128)(2,1)S(1)} %get-tuple-element.370), channel_id=1, source_target_pairs={{0,16},{8,24},{16,0},{24,8},{1,17},{9,25},{17,1},{25,9},{2,18},{10... | collective-permute-start | bytes 442376 | tf_op jit(solution)/shard_map/ppermute | solution.py:547
  120.7 23.5 %collective-permute-start.29 = (bf16[512,768]{1,0:T(8,128)(2,1)S(1)}, bf16[512,768]{1,0:T(8,128)(2,1)S(1)}, u32[]{:S(2)}, u32[]{:S(2)}) collective-permute-start(bf16[512,768]{1,0:T(8,128)(2,1)S(1)} %pad_maximum_fusion.1.refs_1_.skip_ref), channel_id=1, source_target_pairs={{0,1},{1,0},{2,3},{3,2},{4,5},{5,4},{6,7},{7,6},{8,9},{9,8},{10,11... | collective-permute-start | bytes 2359304 | tf_op jit(solution)/shard_map/ppermute | solution.py:547
  123.1 19.6 %collective-permute-start.26 = (bf16[512,768]{1,0:T(8,128)(2,1)S(1)}, bf16[512,768]{1,0:T(8,128)(2,1)S(1)}, u32[]{:S(2)}, u32[]{:S(2)}) collective-permute-start(bf16[512,768]{1,0:T(8,128)(2,1)S(1)} %add_convert_fusion.3.partial_ref), channel_id=1, source_target_pairs={{0,2},{1,3},{2,0},{3,1},{4,6},{5,7},{6,4},{7,5},{8,10},{9,11},{10,... | collective-permute-start | bytes 2359304 | tf_op jit(solution)/shard_map/ppermute | solution.py:547
  123.9 20.3 %collective-permute-start.28 = (bf16[384,768]{1,0:T(8,128)(2,1)S(1)}, bf16[384,768]{1,0:T(8,128)(2,1)S(1)}, u32[]{:S(2)}, u32[]{:S(2)}) collective-permute-start(bf16[384,768]{1,0:T(8,128)(2,1)S(1)} %maximum_maximum_fusion.1.refs_5_.refs_4_), channel_id=1, source_target_pairs={{0,8},{8,0},{16,24},{24,16},{1,9},{9,1},{17,25},{25,17},{2,10},{10... | collective-permute-start | bytes 1769480 | tf_op jit(solution)/shard_map/ppermute | solution.py:547
  126.7 17.5 %collective-permute-start.27 = (bf16[768,384]{1,0:T(8,128)(2,1)S(1)}, bf16[768,384]{1,0:T(8,128)(2,1)S(1)}, u32[]{:S(2)}, u32[]{:S(2)}) collective-permute-start(bf16[768,384]{1,0:T(8,128)(2,1)S(1)} %pad_maximum_fusion.5.refs_3_.refs_2_), channel_id=1, source_target_pairs={{0,4},{4,0},{1,5},{5,1},{2,6},{6,2},{3,7},{7,3},{8,12},{12,8},{9,1... | collective-permute-start | bytes 1769480 | tf_op jit(solution)/shard_map/ppermute | solution.py:547
  149.3 4.4 %collective-permute-start.31 = (bf16[512,768]{1,0:T(8,128)(2,1)S(1)}, bf16[512,768]{1,0:T(8,128)(2,1)S(1)}, u32[]{:S(2)}, u32[]{:S(2)}) collective-permute-start(bf16[512,768]{1,0:T(8,128)(2,1)S(1)} %get-tuple-element.256), channel_id=1, source_target_pairs={{0,1},{1,0},{2,3},{3,2},{4,5},{5,4},{6,7},{7,6},{8,9},{9,8},{10,11... | collective-permute-start | bytes 2359304 | tf_op jit(solution)/shard_map/ppermute | solution.py:547
  153.8 19.9 %collective-permute-start.32 = (bf16[512,768]{1,0:T(8,128)(2,1)S(1)}, bf16[512,768]{1,0:T(8,128)(2,1)S(1)}, u32[]{:S(2)}, u32[]{:S(2)}) collective-permute-start(bf16[512,768]{1,0:T(8,128)(2,1)S(1)} %add_convert_fusion.2.partial_ref), channel_id=1, source_target_pairs={{0,2},{1,3},{2,0},{3,1},{4,6},{5,7},{6,4},{7,5},{8,10},{9,11},{10,... | collective-permute-start | bytes 2359304 | tf_op jit(solution)/shard_map/ppermute | solution.py:547
  156.1 19.3 %collective-permute-start.34 = (bf16[768,384]{1,0:T(8,128)(2,1)S(1)}, bf16[768,384]{1,0:T(8,128)(2,1)S(1)}, u32[]{:S(2)}, u32[]{:S(2)}) collective-permute-start(bf16[768,384]{1,0:T(8,128)(2,1)S(1)} %slice.339), channel_id=1, source_target_pairs={{0,4},{4,0},{1,5},{5,1},{2,6},{6,2},{3,7},{7,3},{8,12},{12,8},{9,1... | collective-permute-start | bytes 1769480 | tf_op jit(solution)/shard_map/ppermute | solution.py:547
  157.7 17.7 %collective-permute-start.33 = (bf16[384,768]{1,0:T(8,128)(2,1)S(1)}, bf16[384,768]{1,0:T(8,128)(2,1)S(1)}, u32[]{:S(2)}, u32[]{:S(2)}) collective-permute-start(bf16[384,768]{1,0:T(8,128)(2,1)S(1)} %slice.279), channel_id=1, source_target_pairs={{0,8},{8,0},{16,24},{24,16},{1,9},{9,1},{17,25},{25,17},{2,10},{10... | collective-permute-start | bytes 1769480 | tf_op jit(solution)/shard_map/ppermute | solution.py:547
  175.4 2.4 collective-permute-start.35
  175.7 11.7 %collective-permute-start.36 = (bf16[384,384]{1,0:T(8,128)(2,1)S(1)}, bf16[384,384]{1,0:T(8,128)(2,1)S(1)}, u32[]{:S(2)}, u32[]{:S(2)}) collective-permute-start(bf16[384,384]{1,0:T(8,128)(2,1)S(1)} %slice.448), channel_id=1, source_target_pairs={{0,8},{8,0},{16,24},{24,16},{1,9},{9,1},{17,25},{25,17},{2,10},{10... | collective-permute-start | bytes 884744 | tf_op jit(solution)/shard_map/ppermute | solution.py:547
  187.4 2.4 collective-permute-start.37
  189.9 19.8 %collective-permute-start.38 = (bf16[512,768]{1,0:T(8,128)(2,1)S(1)}, bf16[512,768]{1,0:T(8,128)(2,1)S(1)}, u32[]{:S(2)}, u32[]{:S(2)}) collective-permute-start(bf16[512,768]{1,0:T(8,128)(2,1)S(1)} %add_convert_fusion.1.partial_ref), channel_id=1, source_target_pairs={{0,2},{1,3},{2,0},{3,1},{4,6},{5,7},{6,4},{7,5},{8,10},{9,11},{10,... | collective-permute-start | bytes 2359304 | tf_op jit(solution)/shard_map/ppermute | solution.py:547
  191.8 23.9 %collective-permute-start.41 = (bf16[768,384]{1,0:T(8,128)(2,1)S(1)}, bf16[768,384]{1,0:T(8,128)(2,1)S(1)}, u32[]{:S(2)}, u32[]{:S(2)}) collective-permute-start(bf16[768,384]{1,0:T(8,128)(2,1)S(1)} %broadcast_select_fusion.1), channel_id=1, source_target_pairs={{0,4},{4,0},{1,5},{5,1},{2,6},{6,2},{3,7},{7,3},{8,12},{12,8},{9,1... | collective-permute-start | bytes 1769480 | tf_op jit(solution)/shard_map/ppermute | solution.py:547
  193.4 22.3 %collective-permute-start.40 = (bf16[192,768]{1,0:T(8,128)(2,1)S(1)}, bf16[192,768]{1,0:T(8,128)(2,1)S(1)}, u32[]{:S(2)}, u32[]{:S(2)}) collective-permute-start(bf16[192,768]{1,0:T(8,128)(2,1)S(1)} %slice.447), channel_id=1, source_target_pairs={{0,16},{8,24},{16,0},{24,8},{1,17},{9,25},{17,1},{25,9},{2,18},{10... | collective-permute-start | bytes 884744 | tf_op jit(solution)/shard_map/ppermute | solution.py:547
  195.0 20.6 %collective-permute-start.39 = (bf16[192,384]{1,0:T(8,128)(2,1)S(1)}, bf16[192,384]{1,0:T(8,128)(2,1)S(1)}, u32[]{:S(2)}, u32[]{:S(2)}) collective-permute-start(bf16[192,384]{1,0:T(8,128)(2,1)S(1)} %slice.452), channel_id=1, source_target_pairs={{0,16},{8,24},{16,0},{24,8},{1,17},{9,25},{17,1},{25,9},{2,18},{10... | collective-permute-start | bytes 442376 | tf_op jit(solution)/shard_map/ppermute | solution.py:547
  220.6 4.7 %collective-permute-start.43 = (bf16[512,768]{1,0:T(8,128)(2,1)S(1)}, bf16[512,768]{1,0:T(8,128)(2,1)S(1)}, u32[]{:S(2)}, u32[]{:S(2)}) collective-permute-start(bf16[512,768]{1,0:T(8,128)(2,1)S(1)} %get-tuple-element.285), channel_id=1, source_target_pairs={{0,1},{1,0},{2,3},{3,2},{4,5},{5,4},{6,7},{7,6},{8,9},{9,8},{10,11... | collective-permute-start | bytes 2359304 | tf_op jit(solution)/shard_map/ppermute | solution.py:547
  225.5 19.9 %collective-permute-start.44 = (bf16[512,768]{1,0:T(8,128)(2,1)S(1)}, bf16[512,768]{1,0:T(8,128)(2,1)S(1)}, u32[]{:S(2)}, u32[]{:S(2)}) collective-permute-start(bf16[512,768]{1,0:T(8,128)(2,1)S(1)} %add_convert_fusion.partial_ref), channel_id=1, source_target_pairs={{0,2},{1,3},{2,0},{3,1},{4,6},{5,7},{6,4},{7,5},{8,10},{9,11},{10,... | collective-permute-start | bytes 2359304 | tf_op jit(solution)/shard_map/ppermute | solution.py:547
  227.6 19.3 %collective-permute-start.47 = (bf16[768,384]{1,0:T(8,128)(2,1)S(1)}, bf16[768,384]{1,0:T(8,128)(2,1)S(1)}, u32[]{:S(2)}, u32[]{:S(2)}) collective-permute-start(bf16[768,384]{1,0:T(8,128)(2,1)S(1)} %slice.347), channel_id=1, source_target_pairs={{0,4},{4,0},{1,5},{5,1},{2,6},{6,2},{3,7},{7,3},{8,12},{12,8},{9,1... | collective-permute-start | bytes 1769480 | tf_op jit(solution)/shard_map/ppermute | solution.py:547
  228.2 21.4 %collective-permute-start.46 = (bf16[384,768]{1,0:T(8,128)(2,1)S(1)}, bf16[384,768]{1,0:T(8,128)(2,1)S(1)}, u32[]{:S(2)}, u32[]{:S(2)}) collective-permute-start(bf16[384,768]{1,0:T(8,128)(2,1)S(1)} %slice.290), channel_id=1, source_target_pairs={{0,8},{8,0},{16,24},{24,16},{1,9},{9,1},{17,25},{25,17},{2,10},{10... | collective-permute-start | bytes 1769480 | tf_op jit(solution)/shard_map/ppermute | solution.py:547
  228.4 57.9 %collective-permute-start.58 = (bf16[512,768]{1,0:T(8,128)(2,1)S(1)}, bf16[512,768]{1,0:T(8,128)(2,1)S(1)}, u32[]{:S(2)}, u32[]{:S(2)}) collective-permute-start(bf16[512,768]{1,0:T(8,128)(2,1)S(1)} %feed_forward.6), channel_id=1, source_target_pairs={{0,1},{1,0},{2,3},{3,2},{4,5},{5,4},{6,7},{7,6},{8,9},{9,8},{10,11... | collective-permute-start | bytes 2359304 | tf_op jit(solution)/shard_map/ppermute | solution.py:547
  228.5 21.2 %collective-permute-start.45 = (bf16[384,384]{1,0:T(8,128)(2,1)S(1)}, bf16[384,384]{1,0:T(8,128)(2,1)S(1)}, u32[]{:S(2)}, u32[]{:S(2)}) collective-permute-start(bf16[384,384]{1,0:T(8,128)(2,1)S(1)} %slice.446), channel_id=1, source_target_pairs={{0,8},{8,0},{16,24},{24,16},{1,9},{9,1},{17,25},{25,17},{2,10},{10... | collective-permute-start | bytes 884744 | tf_op jit(solution)/shard_map/ppermute | solution.py:547
  249.8 31.7 %collective-permute-start.55 = (bf16[192,1152]{1,0:T(8,128)(2,1)S(1)}, bf16[192,1152]{1,0:T(8,128)(2,1)S(1)}, u32[]{:S(2)}, u32[]{:S(2)}) collective-permute-start(bf16[192,1152]{1,0:T(8,128)(2,1)S(1)} %get-tuple-element.391), channel_id=1, source_target_pairs={{0,4},{4,0},{1,5},{5,1},{2,6},{6,2},{3,7},{7,3},{8,12},{12,8},{9,1... | collective-permute-start | bytes 1327112 | tf_op jit(solution)/shard_map/ppermute | solution.py:547
  251.4 2.8 collective-permute-start.48
  251.6 12.6 %collective-permute-start.51 = (bf16[384,384]{1,0:T(8,128)(2,1)S(1)}, bf16[384,384]{1,0:T(8,128)(2,1)S(1)}, u32[]{:S(2)}, u32[]{:S(2)}) collective-permute-start(bf16[384,384]{1,0:T(8,128)(2,1)S(1)} %slice.445), channel_id=1, source_target_pairs={{0,8},{8,0},{16,24},{24,16},{1,9},{9,1},{17,25},{25,17},{2,10},{10... | collective-permute-start | bytes 884744 | tf_op jit(solution)/shard_map/ppermute | solution.py:547
  252.0 12.0 %collective-permute-start.50 = (bf16[192,384]{1,0:T(8,128)(2,1)S(1)}, bf16[192,384]{1,0:T(8,128)(2,1)S(1)}, u32[]{:S(2)}, u32[]{:S(2)}) collective-permute-start(bf16[192,384]{1,0:T(8,128)(2,1)S(1)} %slice.451), channel_id=1, source_target_pairs={{0,16},{8,24},{16,0},{24,8},{1,17},{9,25},{17,1},{25,9},{2,18},{10... | collective-permute-start | bytes 442376 | tf_op jit(solution)/shard_map/ppermute | solution.py:547
  264.2 3.0 collective-permute-start.52
  266.6 16.2 %collective-permute-start.49 = (bf16[768,384]{1,0:T(8,128)(2,1)S(1)}, bf16[768,384]{1,0:T(8,128)(2,1)S(1)}, u32[]{:S(2)}, u32[]{:S(2)}) collective-permute-start(bf16[768,384]{1,0:T(8,128)(2,1)S(1)} %broadcast_select_fusion), channel_id=1, source_target_pairs={{0,4},{4,0},{1,5},{5,1},{2,6},{6,2},{3,7},{7,3},{8,12},{12,8},{9,1... | collective-permute-start | bytes 1769480 | tf_op jit(solution)/shard_map/ppermute | solution.py:547
  267.3 11.3 %collective-permute-start.53 = (bf16[256,768]{1,0:T(8,128)(2,1)S(1)}, bf16[256,768]{1,0:T(8,128)(2,1)S(1)}, u32[]{:S(2)}, u32[]{:S(2)}) collective-permute-start(bf16[256,768]{1,0:T(8,128)(2,1)S(1)} %add_convert_fusion.8), channel_id=1, source_target_pairs={{0,2},{1,3},{2,0},{3,1},{4,6},{5,7},{6,4},{7,5},{8,10},{9,11},{10,... | collective-permute-start | bytes 1179656 | tf_op jit(solution)/shard_map/ppermute | solution.py:547
  268.9 23.2 %collective-permute-start.63 = (bf16[192,768]{1,0:T(8,128)(2,1)S(1)}, bf16[192,768]{1,0:T(8,128)(2,1)S(1)}, u32[]{:S(2)}, u32[]{:S(2)}) collective-permute-start(bf16[192,768]{1,0:T(8,128)(2,1)S(1)} %slice.443), channel_id=1, source_target_pairs={{0,16},{8,24},{16,0},{24,8},{1,17},{9,25},{17,1},{25,9},{2,18},{10... | collective-permute-start | bytes 884744 | tf_op jit(solution)/shard_map/ppermute | solution.py:547
  280.1 4.2 %collective-permute-start.54 = (f32[16,768]{1,0:T(8,128)S(1)}, f32[16,768]{1,0:T(8,128)S(1)}, u32[]{:S(2)}, u32[]{:S(2)}) collective-permute-start(f32[16,768]{1,0:T(8,128)S(1)} %get-tuple-element.307), channel_id=1, source_target_pairs={{0,1},{1,0},{2,3},{3,2},{4,5},{5,4},{6,7},{7,6},{8,9},{9,8},{10,11... | collective-permute-start | bytes 147464 | tf_op jit(solution)/shard_map/ppermute | solution.py:547
  281.5 10.6 %collective-permute-start.62 = (bf16[192,384]{1,0:T(8,128)(2,1)S(1)}, bf16[192,384]{1,0:T(8,128)(2,1)S(1)}, u32[]{:S(2)}, u32[]{:S(2)}) collective-permute-start(bf16[192,384]{1,0:T(8,128)(2,1)S(1)} %slice.449), channel_id=1, source_target_pairs={{0,16},{8,24},{16,0},{24,8},{1,17},{9,25},{17,1},{25,9},{2,18},{10... | collective-permute-start | bytes 442376 | tf_op jit(solution)/shard_map/ppermute | solution.py:547
  282.7 7.0 %collective-permute-start.59 = (bf16[128,768]{1,0:T(8,128)(2,1)S(1)}, bf16[128,768]{1,0:T(8,128)(2,1)S(1)}, u32[]{:S(2)}, u32[]{:S(2)}) collective-permute-start(bf16[128,768]{1,0:T(8,128)(2,1)S(1)} %slice_select_fusion.1), channel_id=1, source_target_pairs={{0,4},{4,0},{1,5},{5,1},{2,6},{6,2},{3,7},{7,3},{8,12},{12,8},{9,1... | collective-permute-start | bytes 589832 | tf_op jit(solution)/shard_map/ppermute | solution.py:547
  284.3 4.2 %collective-permute-start.57 = (f32[16,768]{1,0:T(8,128)S(1)}, f32[16,768]{1,0:T(8,128)S(1)}, u32[]{:S(2)}, u32[]{:S(2)}) collective-permute-start(f32[16,768]{1,0:T(8,128)S(1)} %add.147), channel_id=1, source_target_pairs={{0,2},{1,3},{2,0},{3,1},{4,6},{5,7},{6,4},{7,5},{8,10},{9,11},{10,... | collective-permute-start | bytes 147464 | tf_op jit(solution)/shard_map/ppermute | solution.py:547
  286.2 11.7 %collective-permute-start.56 = (bf16[384,384]{1,0:T(8,128)(2,1)S(1)}, bf16[384,384]{1,0:T(8,128)(2,1)S(1)}, u32[]{:S(2)}, u32[]{:S(2)}) collective-permute-start(bf16[384,384]{1,0:T(8,128)(2,1)S(1)} %slice.444), channel_id=1, source_target_pairs={{0,8},{8,0},{16,24},{24,16},{1,9},{9,1},{17,25},{25,17},{2,10},{10... | collective-permute-start | bytes 884744 | tf_op jit(solution)/shard_map/ppermute | solution.py:547
  290.5 9.3 %collective-permute-start.60 = (f32[256,256]{1,0:T(8,128)S(1)}, f32[256,256]{1,0:T(8,128)S(1)}, u32[]{:S(2)}, u32[]{:S(2)}) collective-permute-start(f32[256,256]{1,0:T(8,128)S(1)} %pack_grads.1), channel_id=1, source_target_pairs={{0,4},{4,0},{1,5},{5,1},{2,6},{6,2},{3,7},{7,3},{8,12},{12,8},{9,1... | collective-permute-start | bytes 786440 | tf_op jit(solution)/shard_map/ppermute | solution.py:547
  292.4 21.7 %collective-permute-start.69 = (bf16[192,1536]{1,0:T(8,128)(2,1)S(1)}, bf16[192,1536]{1,0:T(8,128)(2,1)S(1)}, u32[]{:S(2)}, u32[]{:S(2)}) collective-permute-start(bf16[192,1536]{1,0:T(8,128)(2,1)S(1)} %pad_maximum_fusion.6), channel_id=1, source_target_pairs={{0,4},{4,0},{1,5},{5,1},{2,6},{6,2},{3,7},{7,3},{8,12},{12,8},{9,1... | collective-permute-start | bytes 1769480 | tf_op jit(solution)/shard_map/ppermute | solution.py:547
  293.9 10.8 %collective-permute-start.65 = (bf16[256,768]{1,0:T(8,128)(2,1)S(1)}, bf16[256,768]{1,0:T(8,128)(2,1)S(1)}, u32[]{:S(2)}, u32[]{:S(2)}) collective-permute-start(bf16[256,768]{1,0:T(8,128)(2,1)S(1)} %add_convert_fusion.7), channel_id=1, source_target_pairs={{0,2},{1,3},{2,0},{3,1},{4,6},{5,7},{6,4},{7,5},{8,10},{9,11},{10,... | collective-permute-start | bytes 1179656 | tf_op jit(solution)/shard_map/ppermute | solution.py:547
  298.0 8.8 %collective-permute-start.61 = (bf16[192,384]{1,0:T(8,128)(2,1)S(1)}, bf16[192,384]{1,0:T(8,128)(2,1)S(1)}, u32[]{:S(2)}, u32[]{:S(2)}) collective-permute-start(bf16[192,384]{1,0:T(8,128)(2,1)S(1)} %slice.450), channel_id=1, source_target_pairs={{0,16},{8,24},{16,0},{24,8},{1,17},{9,25},{17,1},{25,9},{2,18},{10... | collective-permute-start | bytes 442376 | tf_op jit(solution)/shard_map/ppermute | solution.py:547
  299.9 8.2 %collective-permute-start.64 = (f32[128,256]{1,0:T(8,128)S(1)}, f32[128,256]{1,0:T(8,128)S(1)}, u32[]{:S(2)}, u32[]{:S(2)}) collective-permute-start(f32[128,256]{1,0:T(8,128)S(1)} %slice.365), channel_id=1, source_target_pairs={{0,8},{8,0},{16,24},{24,16},{1,9},{9,1},{17,25},{25,17},{2,10},{10... | collective-permute-start | bytes 393224 | tf_op jit(solution)/shard_map/ppermute | solution.py:547
  308.2 5.2 %collective-permute-start.68 = (f32[64,256]{1,0:T(8,128)S(1)}, f32[64,256]{1,0:T(8,128)S(1)}, u32[]{:S(2)}, u32[]{:S(2)}) collective-permute-start(f32[64,256]{1,0:T(8,128)S(1)} %slice.367), channel_id=1, source_target_pairs={{0,16},{8,24},{16,0},{24,8},{1,17},{9,25},{17,1},{25,9},{2,18},{10... | collective-permute-start | bytes 196616 | tf_op jit(solution)/shard_map/ppermute | solution.py:547
  308.3 9.1 %collective-permute-start.67 = (bf16[128,768]{1,0:T(8,128)(2,1)S(1)}, bf16[128,768]{1,0:T(8,128)(2,1)S(1)}, u32[]{:S(2)}, u32[]{:S(2)}) collective-permute-start(bf16[128,768]{1,0:T(8,128)(2,1)S(1)} %get-tuple-element.379), channel_id=1, source_target_pairs={{0,4},{4,0},{1,5},{5,1},{2,6},{6,2},{3,7},{7,3},{8,12},{12,8},{9,1... | collective-permute-start | bytes 589832 | tf_op jit(solution)/shard_map/ppermute | solution.py:547
  308.5 9.8 %collective-permute-start.66 = (bf16[192,384]{1,0:T(8,128)(2,1)S(1)}, bf16[192,384]{1,0:T(8,128)(2,1)S(1)}, u32[]{:S(2)}, u32[]{:S(2)}) collective-permute-start(bf16[192,384]{1,0:T(8,128)(2,1)S(1)} %add_convert_fusion.11.refs_0_), channel_id=1, source_target_pairs={{0,4},{4,0},{1,5},{5,1},{2,6},{6,2},{3,7},{7,3},{8,12},{12,8},{9,1... | collective-permute-start | bytes 442376 | tf_op jit(solution)/shard_map/ppermute | solution.py:547
  (16 other events, 167.2 us)
